TPU v7x, 32 devices: a whole 2x2x4 slice. The times are simulated.
32 devices in a mesh: grp: 8 (over y, x, core), fsdp: 4 (over z).
Axes of the slice: x: 2, y: 2, z: 4, core: 2. Of those that a mesh axis runs over, the one named last changes fastest.
Arguments:
- tokens: bfloat16 [10240, 768], P(('grp', 'fsdp')), may hold values from -6 to 6
- cotangent: bfloat16 [10240, 768], P(('grp', 'fsdp')), may hold values from -6 to 6
- prev_logits: float32 [10240, 12], P(('grp', 'fsdp')), may hold values from -6 to 6
- lengths: int32 [8, 8], P('grp'), may hold values from 64 to 256, as said below
- dealing: int32 [8, 8], P('grp'), may hold values from 0 to 7, as said below
- routes: int32 [10240, 2], P(('grp', 'fsdp')), may hold values from 0 to 11, all different within a row; in each aligned block of 320 rows (0 to 319, 320 to 639, ...) at most 80 rows name the same one
- gain_one: bfloat16 [768], P(('grp', 'fsdp')), may hold values from 0.5 to 1.5
- w_query: bfloat16 [768, 768], P('fsdp', 'grp'), may hold values from -0.21875 to 0.21875
- w_key: bfloat16 [768, 768], P('fsdp', 'grp'), may hold values from -0.21875 to 0.21875
- w_value: bfloat16 [768, 768], P('fsdp', 'grp'), may hold values from -0.21875 to 0.21875
- w_out: bfloat16 [768, 768], P('fsdp', 'grp'), may hold values from -2.5 to 2.5
- gain_two: bfloat16 [768], P(('grp', 'fsdp')), may hold values from 0.5 to 1.5
- w_router: bfloat16 [768, 12], P(('grp', 'fsdp')), may hold values from -0.109375 to 0.109375
- w_mix: bfloat16 [12, 12], replicated, may hold values from -0.875 to 0.875
- w_const: bfloat16 [768, 4], P(('grp', 'fsdp')), may hold values from -0.21875 to 0.21875
- v_const: bfloat16 [768, 2], P(('grp', 'fsdp')), may hold values from -6 to 6
- w_gate: bfloat16 [8, 768, 2048], P(None, 'fsdp', 'grp'), may hold values from -0.21875 to 0.21875
- w_up: bfloat16 [8, 768, 2048], P(None, 'fsdp', 'grp'), may hold values from -0.21875 to 0.21875
- w_down: bfloat16 [8, 2048, 768], P(None, 'grp', 'fsdp'), may hold values from -1 to 1
Outputs:
- output: bfloat16 [10240, 768], P(('grp', 'fsdp'))
- grad_tokens: float32 [10240, 768], P(('grp', 'fsdp'))
- grad_prev: float32 [10240, 12], P(('grp', 'fsdp'))
- grad_gain_one: float32 [768], P(('grp', 'fsdp'))
- grad_query: float32 [768, 768], P('fsdp', 'grp')
- grad_key: float32 [768, 768], P('fsdp', 'grp')
- grad_value: float32 [768, 768], P('fsdp', 'grp')
- grad_out_proj: float32 [768, 768], P('fsdp', 'grp')
- grad_gain_two: float32 [768], P(('grp', 'fsdp'))
- grad_router: float32 [768, 12], P(('grp', 'fsdp'))
- grad_mix: float32 [12, 12], replicated
- grad_const: float32 [768, 4], P(('grp', 'fsdp'))
- grad_vconst: float32 [768, 2], P(('grp', 'fsdp'))
- grad_gate: float32 [8, 768, 2048], P(None, 'fsdp', 'grp')
- grad_up: float32 [8, 768, 2048], P(None, 'fsdp', 'grp')
- grad_down: float32 [8, 2048, 768], P(None, 'grp', 'fsdp')
Inputs may be any that keep to these rules, and one draw needn't show every extreme that they name: Row g holds the lengths of group g's 8 sequences in the given order; they sum to 1280. The two sequences that dealing sends to one device have lengths that, each rounded up to a multiple of 128, sum to 384. `dealing`: each row is a permutation of the group's sequence numbers; entries 2i and 2i + 1 name the two sequences that device i of fsdp holds, in that order. `routes`: the two experts of a row differ; no expert is named by more than 80 rows of one device.
All inputs are finite; a program needn't handle non-finite values.
Results may differ from a plain program's by a relative error of at most 0.02.
Values may be sent and summed in bfloat16 or wider, within the bound.
A program may use at most 384 MiB of HBM per device.

v0:
```python
import math

import jax
import jax.numpy as jnp
from jax import lax
from jax.sharding import PartitionSpec as P

HEADS = 12
HEAD_DIM = 64
E = 8
CONSTS = 2
BLOCK = 128
EXPERTS_ALL = 12
CAP = 384
TOK_DEV = 320
MOST = 80


NORM_EPS = 1e-05
EXACT = lax.Precision.HIGHEST


def rotation_tables(positions, head_dim):
    half_dim = head_dim // 2
    inv_freq = jnp.exp(
        jnp.arange(half_dim, dtype=jnp.float32) * (-2.0 * math.log(10000.0) / head_dim)
    )
    angles = positions.astype(jnp.float32)[:, None] * inv_freq[None, :]
    return (jnp.cos(angles), jnp.sin(angles))


def rotate(values, cos_table, sin_table):
    row_count = values.shape[0]
    half_dim = cos_table.shape[1]
    heads_view = values.reshape(row_count, -1, 2 * half_dim)
    front_half = heads_view[:, :, :half_dim]
    back_half = heads_view[:, :, half_dim:]
    cos_view = cos_table[:, None, :]
    sin_view = sin_table[:, None, :]
    turned = jnp.concatenate(
        [
            front_half * cos_view - back_half * sin_view,
            back_half * cos_view + front_half * sin_view,
        ],
        axis=2,
    )
    return turned.reshape(row_count, -1)


def exact_dot(left_side, right_side):
    return jnp.dot(left_side, right_side, precision=EXACT, preferred_element_type=jnp.float32)


def per_device(
    tokens,
    cotangent,
    prev_logits,
    lengths,
    dealing,
    routes,
    gain_one,
    w_query,
    w_key,
    w_value,
    w_out,
    gain_two,
    w_router,
    w_mix,
    w_const,
    v_const,
    w_gate,
    w_up,
    w_down,
):
    groups = lax.axis_size("grp")
    dealers = lax.axis_size("fsdp")
    device = lax.axis_index("fsdp")
    model_width = tokens.shape[1]
    per_shard = model_width // (groups * dealers)
    pairs = HEADS // 2
    pair_width = 2 * HEAD_DIM
    scale = HEAD_DIM ** (-0.5)
    seq_len = lengths[0]
    deal_order = dealing[0]
    seq_count = seq_len.shape[0]
    seq_ids = jnp.arange(seq_count, dtype=jnp.int32)
    seq_ends = jnp.cumsum(seq_len)
    starts = seq_ends - seq_len
    padded = (seq_len + BLOCK - 1) // BLOCK * BLOCK
    order_hot = (deal_order[:, None] == seq_ids[None, :]).astype(jnp.int32)
    dealt_len = jnp.sum(order_hot * seq_len[None, :], axis=1)
    dealt_pad = jnp.sum(order_hot * padded[None, :], axis=1)
    dealt_start = jnp.sum(order_hot * starts[None, :], axis=1)
    slot_of = jnp.sum(order_hot * seq_ids[:, None], axis=0)
    pair_index = 2 * device
    row_ids = jnp.arange(CAP, dtype=jnp.int32)
    in_second = row_ids >= dealt_pad[pair_index]
    position = row_ids - jnp.where(in_second, dealt_pad[pair_index], 0)
    seq_limit = jnp.where(in_second, dealt_len[pair_index + 1], dealt_len[pair_index])
    live_rows = position < seq_limit
    source = jnp.where(in_second, dealt_start[pair_index + 1], dealt_start[pair_index]) + position
    source = jnp.where(live_rows, source, -1)
    given_rows = device * TOK_DEV + jnp.arange(TOK_DEV, dtype=jnp.int32)
    seq_hot = (
        (given_rows[:, None] >= starts[None, :]) & (given_rows[:, None] < seq_ends[None, :])
    ).astype(jnp.int32)
    offset_in = given_rows - jnp.sum(seq_hot * starts[None, :], axis=1)
    slot_rank = jnp.sum(seq_hot * slot_of[None, :], axis=1)
    is_second = slot_rank % 2
    lead_pad = jnp.take(dealt_pad, slot_rank - is_second)
    target = slot_rank // 2 * CAP + jnp.where(is_second == 1, lead_pad, 0) + offset_in

    def deal(values):
        shard_rows = lax.all_gather(values, "fsdp", axis=0, tiled=True)
        row_span = shard_rows.shape[0]
        inside = (source >= 0) & (source < row_span)
        taken_rows = jnp.take(shard_rows, jnp.clip(source, 0, row_span - 1), axis=0)
        return jnp.where(inside[:, None], taken_rows, jnp.zeros((CAP, model_width), jnp.bfloat16))

    def give_back(values):
        shard_rows = lax.all_gather(values, "fsdp", axis=0, tiled=True)
        row_span = shard_rows.shape[0]
        inside = (target >= 0) & (target < row_span)
        taken_rows = jnp.take(shard_rows, jnp.clip(target, 0, row_span - 1), axis=0)
        return jnp.where(
            inside[:, None], taken_rows, jnp.zeros((TOK_DEV, model_width), jnp.bfloat16)
        )

    def collect():
        gate_in, up_in, down_in = (w_gate, w_up, w_down)
        sectioned = (
            lax.all_gather(gain_one, "fsdp", axis=0, tiled=True),
            lax.all_gather(w_query, "fsdp", axis=0, tiled=True),
            lax.all_gather(w_key, "fsdp", axis=0, tiled=True),
            lax.all_gather(w_value, "fsdp", axis=0, tiled=True),
            lax.all_gather(w_out, "fsdp", axis=0, tiled=True),
            lax.all_gather(gain_two, "fsdp", axis=0, tiled=True),
            lax.all_gather(w_router, "fsdp", axis=0, tiled=True),
            lax.all_gather(w_const, "fsdp", axis=0, tiled=True),
            lax.all_gather(v_const, "fsdp", axis=0, tiled=True),
            lax.all_gather(gate_in, "fsdp", axis=1, tiled=True),
            lax.all_gather(up_in, "fsdp", axis=1, tiled=True),
            lax.all_gather(down_in, "fsdp", axis=2, tiled=True),
        )
        (
            part_g1,
            part_q,
            part_k,
            part_v,
            part_o,
            part_g2,
            part_r,
            part_c,
            part_vc,
            part_gate,
            part_up,
            part_down,
        ) = sectioned
        small = (
            lax.all_gather(part_g1, "grp", axis=0, tiled=True),
            lax.all_gather(part_q, "grp", axis=1, tiled=True),
            lax.all_gather(part_k, "grp", axis=1, tiled=True),
            lax.all_gather(part_v, "grp", axis=1, tiled=True),
            lax.all_gather(part_o, "grp", axis=1, tiled=True),
            lax.all_gather(part_g2, "grp", axis=0, tiled=True),
            lax.all_gather(part_r, "grp", axis=0, tiled=True),
            lax.all_gather(part_c, "grp", axis=0, tiled=True),
            lax.all_gather(part_vc, "grp", axis=0, tiled=True),
        )
        experts = (
            lax.all_gather(part_gate, "grp", axis=2, tiled=True),
            lax.all_gather(part_up, "grp", axis=2, tiled=True),
            lax.all_gather(part_down, "grp", axis=1, tiled=True),
        )
        return tuple(small) + tuple(experts)

    (
        gain1,
        weight_q,
        weight_k,
        weight_v,
        weight_o,
        gain2,
        router,
        wconst,
        vconst,
        wgate,
        wup,
        wdown,
    ) = collect()
    dealt = deal(tokens)
    dealt_f = dealt.astype(jnp.float32)
    inv_one = lax.rsqrt(jnp.mean(dealt_f * dealt_f, axis=1, keepdims=True) + NORM_EPS)
    unit_one = dealt_f * inv_one
    gain1_f = gain1.astype(jnp.float32)
    normed_one = (unit_one * gain1_f).astype(jnp.bfloat16)
    cos_table, sin_table = rotation_tables(position, HEAD_DIM)
    query = rotate(
        jnp.dot(normed_one, weight_q, preferred_element_type=jnp.float32), cos_table, sin_table
    ).astype(jnp.bfloat16)
    keyed = rotate(
        jnp.dot(normed_one, weight_k, preferred_element_type=jnp.float32), cos_table, sin_table
    ).astype(jnp.bfloat16)
    values_proj = jnp.dot(normed_one, weight_v, preferred_element_type=jnp.float32).astype(
        jnp.bfloat16
    )
    allowed = (
        (in_second[:, None] == in_second[None, :])
        & (position[None, :] <= position[:, None])
        & live_rows[None, :]
    )

    def by_pairs(values):
        return values.reshape(CAP, pairs, pair_width).transpose(1, 0, 2)

    def from_pairs(values):
        return values.transpose(1, 0, 2).reshape(CAP, model_width)

    def pair_scores(q_pair, k_pair):
        query_heads = q_pair.reshape(CAP, 2, HEAD_DIM)
        key_heads = k_pair.reshape(CAP, 2, HEAD_DIM)
        scores = (
            jnp.einsum("qhd,khd->hqk", query_heads, key_heads, preferred_element_type=jnp.float32)
            * scale
        )
        return (jnp.where(allowed[None], scores, -1e30), query_heads, key_heads)

    def attend(pair_items):
        q_pair, k_pair, v_pair = pair_items
        scores, query_heads, key_heads = pair_scores(q_pair, k_pair)
        row_top = jnp.max(scores, axis=-1, keepdims=True)
        weights_exp = jnp.exp(scores - row_top)
        row_total = jnp.sum(weights_exp, axis=-1, keepdims=True)
        attn_probs = weights_exp / row_total
        value_heads = v_pair.reshape(CAP, 2, HEAD_DIM)
        mixed_pair = jnp.einsum(
            "hqk,khd->qhd",
            attn_probs.astype(jnp.bfloat16),
            value_heads,
            preferred_element_type=jnp.float32,
        )
        return (mixed_pair.reshape(CAP, pair_width), (row_top + jnp.log(row_total))[:, :, 0])

    mixed_pairs, log_sums = lax.map(
        attend, (by_pairs(query), by_pairs(keyed), by_pairs(values_proj))
    )
    mixed = from_pairs(mixed_pairs).astype(jnp.bfloat16)
    attn_out = jnp.dot(mixed, weight_o, preferred_element_type=jnp.float32).astype(jnp.bfloat16)
    returned = give_back(attn_out)
    resid = tokens.astype(jnp.float32) + returned.astype(jnp.float32)
    inv_two = lax.rsqrt(jnp.mean(resid * resid, axis=1, keepdims=True) + NORM_EPS)
    unit_two = resid * inv_two
    gain2_f = gain2.astype(jnp.float32)
    normed = unit_two * gain2_f
    narrow = normed.astype(jnp.bfloat16)
    mix_f = w_mix.astype(jnp.float32)
    router_f = router.astype(jnp.float32)
    wconst_f = wconst.astype(jnp.float32)
    logits = jnp.dot(narrow, router, preferred_element_type=jnp.float32) + exact_dot(
        prev_logits, mix_f
    )
    logit_top = jnp.max(logits, axis=1, keepdims=True)
    logit_exp = jnp.exp(logits - logit_top)
    route_probs = logit_exp / jnp.sum(logit_exp, axis=1, keepdims=True)
    expert_ids = jnp.arange(EXPERTS_ALL, dtype=jnp.int32)
    chosen = (
        (routes[:, 0:1] == expert_ids[None, :]) | (routes[:, 1:2] == expert_ids[None, :])
    ).astype(jnp.float32)
    gate_weights = route_probs * chosen
    result = resid + gate_weights[:, E + 1 : E + 2] * normed
    const_logits = jnp.dot(narrow, wconst, preferred_element_type=jnp.float32)
    vconst_f = vconst.astype(jnp.float32)
    const_mixes = []
    const_branches = []
    for const_idx in range(CONSTS):
        part_logits = const_logits[:, 2 * const_idx : 2 * const_idx + 2]
        part_exp = jnp.exp(part_logits - jnp.max(part_logits, axis=1, keepdims=True))
        const_mix = part_exp / jnp.sum(part_exp, axis=1, keepdims=True)
        branch = const_mix[:, 0:1] * normed + const_mix[:, 1:2] * vconst_f[:, const_idx][None, :]
        const_mixes.append(const_mix)
        const_branches.append(branch)
        result = result + gate_weights[:, E + 2 + const_idx : E + 3 + const_idx] * branch
    slot_list = []
    filled_list = []
    slot_gate_list = []
    for expert in range(E):
        member = (routes[:, 0] == expert) | (routes[:, 1] == expert)
        place_at = jnp.cumsum(member.astype(jnp.int32)) - 1
        slot_table = (
            jnp.zeros((MOST,), jnp.int32)
            .at[jnp.where(member, place_at, MOST)]
            .set(jnp.arange(TOK_DEV, dtype=jnp.int32), mode="drop")
        )
        filled = jnp.arange(MOST, dtype=jnp.int32) < jnp.sum(member.astype(jnp.int32))
        slot_list.append(slot_table)
        filled_list.append(filled)
        slot_gate_list.append(jnp.where(filled, jnp.take(gate_weights[:, expert], slot_table), 0.0))
    slot_tables = jnp.stack(slot_list, axis=0)
    filled_all = jnp.stack(filled_list, axis=0)
    slot_gates = jnp.stack(slot_gate_list, axis=0)
    expert_kept = []
    out_list = []
    for expert in range(E):
        picked = jnp.take(narrow, slot_tables[expert], axis=0)
        gate_part = jnp.dot(picked, wgate[expert], preferred_element_type=jnp.float32)
        up_part = jnp.dot(picked, wup[expert], preferred_element_type=jnp.float32)
        hidden = (jax.nn.silu(gate_part) * up_part).astype(jnp.bfloat16)
        out_list.append(jnp.dot(hidden, wdown[expert], preferred_element_type=jnp.float32))
        expert_kept.append((picked, gate_part, up_part, hidden))
    expert_outs = jnp.stack(out_list, axis=0)
    for expert in range(E):
        result = result.at[slot_tables[expert]].add(
            slot_gates[expert][:, None] * expert_outs[expert]
        )
    output = result.astype(jnp.bfloat16)
    (
        gain1,
        weight_q,
        weight_k,
        weight_v,
        weight_o,
        gain2,
        router,
        wconst,
        vconst,
        wgate,
        wup,
        wdown,
    ) = collect()
    gain1_f = gain1.astype(jnp.float32)
    gain2_f = gain2.astype(jnp.float32)
    router_f = router.astype(jnp.float32)
    wconst_f = wconst.astype(jnp.float32)
    vconst_f = vconst.astype(jnp.float32)
    grad_out = cotangent.astype(jnp.float32)
    d_gate_cols = [jnp.zeros((TOK_DEV,), jnp.float32) for expert in range(EXPERTS_ALL)]
    d_gate_cols[E + 1] = jnp.sum(grad_out * normed, axis=1)
    d_normed = gate_weights[:, E + 1 : E + 2] * grad_out
    d_const_parts = []
    d_vconst_cols = []
    for const_idx in range(CONSTS):
        const_mix = const_mixes[const_idx]
        gate_col = gate_weights[:, E + 2 + const_idx]
        d_gate_cols[E + 2 + const_idx] = jnp.sum(grad_out * const_branches[const_idx], axis=1)
        d_piece = gate_col[:, None] * grad_out
        d_normed = d_normed + const_mix[:, 0:1] * d_piece
        d_cmix = jnp.stack(
            [
                jnp.sum(d_piece * normed, axis=1),
                jnp.sum(d_piece * vconst_f[:, const_idx][None, :], axis=1),
            ],
            axis=1,
        )
        d_const_parts.append(
            const_mix * (d_cmix - jnp.sum(const_mix * d_cmix, axis=1, keepdims=True))
        )
        d_vconst_cols.append(exact_dot(const_mix[:, 1] * gate_col, grad_out))
    d_const_logits = jnp.concatenate(d_const_parts, axis=1)
    grad_rows_all = jnp.take(grad_out, slot_tables.reshape(-1), axis=0).reshape(
        E, MOST, model_width
    )
    d_slot_gates = jnp.where(filled_all, jnp.sum(grad_rows_all * expert_outs, axis=2), 0.0)
    for expert in range(E):
        d_gate_cols[expert] = (
            jnp.zeros((TOK_DEV,), jnp.float32).at[slot_tables[expert]].add(d_slot_gates[expert])
        )
    d_expert_all = (slot_gates[:, :, None] * grad_rows_all).astype(jnp.bfloat16)
    d_wgate_list = []
    d_wup_list = []
    d_wdown_list = []
    d_picked_list = []
    for expert in range(E):
        picked, gate_part, up_part, hidden = expert_kept[expert]
        d_expert = d_expert_all[expert]
        d_wdown_list.append(jnp.dot(hidden.T, d_expert, preferred_element_type=jnp.float32))
        d_hidden = jnp.dot(d_expert, wdown[expert].T, preferred_element_type=jnp.float32)
        sigmoid_g = jax.nn.sigmoid(gate_part)
        d_up_part = (d_hidden * gate_part * sigmoid_g).astype(jnp.bfloat16)
        d_gate_part = (
            d_hidden * up_part * sigmoid_g * (1.0 + gate_part * (1.0 - sigmoid_g))
        ).astype(jnp.bfloat16)
        d_wgate_list.append(jnp.dot(picked.T, d_gate_part, preferred_element_type=jnp.float32))
        d_wup_list.append(jnp.dot(picked.T, d_up_part, preferred_element_type=jnp.float32))
        d_picked_list.append(
            jnp.dot(d_gate_part, wgate[expert].T, preferred_element_type=jnp.float32)
            + jnp.dot(d_up_part, wup[expert].T, preferred_element_type=jnp.float32)
        )
    d_picked_all = jnp.stack(d_picked_list, axis=0)
    d_wgate_full = jnp.stack(d_wgate_list, axis=0)
    d_wup_full = jnp.stack(d_wup_list, axis=0)
    d_wdown_full = jnp.stack(d_wdown_list, axis=0)
    d_narrow = jnp.zeros((TOK_DEV, model_width), jnp.float32)
    for expert in range(E):
        d_narrow = d_narrow.at[slot_tables[expert]].add(
            jnp.where(filled_all[expert][:, None], d_picked_all[expert], 0.0)
        )
    d_gate_w = jnp.stack(d_gate_cols, axis=1)
    d_probs = d_gate_w * chosen
    d_logits = route_probs * (d_probs - jnp.sum(route_probs * d_probs, axis=1, keepdims=True))
    narrow_f = narrow.astype(jnp.float32)
    d_narrow = d_narrow + exact_dot(d_logits, router_f.T) + exact_dot(d_const_logits, wconst_f.T)
    d_router_full = exact_dot(narrow_f.T, d_logits)
    d_wconst_full = exact_dot(narrow_f.T, d_const_logits)
    d_vconst_full = jnp.stack(d_vconst_cols, axis=1)
    d_mix_full = exact_dot(prev_logits.T, d_logits)
    grad_prev = exact_dot(d_logits, mix_f.T)
    d_normed_total = d_normed + d_narrow
    d_gain2_full = jnp.sum(d_normed_total * unit_two, axis=0)
    d_unit_two = d_normed_total * gain2_f
    d_resid = grad_out + inv_two * (
        d_unit_two - unit_two * jnp.mean(d_unit_two * unit_two, axis=1, keepdims=True)
    )
    d_attn = deal(d_resid.astype(jnp.bfloat16))
    d_wo_full = jnp.dot(mixed.T, d_attn, preferred_element_type=jnp.float32)
    d_mixed = jnp.dot(d_attn, weight_o.T, preferred_element_type=jnp.float32).astype(jnp.bfloat16)

    def attend_back(pair_items):
        q_pair, k_pair, v_pair, dm_pair, lse_pair = pair_items
        scores, query_heads, key_heads = pair_scores(q_pair, k_pair)
        attn_probs = jnp.where(allowed[None], jnp.exp(scores - lse_pair[:, :, None]), 0.0)
        value_heads = v_pair.reshape(CAP, 2, HEAD_DIM)
        dm_heads = dm_pair.reshape(CAP, 2, HEAD_DIM)
        d_p = jnp.einsum("qhd,khd->hqk", dm_heads, value_heads, preferred_element_type=jnp.float32)
        row_delta = jnp.sum(attn_probs * d_p, axis=-1, keepdims=True)
        d_scores = (attn_probs * (d_p - row_delta)).astype(jnp.bfloat16)
        d_q = (
            jnp.einsum("hqk,khd->qhd", d_scores, key_heads, preferred_element_type=jnp.float32)
            * scale
        )
        d_k = (
            jnp.einsum("hqk,qhd->khd", d_scores, query_heads, preferred_element_type=jnp.float32)
            * scale
        )
        d_v = jnp.einsum(
            "hqk,qhd->khd",
            attn_probs.astype(jnp.bfloat16),
            dm_heads,
            preferred_element_type=jnp.float32,
        )
        return (
            d_q.reshape(CAP, pair_width),
            d_k.reshape(CAP, pair_width),
            d_v.reshape(CAP, pair_width),
        )

    dq_pairs, dk_pairs, dv_pairs = lax.map(
        attend_back,
        (by_pairs(query), by_pairs(keyed), by_pairs(values_proj), by_pairs(d_mixed), log_sums),
    )
    d_query = rotate(from_pairs(dq_pairs), cos_table, -sin_table).astype(jnp.bfloat16)
    d_key = rotate(from_pairs(dk_pairs), cos_table, -sin_table).astype(jnp.bfloat16)
    d_value = from_pairs(dv_pairs).astype(jnp.bfloat16)
    d_wq_full = jnp.dot(normed_one.T, d_query, preferred_element_type=jnp.float32)
    d_wk_full = jnp.dot(normed_one.T, d_key, preferred_element_type=jnp.float32)
    d_wv_full = jnp.dot(normed_one.T, d_value, preferred_element_type=jnp.float32)
    d_normed_one = (
        jnp.dot(d_query, weight_q.T, preferred_element_type=jnp.float32)
        + jnp.dot(d_key, weight_k.T, preferred_element_type=jnp.float32)
        + jnp.dot(d_value, weight_v.T, preferred_element_type=jnp.float32)
    )
    d_gain1_full = jnp.sum(d_normed_one * unit_one, axis=0)
    d_unit_one = d_normed_one * gain1_f
    d_dealt = (
        inv_one * (d_unit_one - unit_one * jnp.mean(d_unit_one * unit_one, axis=1, keepdims=True))
    ).astype(jnp.bfloat16)
    grad_tokens = d_resid + give_back(d_dealt).astype(jnp.float32)

    def regroup(grads_in):
        tail_shape = grads_in.shape[1:]
        split_view = grads_in.reshape((groups, dealers, per_shard) + tail_shape)
        return jnp.swapaxes(split_view, 0, 1).reshape((model_width,) + tail_shape)

    mix_tile = jnp.broadcast_to(d_mix_full[None], (dealers, EXPERTS_ALL, EXPERTS_ALL))
    sectioned = (
        lax.psum_scatter(
            regroup(d_gain1_full).astype(jnp.bfloat16), "fsdp", scatter_dimension=0, tiled=True
        ).astype(jnp.float32),
        lax.psum_scatter(
            d_wq_full.astype(jnp.bfloat16), "fsdp", scatter_dimension=0, tiled=True
        ).astype(jnp.float32),
        lax.psum_scatter(
            d_wk_full.astype(jnp.bfloat16), "fsdp", scatter_dimension=0, tiled=True
        ).astype(jnp.float32),
        lax.psum_scatter(
            d_wv_full.astype(jnp.bfloat16), "fsdp", scatter_dimension=0, tiled=True
        ).astype(jnp.float32),
        lax.psum_scatter(
            d_wo_full.astype(jnp.bfloat16), "fsdp", scatter_dimension=0, tiled=True
        ).astype(jnp.float32),
        lax.psum_scatter(
            regroup(d_gain2_full).astype(jnp.bfloat16), "fsdp", scatter_dimension=0, tiled=True
        ).astype(jnp.float32),
        lax.psum_scatter(
            regroup(d_router_full).astype(jnp.bfloat16), "fsdp", scatter_dimension=0, tiled=True
        ).astype(jnp.float32),
        lax.psum_scatter(
            regroup(d_wconst_full).astype(jnp.bfloat16), "fsdp", scatter_dimension=0, tiled=True
        ).astype(jnp.float32),
        lax.psum_scatter(
            regroup(d_vconst_full).astype(jnp.bfloat16), "fsdp", scatter_dimension=0, tiled=True
        ).astype(jnp.float32),
        lax.psum_scatter(
            mix_tile.astype(jnp.bfloat16), "fsdp", scatter_dimension=0, tiled=True
        ).astype(jnp.float32),
        lax.psum_scatter(
            d_wgate_full.astype(jnp.bfloat16), "fsdp", scatter_dimension=1, tiled=True
        ).astype(jnp.float32),
        lax.psum_scatter(
            d_wup_full.astype(jnp.bfloat16), "fsdp", scatter_dimension=1, tiled=True
        ).astype(jnp.float32),
        lax.psum_scatter(
            d_wdown_full.astype(jnp.bfloat16), "fsdp", scatter_dimension=2, tiled=True
        ).astype(jnp.float32),
    )
    s_g1, s_q, s_k, s_v, s_o, s_g2, s_r, s_c, s_vc, s_mix, s_gate, s_up, s_down = sectioned
    summed = (
        lax.psum_scatter(s_g1.astype(jnp.bfloat16), "grp", scatter_dimension=0, tiled=True).astype(
            jnp.float32
        ),
        lax.psum_scatter(s_q.astype(jnp.bfloat16), "grp", scatter_dimension=1, tiled=True).astype(
            jnp.float32
        ),
        lax.psum_scatter(s_k.astype(jnp.bfloat16), "grp", scatter_dimension=1, tiled=True).astype(
            jnp.float32
        ),
        lax.psum_scatter(s_v.astype(jnp.bfloat16), "grp", scatter_dimension=1, tiled=True).astype(
            jnp.float32
        ),
        lax.psum_scatter(s_o.astype(jnp.bfloat16), "grp", scatter_dimension=1, tiled=True).astype(
            jnp.float32
        ),
        lax.psum_scatter(s_g2.astype(jnp.bfloat16), "grp", scatter_dimension=0, tiled=True).astype(
            jnp.float32
        ),
        lax.psum_scatter(s_r.astype(jnp.bfloat16), "grp", scatter_dimension=0, tiled=True).astype(
            jnp.float32
        ),
        lax.psum_scatter(s_c.astype(jnp.bfloat16), "grp", scatter_dimension=0, tiled=True).astype(
            jnp.float32
        ),
        lax.psum_scatter(s_vc.astype(jnp.bfloat16), "grp", scatter_dimension=0, tiled=True).astype(
            jnp.float32
        ),
        lax.psum_scatter(
            jnp.broadcast_to(s_mix, (groups, EXPERTS_ALL, EXPERTS_ALL)).astype(jnp.bfloat16),
            "grp",
            scatter_dimension=0,
            tiled=True,
        ).astype(jnp.float32),
    )
    (
        grad_gain_one,
        grad_query,
        grad_key,
        grad_value,
        grad_out_proj,
        grad_gain_two,
        grad_router,
        grad_const,
        grad_vconst,
        mix_part,
    ) = summed
    grad_mix = mix_part[0]
    grad_gate, grad_up, grad_down = (
        lax.psum_scatter(
            s_gate.astype(jnp.bfloat16), "grp", scatter_dimension=2, tiled=True
        ).astype(jnp.float32),
        lax.psum_scatter(s_up.astype(jnp.bfloat16), "grp", scatter_dimension=2, tiled=True).astype(
            jnp.float32
        ),
        lax.psum_scatter(
            s_down.astype(jnp.bfloat16), "grp", scatter_dimension=1, tiled=True
        ).astype(jnp.float32),
    )
    return (
        output,
        grad_tokens,
        grad_prev,
        grad_gain_one,
        grad_query,
        grad_key,
        grad_value,
        grad_out_proj,
        grad_gain_two,
        grad_router,
        grad_mix,
        grad_const,
        grad_vconst,
        grad_gate,
        grad_up,
        grad_down,
    )


def solution(mesh):
    return jax.shard_map(
        per_device,
        mesh=mesh,
        in_specs=(
            P(("grp", "fsdp"), None),
            P(("grp", "fsdp"), None),
            P(("grp", "fsdp"), None),
            P("grp", None),
            P("grp", None),
            P(("grp", "fsdp"), None),
            P(("grp", "fsdp")),
            P("fsdp", "grp"),
            P("fsdp", "grp"),
            P("fsdp", "grp"),
            P("fsdp", "grp"),
            P(("grp", "fsdp")),
            P(("grp", "fsdp"), None),
            P(),
            P(("grp", "fsdp"), None),
            P(("grp", "fsdp"), None),
            P(None, "fsdp", "grp"),
            P(None, "fsdp", "grp"),
            P(None, "grp", "fsdp"),
        ),
        out_specs=(
            P(("grp", "fsdp"), None),
            P(("grp", "fsdp"), None),
            P(("grp", "fsdp"), None),
            P(("grp", "fsdp")),
            P("fsdp", "grp"),
            P("fsdp", "grp"),
            P("fsdp", "grp"),
            P("fsdp", "grp"),
            P(("grp", "fsdp")),
            P(("grp", "fsdp"), None),
            P(),
            P(("grp", "fsdp"), None),
            P(("grp", "fsdp"), None),
            P(None, "fsdp", "grp"),
            P(None, "fsdp", "grp"),
            P(None, "grp", "fsdp"),
        ),
        check_vma=False,
    )
```

profile of v0, /device:TPU:0, one launch (start us, length us, event | category | flops | bytes accessed | tf_op | source)
XLA Modules:
  0.0 2877.5 jit_solution(10098351158578201075)
XLA Ops:
  24.6 16.1 all_gather.115
  123.0 19.6 all-gather.25.cloned.1.call-done
  171.9 62.1 %all-gather.37.cloned.1.call-done = bf16[8,768,256]{2,1,0:T(8,128)(2,1)} async-done(((bf16[8,192,256]{2,1,0:T(8,128)(2,1)}), bf16[8,768,256]{2,1,0:T(8,128)(2,1)}) %all-gather.37.cloned.1.call-update) | async-done | bytes 3145744 | tf_op jit(solution)/shard_map/all_gather | solution.py:142
  234.1 63.6 %all-gather.33.cloned.1.call-done = bf16[8,768,256]{2,1,0:T(8,128)(2,1)} async-done(((bf16[8,192,256]{2,1,0:T(8,128)(2,1)}), bf16[8,768,256]{2,1,0:T(8,128)(2,1)}) %all-gather.33.cloned.1.call-update) | async-done | bytes 3145744 | tf_op jit(solution)/shard_map/all_gather | solution.py:141
  297.8 63.7 %all-gather.41.cloned.1.call-done = bf16[8,256,768]{1,2,0:T(8,128)(2,1)} async-done(((bf16[8,256,192]{1,2,0:T(8,128)(2,1)}), bf16[8,256,768]{1,2,0:T(8,128)(2,1)}) %all-gather.41.cloned.1.call-update) | async-done | bytes 3145744 | tf_op jit(solution)/shard_map/all_gather | solution.py:143
  547.4 128.6 %all-gather.35.cloned.1.call-done = bf16[8,768,2048]{2,1,0:T(8,128)(2,1)} async-done(((bf16[8,768,256]{2,1,0:T(8,128)(2,1)}), bf16[8,768,2048]{2,1,0:T(8,128)(2,1)}) %all-gather.35.cloned.1.call-update) | async-done | bytes 25165840 | tf_op jit(solution)/shard_map/all_gather | solution.py:171
  729.3 78.8 %all-gather.43.cloned.1.call-done = bf16[8,2048,768]{1,2,0:T(8,128)(2,1)} async-done(((bf16[8,256,768]{1,2,0:T(8,128)(2,1)}), bf16[8,2048,768]{1,2,0:T(8,128)(2,1)}) %all-gather.43.cloned.1.call-update) | async-done | bytes 25165840 | tf_op jit(solution)/shard_map/all_gather | solution.py:173
  928.8 42.3 %all-gather.45.cloned.1.call-done = bf16[1280,768]{1,0:T(8,128)(2,1)} async-done(((bf16[320,768]{1,0:T(8,128)(2,1)}), bf16[1280,768]{1,0:T(8,128)(2,1)}) %all-gather.45.cloned.1.call-update) | async-done | bytes 1966096 | tf_op jit(solution)/shard_map/all_gather | solution.py:114
  984.4 45.9 %while.29 = (s32[]{:T(128)}, f32[6,384,128]{1,2,0:T(8,128)}, f32[6,384,128]{1,2,0:T(8,128)}, bf16[6,384,128]{1,2,0:T(8,128)(2,1)}, bf16[6,384,128]{1,2,0:T(8,128...) while((s32[]{:T(128)}, f32[6,384,128]{1,2,0:T(8,128)}, ...), condition=%wide.region_89.94_spmd.clone, body=%wide.region_87.93_spmd.clone.sunk | while | flops 192380160 | bytes 16827864 | solution.py:446
  1066.4 32.6 %copy.190 = bf16[8,2048,768]{1,0,2:T(8,128)(2,1)} copy(bf16[8,2048,768]{2,1,0:T(8,128)(2,1)} %bitcast_dynamic-update-slice_fusion.1) | data formatting | bytes 50331648 | tf_op jit(solution)/shard_map/stack | solution.py:391
  1177.9 361.1 %reduce-scatter.57.cloned.1.call-done = bf16[8,2048,192]{1,0,2:T(8,128)(2,1)} async-done(((bf16[8,2048,768]{1,0,2:T(8,128)(2,1)}), bf16[8,2048,192]{1,0,2:T(8,128)(2,1)}) %reduce-scatter.57.cloned.1.call-update) | async-done | bytes 6291472 | tf_op jit(solution)/shard_map/reduce_scatter | solution.py:511
  1539.0 418.4 %reduce-scatter.53.cloned.1.call-done = bf16[8,192,2048]{2,1,0:T(8,128)(2,1)} async-done(((bf16[8,768,2048]{2,1,0:T(8,128)(2,1)}), bf16[8,192,2048]{2,1,0:T(8,128)(2,1)}) %reduce-scatter.53.cloned.1.call-update) | async-done | bytes 6291472 | tf_op jit(solution)/shard_map/reduce_scatter | solution.py:508
  1957.5 418.6 %reduce-scatter.49.cloned.1.call-done = bf16[8,192,2048]{2,1,0:T(8,128)(2,1)} async-done(((bf16[8,768,2048]{2,1,0:T(8,128)(2,1)}), bf16[8,192,2048]{2,1,0:T(8,128)(2,1)}) %reduce-scatter.49.cloned.1.call-update) | async-done | bytes 6291472 | tf_op jit(solution)/shard_map/reduce_scatter | solution.py:505
  2377.6 22.0 reduce-scatter.73.cloned.1.call-done
  2400.5 19.6 reduce-scatter.71.cloned.1.call-done
  2454.3 20.5 reduce-scatter.69.cloned.1.call-done
  2484.9 22.3 all-reduce.19
  2511.9 34.7 %reduce-scatter.65.cloned.1.call-done = bf16[96,192]{1,0:T(8,128)(2,1)} async-done(((bf16[768,192]{1,0:T(8,128)(2,1)}), bf16[96,192]{1,0:T(8,128)(2,1)}) %reduce-scatter.65.cloned.1.call-update) | async-done | bytes 36880
  2548.1 35.4 %reduce-scatter.63.cloned.1.call-done = bf16[96,192]{1,0:T(8,128)(2,1)} async-done(((bf16[768,192]{1,0:T(8,128)(2,1)}), bf16[96,192]{1,0:T(8,128)(2,1)}) %reduce-scatter.63.cloned.1.call-update) | async-done | bytes 36880
  2585.1 35.9 %reduce-scatter.61.cloned.1.call-done = bf16[96,192]{1,0:T(8,128)(2,1)} async-done(((bf16[768,192]{1,0:T(8,128)(2,1)}), bf16[96,192]{1,0:T(8,128)(2,1)}) %reduce-scatter.61.cloned.1.call-update) | async-done | bytes 36880
  2622.6 50.9 %all-gather.47.cloned.1.call-done = bf16[1536,768]{1,0:T(8,128)(2,1)} async-done(((bf16[384,768]{1,0:T(8,128)(2,1)}), bf16[1536,768]{1,0:T(8,128)(2,1)}) %all-gather.47.cloned.1.call-update) | async-done | bytes 2359312 | tf_op jit(solution)/shard_map/all_gather | solution.py:121
  2679.5 58.0 %reduce-scatter.59.cloned.1.call-done = bf16[8,256,192]{1,0,2:T(8,128)(2,1)} async-done(((bf16[8,2048,192]{1,0,2:T(8,128)(2,1)}), bf16[8,256,192]{1,0,2:T(8,128)(2,1)}) %reduce-scatter.59.cloned.1.call-update) | async-done | bytes 786448 | tf_op jit(solution)/shard_map/reduce_scatter | solution.py:571
  2739.9 63.1 %reduce-scatter.55.cloned.1.call-done = bf16[8,192,256]{2,1,0:T(8,128)(2,1)} async-done(((bf16[8,192,2048]{2,1,0:T(8,128)(2,1)}), bf16[8,192,256]{2,1,0:T(8,128)(2,1)}) %reduce-scatter.55.cloned.1.call-update) | async-done | bytes 786448 | tf_op jit(solution)/shard_map/reduce_scatter | solution.py:568
  2805.4 62.6 %reduce-scatter.51.cloned.1.call-done = bf16[8,192,256]{2,1,0:T(8,128)(2,1)} async-done(((bf16[8,192,2048]{2,1,0:T(8,128)(2,1)}), bf16[8,192,256]{2,1,0:T(8,128)(2,1)}) %reduce-scatter.51.cloned.1.call-update) | async-done | bytes 786448 | tf_op jit(solution)/shard_map/reduce_scatter | solution.py:565
  (1130 shorter events, 737.1 us)
Async XLA Ops:
  73.6 224.1 %all-gather.33.cloned.1.call-start = ((), (), s32[]{:S(2)}) async-start(), calls=%async_computation.25 | async-start | bytes 3932160 | tf_op jit(solution)/shard_map/all_gather | solution.py:141
  74.3 287.1 %all-gather.41.cloned.1.call-start = ((), (), s32[]{:S(2)}) async-start(), calls=%async_computation.29 | async-start | bytes 3932160 | tf_op jit(solution)/shard_map/all_gather | solution.py:143
  75.1 403.6 %all-gather.31.cloned.1.call-start = ((), (), s32[]{:S(2)}) async-start(), calls=%async_computation.24 | async-start | bytes 2949120 | tf_op jit(solution)/shard_map/all_gather | solution.py:121
  171.8 372.0 %all-gather.39.cloned.1.call-start = ((), (), s32[]{:S(2)}) async-start(), calls=%async_computation.28 | async-start | bytes 28311552 | tf_op jit(solution)/shard_map/all_gather | solution.py:172
  234.0 441.9 %all-gather.35.cloned.1.call-start = ((), (), s32[]{:S(2)}) async-start(), calls=%async_computation.26 | async-start | bytes 28311552 | tf_op jit(solution)/shard_map/all_gather | solution.py:171
  297.7 510.3 %all-gather.43.cloned.1.call-start = ((), (), s32[]{:S(2)}) async-start(), calls=%async_computation.30 | async-start | bytes 28311552 | tf_op jit(solution)/shard_map/all_gather | solution.py:173
  361.5 609.6 %all-gather.45.cloned.1.call-start = ((), (), s32[]{:S(2)}) async-start(), calls=%async_computation.31 | async-start | bytes 2457600 | tf_op jit(solution)/shard_map/all_gather | solution.py:114
  927.4 229.1 %reduce-scatter.45.cloned.1.call-start = ((), (), s32[]{:S(2)}) async-start(), calls=%async_computation.37 | async-start | bytes 20480 | tf_op jit(solution)/shard_map/reduce_scatter | solution.py:502
  928.4 231.1 %reduce-scatter.43.cloned.1.call-start = ((), (), s32[]{:S(2)}) async-start(), calls=%async_computation.36 | async-start | bytes 1474560 | tf_op jit(solution)/shard_map/reduce_scatter | solution.py:487
  1043.3 495.6 %reduce-scatter.57.cloned.1.call-start = ((), (), s32[]{:S(2)}) async-start(), calls=%async_computation.43 | async-start | bytes 31457280 | tf_op jit(solution)/shard_map/reduce_scatter | solution.py:511
  1099.1 858.3 %reduce-scatter.53.cloned.1.call-start = ((), (), s32[]{:S(2)}) async-start(), calls=%async_computation.41 | async-start | bytes 31457280 | tf_op jit(solution)/shard_map/reduce_scatter | solution.py:508
  1123.3 1252.8 %reduce-scatter.49.cloned.1.call-start = ((), (), s32[]{:S(2)}) async-start(), calls=%async_computation.39 | async-start | bytes 31457280 | tf_op jit(solution)/shard_map/reduce_scatter | solution.py:505
  1146.6 1253.0 %reduce-scatter.73.cloned.1.call-start = ((), (), s32[]{:S(2)}) async-start(), calls=%async_computation.51 | async-start | bytes 245760
  1155.0 1265.1 %reduce-scatter.71.cloned.1.call-start = ((), (), s32[]{:S(2)}) async-start(), calls=%async_computation.50 | async-start | bytes 245760
  1156.5 1296.6 %reduce-scatter.47.cloned.1.call-start = ((), (), s32[]{:S(2)}) async-start(), calls=%async_computation.38 | async-start | bytes 36864 | tf_op jit(solution)/shard_map/reduce_scatter | solution.py:544
  1157.9 1316.9 %reduce-scatter.69.cloned.1.call-start = ((), (), s32[]{:S(2)}) async-start(), calls=%async_computation.49 | async-start | bytes 245760
  1159.4 1351.0 %reduce-scatter.67.cloned.1.call-start = ((), (), s32[]{:S(2)}) async-start(), calls=%async_computation.48 | async-start | bytes 442368
  1161.4 1385.2 %reduce-scatter.65.cloned.1.call-start = ((), (), s32[]{:S(2)}) async-start(), calls=%async_computation.47 | async-start | bytes 442368
  1163.4 1420.1 %reduce-scatter.63.cloned.1.call-start = ((), (), s32[]{:S(2)}) async-start(), calls=%async_computation.46 | async-start | bytes 442368
  1168.5 1452.5 %reduce-scatter.61.cloned.1.call-start = ((), (), s32[]{:S(2)}) async-start(), calls=%async_computation.45 | async-start | bytes 442368
  1175.2 1498.3 %all-gather.47.cloned.1.call-start = ((), (), s32[]{:S(2)}) async-start(), calls=%async_computation.32 | async-start | bytes 2949120 | tf_op jit(solution)/shard_map/all_gather | solution.py:121
  1177.8 1559.7 %reduce-scatter.59.cloned.1.call-start = ((), (), s32[]{:S(2)}) async-start(), calls=%async_computation.44 | async-start | bytes 7077888 | tf_op jit(solution)/shard_map/reduce_scatter | solution.py:571
  1539.0 1264.0 %reduce-scatter.55.cloned.1.call-start = ((), (), s32[]{:S(2)}) async-start(), calls=%async_computation.42 | async-start | bytes 7077888 | tf_op jit(solution)/shard_map/reduce_scatter | solution.py:568
  1957.4 910.6 %reduce-scatter.51.cloned.1.call-start = ((), (), s32[]{:S(2)}) async-start(), calls=%async_computation.40 | async-start | bytes 7077888 | tf_op jit(solution)/shard_map/reduce_scatter | solution.py:565
  (255 other events, 7762.0 us)
Sparse Core Ops, SparseCore 0:
  9.6 54.2 all-gather.20
  170.5 63.4 all-gather.36
  235.5 62.1 all-gather.32
  299.3 62.1 all-gather.40
  363.6 49.2 all-gather.30
  414.6 129.1 all-gather.38
  545.7 130.2 all-gather.34
  677.7 130.2 all-gather.42
  927.5 43.5 all-gather.44
  1033.7 28.0 reduce-scatter.40
  1064.6 27.8 reduce-scatter.38
  1095.4 27.8 reduce-scatter.36
  1125.8 413.0 reduce-scatter.56
  1541.2 416.1 reduce-scatter.52
  1959.9 416.1 reduce-scatter.48
  2423.5 29.4 reduce-scatter.46
  2477.7 32.0 reduce-scatter.66
  2512.7 33.8 reduce-scatter.64
  2549.6 33.8 reduce-scatter.62
  2587.1 33.8 reduce-scatter.60
  2623.0 50.4 all-gather.46
  2676.9 60.5 reduce-scatter.58
  2741.3 61.7 reduce-scatter.54
  2806.2 61.7 reduce-scatter.50
  (9 shorter events, 198.1 us)
where the time goes:
time: 2890 us; the launch traced here: 2880 us
  waiting for transfers between devices  2100 us (73%)
  matrix products  272 us (9%)
  local copies, waits for them, and re-layouts  184 us (6%)
  blocking collectives  173 us (6%)
  other arithmetic  128 us (4%)
    reduce_scatter x1, waiting for transfers between devices, per_device(): lax.psum_scatter(d_wgate_full.astype(jnp.bfloat16), 'fsdp', scatter_dimen...  419 us
    reduce_scatter x1, waiting for transfers between devices, per_device(): lax.psum_scatter(d_wup_full.astype(jnp.bfloat16), 'fsdp', scatter_dimensi...  418 us
    reduce_scatter x1, waiting for transfers between devices, per_device(): lax.psum_scatter(d_wdown_full.astype(jnp.bfloat16), 'fsdp', scatter_dimen...  361 us
    unnamed x40, waiting for transfers between devices  171 us
    all_gather x1, waiting for transfers between devices, collect(): lax.all_gather(part_gate, 'grp', axis=2, tiled=True)  129 us
    all_gather x1, waiting for transfers between devices, collect(): lax.all_gather(part_down, 'grp', axis=1, tiled=True)  78.8 us
    all_gather x1, waiting for transfers between devices, collect(): lax.all_gather(down_in, 'fsdp', axis=2, tiled=True)  63.7 us
    all_gather x1, waiting for transfers between devices, collect(): lax.all_gather(gate_in, 'fsdp', axis=1, tiled=True)  63.6 us
  transfers between devices with their start and end apart: 33, of which 23 were waited for; matrix products, arithmetic and copies ran while one was open for 16% of the time, Pallas kernels for 0%

commit v1 on v0

--- a/solution.py
+++ b/solution.py
@@ -3,6 +3,8 @@
 import jax
 import jax.numpy as jnp
 from jax import lax
+from jax.experimental import pallas as pl
+from jax.experimental.pallas import tpu as pltpu
 from jax.sharding import PartitionSpec as P
 
 HEADS = 12
@@ -592,9 +594,811 @@
     )
 
 
+HALO = 256
+KEYS = HALO + TOK_DEV
+ROWS = E * MOST
+WIDE = 896
+NEG = -1e30
+F32 = jnp.float32
+BF16 = jnp.bfloat16
+NT = (((1,), (1,)), ((), ()))
+TN = (((0,), (0,)), ((), ()))
+NN = (((1,), (0,)), ((), ()))
+
+
+def mm(a, b, dims=NN):
+    return lax.dot_general(a, b, dims, preferred_element_type=F32)
+
+
+def lane_iota(rows, width=128):
+    return lax.broadcasted_iota(jnp.int32, (rows, width), 1)
+
+
+def pick(values, lane_mask):
+    return jnp.sum(jnp.where(lane_mask, values, 0.0), axis=1, keepdims=True)
+
+
+def split_mm(mat, wide, dims):
+    high = wide.astype(BF16)
+    low = (wide - high.astype(F32)).astype(BF16)
+    return mm(mat, high, dims) + mm(mat, low, dims)
+
+
+def params(mb, **kw):
+    return pltpu.CompilerParams(vmem_limit_bytes=mb << 20, **kw)
+
+
+def whole(count):
+    return [pl.BlockSpec(memory_space=pltpu.VMEM) for _ in range(count)]
+
+
+def sds(shape, dtype):
+    return jax.ShapeDtypeStruct(shape, dtype)
+
+
+def prepare_kernel(own_ref, routes_ref, cot_ref, wg_ref, wu_ref, wd_ref, slots_ref, *outs):
+    own = own_ref[0]
+    g_refs, w_refs = outs[:E], outs[E:]
+    lanes = lane_iota(TOK_DEV)
+    r0 = routes_ref[:, 0:1]
+    r1 = routes_ref[:, 1:2]
+    hot0 = lanes == r0
+    hot1 = lanes == r1
+    member = jnp.where(hot0 | hot1, 1.0, 0.0).astype(BF16)
+    earlier = (
+        lax.broadcasted_iota(jnp.int32, (TOK_DEV, TOK_DEV), 1)
+        < lax.broadcasted_iota(jnp.int32, (TOK_DEV, TOK_DEV), 0)
+    )
+    rank = mm(jnp.where(earlier, 1.0, 0.0).astype(BF16), member)
+    c0 = jnp.where(
+        r0 < E, lax.rem(r0 - own + E, E) * MOST + pick(rank, hot0).astype(jnp.int32), -1
+    )
+    c1 = jnp.where(
+        r1 < E, lax.rem(r1 - own + E, E) * MOST + pick(rank, hot1).astype(jnp.int32), -1
+    )
+    slots_ref[...] = jnp.where(lanes == 0, c0, jnp.where(lanes == 1, c1, -1))
+    cols = lane_iota(TOK_DEV, ROWS)
+    spread = jnp.where((cols == c0) | (cols == c1), 1.0, 0.0).astype(BF16)
+    rows = mm(spread, cot_ref[...], TN).astype(BF16)
+    for k in range(E):
+        g_refs[k][...] = rows[k * MOST : (k + 1) * MOST]
+        expert = lax.rem(own + k, E)
+        w_refs[k][0] = wg_ref[expert]
+        w_refs[k][1] = wu_ref[expert]
+        w_refs[k][2] = wd_ref[expert].T
+
+
+def prepare(own, routes, cotangent, w_gate, w_up, w_down):
+    tile = w_gate.shape[1:]
+    width = cotangent.shape[1]
+    return pl.pallas_call(
+        prepare_kernel,
+        out_shape=[sds((TOK_DEV, 128), jnp.int32)]
+        + [sds((MOST, width), BF16)] * E
+        + [sds((3,) + tile, BF16)] * E,
+        in_specs=[pl.BlockSpec(memory_space=pltpu.SMEM)] + whole(5),
+        out_specs=whole(1 + 2 * E),
+        compiler_params=params(56),
+        name="prepare",
+    )(own, routes, cotangent, w_gate, w_up, w_down)
+
+
+def turn(values, cos, sin):
+    half = HEAD_DIM // 2
+    width = values.shape[1]
+    reps = width // 128
+    front = lax.rem(lane_iota(values.shape[0], width), HEAD_DIM) < half
+    swapped = jnp.where(
+        front, pltpu.roll(values, width - half, 1), pltpu.roll(values, half, 1)
+    )
+    cos_w = jnp.concatenate([cos] * reps, axis=1)
+    sin_w = jnp.concatenate([sin] * reps, axis=1)
+    return values * cos_w + swapped * sin_w
+
+
+QBLOCKS = [(0, 128), (128, 128), (256, 64)]
+
+
+def allowed_mask(pos_ref, first, count):
+    ii = lax.broadcasted_iota(jnp.int32, (count, 384), 0) + HALO
+    jj = lax.broadcasted_iota(jnp.int32, (count, 384), 1)
+    return (jj <= ii) & (jj >= ii - pos_ref[pl.ds(first, count), 0:1])
+
+
+def key_span(first):
+    return min(384, KEYS - first)
+
+
+def forward_kernel(
+    tok_ref,
+    halo_ref,
+    g1_ref,
+    g2_ref,
+    cos_ref,
+    sin_ref,
+    pos_ref,
+    wq_ref,
+    wk_ref,
+    wv_ref,
+    wo_ref,
+    wr_ref,
+    vc_ref,
+    mixed_prev_ref,
+    routes_ref,
+    slots_ref,
+    q_ref,
+    k_ref,
+    v_ref,
+    n1_ref,
+    inv1_ref,
+    mix_ref,
+    lse_ref,
+    resid_ref,
+    part_ref,
+    probs_ref,
+    cols_ref,
+    *x_refs,
+):
+    scale = HEAD_DIM ** (-0.5)
+    rows = jnp.concatenate([halo_ref[...], tok_ref[...]], axis=0).astype(F32)
+    inv1 = lax.rsqrt(jnp.mean(rows * rows, axis=1, keepdims=True) + NORM_EPS)
+    inv1_ref[...] = jnp.broadcast_to(inv1, (KEYS, 128))
+    n1_ref[...] = (rows * inv1 * g1_ref[...]).astype(BF16)
+
+    def project(i, _):
+        span = pl.ds(pl.multiple_of(i * 256, 256), 256)
+        cos = cos_ref[...]
+        sin = sin_ref[...]
+        q = mm(n1_ref[HALO:, :], wq_ref[:, span])
+        q_ref[:, span] = turn(q, cos[HALO:], sin[HALO:]).astype(BF16)
+        k = mm(n1_ref[...], wk_ref[:, span])
+        k_ref[:, span] = turn(k, cos, sin).astype(BF16)
+        v_ref[:, span] = mm(n1_ref[...], wv_ref[:, span]).astype(BF16)
+        return 0
+
+    lax.fori_loop(0, q_ref.shape[1] // 256, project, 0)
+    lse_ref[...] = jnp.zeros((TOK_DEV, 128), F32)
+
+    def pair(p, _):
+        span = pl.ds(pl.multiple_of(p * 128, 128), 128)
+        for first, count in QBLOCKS:
+            keys = key_span(first)
+            ok = allowed_mask(pos_ref, first, count)[:, :keys]
+            q = q_ref[pl.ds(first, count), span]
+            k = k_ref[pl.ds(first, keys), span]
+            v = v_ref[pl.ds(first, keys), span]
+            lane = lane_iota(count)
+            out = None
+            lse = lse_ref[pl.ds(first, count), :]
+            for h in range(2):
+                mine = (lane < HEAD_DIM) if h == 0 else (lane >= HEAD_DIM)
+                qh = jnp.where(mine, q, jnp.zeros_like(q))
+                s = jnp.where(ok, mm(qh, k, NT) * scale, NEG)
+                top = jnp.max(s, axis=1, keepdims=True)
+                e = jnp.exp(s - top)
+                total = jnp.sum(e, axis=1, keepdims=True)
+                o = mm((e / total).astype(BF16), v)
+                out = o if h == 0 else jnp.where(mine, o, out)
+                lse = jnp.where(lane == 2 * p + h, top + jnp.log(total), lse)
+            mix_ref[pl.ds(first, count), span] = out.astype(BF16)
+            lse_ref[pl.ds(first, count), :] = lse
+        return 0
+
+    lax.fori_loop(0, HEADS // 2, pair, 0)
+    attn_out = mm(mix_ref[...], wo_ref[...]).astype(BF16)
+    resid = tok_ref[...].astype(F32) + attn_out.astype(F32)
+    resid_ref[...] = resid
+    inv2 = lax.rsqrt(jnp.mean(resid * resid, axis=1, keepdims=True) + NORM_EPS)
+    normed = resid * inv2 * g2_ref[...]
+    narrow = normed.astype(BF16)
+    lanes = lane_iota(TOK_DEV)
+    raw = mm(narrow, wr_ref[...])
+    logits = jnp.where(lanes < EXPERTS_ALL, raw + mixed_prev_ref[...], NEG)
+    top = jnp.max(logits, axis=1, keepdims=True)
+    e = jnp.exp(logits - top)
+    probs = e / jnp.sum(e, axis=1, keepdims=True)
+    probs_ref[...] = probs
+    r0 = routes_ref[:, 0:1]
+    r1 = routes_ref[:, 1:2]
+    gate0 = pick(probs, lanes == r0)
+    gate1 = pick(probs, lanes == r1)
+
+    def gate_of(expert):
+        return jnp.where(r0 == expert, gate0, 0.0) + jnp.where(r1 == expert, gate1, 0.0)
+
+    gate_id = gate_of(E + 1)
+    part = resid + gate_id * normed
+    cols = jnp.where(lanes == 0, gate0, 0.0)
+    cols = jnp.where(lanes == 1, gate1, cols)
+    cols = jnp.where(lanes == 2, gate_id, cols)
+    cols = jnp.where(lanes == 3, inv2, cols)
+    for c in range(CONSTS):
+        la = pick(raw, lanes == 16 + 2 * c)
+        lb = pick(raw, lanes == 17 + 2 * c)
+        big = jnp.maximum(la, lb)
+        ea = jnp.exp(la - big)
+        eb = jnp.exp(lb - big)
+        ma = ea / (ea + eb)
+        mb = eb / (ea + eb)
+        gate_c = gate_of(E + 2 + c)
+        part = part + gate_c * (ma * normed + mb * vc_ref[c : c + 1, :])
+        cols = jnp.where(lanes == 4 + 3 * c, gate_c, cols)
+        cols = jnp.where(lanes == 5 + 3 * c, ma, cols)
+        cols = jnp.where(lanes == 6 + 3 * c, mb, cols)
+    part_ref[...] = part
+    cols_ref[...] = cols
+    c0 = slots_ref[:, 0:1]
+    c1 = slots_ref[:, 1:2]
+    slot = lane_iota(TOK_DEV, ROWS)
+    hot0 = jnp.where(slot == c0, 1.0, 0.0).astype(BF16)
+    hot1 = jnp.where(slot == c1, 1.0, 0.0).astype(BF16)
+
+    def two_parts(gate):
+        high = gate.astype(BF16).astype(F32)
+        return jnp.where(lanes == 0, high, jnp.where(lanes == 1, gate - high, 0.0)).astype(BF16)
+
+    x = mm(hot0 + hot1, narrow, TN).astype(BF16)
+    gates = (mm(hot0, two_parts(gate0), TN) + mm(hot1, two_parts(gate1), TN)).astype(BF16)
+    for k in range(E):
+        x_refs[k][:, : x.shape[1]] = x[k * MOST : (k + 1) * MOST]
+        x_refs[k][:, x.shape[1] :] = gates[k * MOST : (k + 1) * MOST]
+
+
+def forward(tok, halo, g1, g2, cos, sin, pos, wq, wk, wv, wo, wr, vc, mixed_prev, routes, slots):
+    width = tok.shape[1]
+    return pl.pallas_call(
+        forward_kernel,
+        out_shape=[
+            sds((TOK_DEV, width), BF16),
+            sds((KEYS, width), BF16),
+            sds((KEYS, width), BF16),
+            sds((KEYS, width), BF16),
+            sds((KEYS, 128), F32),
+            sds((TOK_DEV, width), BF16),
+            sds((TOK_DEV, 128), F32),
+            sds((TOK_DEV, width), F32),
+            sds((TOK_DEV, width), F32),
+            sds((TOK_DEV, 128), F32),
+            sds((TOK_DEV, 128), F32),
+        ]
+        + [sds((MOST, WIDE), BF16)] * E,
+        in_specs=whole(16),
+        out_specs=whole(11 + E),
+        compiler_params=params(56),
+        name="forward",
+    )(tok, halo, g1, g2, cos, sin, pos, wq, wk, wv, wo, wr, vc, mixed_prev, routes, slots)
+
+
+def expert_kernel(own_ref, *refs):
+    lo = 4
+    x_refs = refs[:lo]
+    g_refs = refs[lo : 2 * lo]
+    t_refs = refs[2 * lo : 2 * lo + E]
+    od_refs = refs[2 * lo + E : 3 * lo + E]
+    gt_refs = refs[3 * lo + E : 3 * lo + 2 * E]
+    w_refs = refs[3 * lo + 2 * E : 3 * lo + 2 * E + 3]
+    acc_refs = refs[3 * lo + 2 * E + 3 :]
+    own = own_ref[0]
+    tile = t_refs[0].shape[1:]
+    width = w_refs[0].shape[0]
+    his = w_refs[0].shape[1] // tile[1]
+
+    def place(k):
+        source = lax.rem(own - k + E, E)
+        row = pl.multiple_of(source // his * tile[0], tile[0])
+        col = pl.multiple_of(lax.rem(source, his) * tile[1], tile[1])
+        return pl.ds(row, tile[0]), pl.ds(col, tile[1])
+
+    for k in range(E):
+        at = place(k)
+        for w in range(3):
+            w_refs[w][at] = t_refs[k][w]
+    for w in range(3):
+        acc_refs[w][...] = jnp.zeros_like(acc_refs[w])
+    rows = x_refs[0].shape[0]
+    step = rows // 2
+    for j in range(lo):
+
+        def block(i, _, j=j):
+            at = pl.ds(pl.multiple_of(i * step, step), step)
+            x = x_refs[j][at, :width]
+            gate = (
+                x_refs[j][at, width : width + 1].astype(F32)
+                + x_refs[j][at, width + 1 : width + 2].astype(F32)
+            )
+            d_exp = (g_refs[j][at, :].astype(F32) * gate).astype(BF16)
+            wg = w_refs[0][...]
+            wu = w_refs[1][...]
+            wd = w_refs[2][...]
+            a = mm(x, wg)
+            b = mm(x, wu)
+            sig = 1.0 / (1.0 + jnp.exp(-a))
+            hidden = (a * sig * b).astype(BF16)
+            od_refs[j][at, :width] = mm(hidden, wd, NT).astype(BF16)
+            dh = mm(d_exp, wd)
+            d_up = (dh * a * sig).astype(BF16)
+            d_gate = (dh * b * sig * (1.0 + a * (1.0 - sig))).astype(BF16)
+            od_refs[j][at, width:] = (mm(d_gate, wg, NT) + mm(d_up, wu, NT)).astype(BF16)
+            acc_refs[0][...] += mm(x, d_gate, TN)
+            acc_refs[1][...] += mm(x, d_up, TN)
+            acc_refs[2][...] += mm(d_exp, hidden, TN)
+            return 0
+
+        lax.fori_loop(0, rows // step, block, 0)
+    for k in range(E):
+        at = place(k)
+        for w in range(3):
+            gt_refs[k][w] = acc_refs[w][at].astype(BF16)
+
+
+def experts(own, x, g, tiles, his):
+    tile = tiles[0].shape[1:]
+    width = g[0].shape[1]
+    lo = len(x)
+    rows = x[0].shape[0]
+    full = (width, tile[1] * his)
+    return pl.pallas_call(
+        expert_kernel,
+        out_shape=[sds((rows, 2 * width), BF16)] * lo + [sds((3,) + tile, BF16)] * E,
+        in_specs=[pl.BlockSpec(memory_space=pltpu.SMEM)] + whole(2 * lo + E),
+        out_specs=whole(lo + E),
+        scratch_shapes=[pltpu.VMEM(full, BF16)] * 3 + [pltpu.VMEM(full, F32)] * 3,
+        compiler_params=params(60),
+        name="experts",
+    )(own, *x, *g, *tiles)
+
+
+def combine_kernel(
+    cot_ref,
+    resid_ref,
+    part_ref,
+    probs_ref,
+    cols_ref,
+    slots_ref,
+    routes_ref,
+    g2_ref,
+    wr_ref,
+    vc_ref,
+    *refs,
+):
+    od_refs = refs[:E]
+    out_ref, dres_ref, dl_ref, dw_ref, dv_ref, dg2_ref = refs[E:]
+    width = cot_ref.shape[1]
+    g = cot_ref[...].astype(F32)
+    lanes = lane_iota(TOK_DEV)
+    cols = cols_ref[...]
+
+    def col(i):
+        return pick(cols, lanes == i)
+
+    gate0, gate1, gate_id, inv2 = col(0), col(1), col(2), col(3)
+    resid = resid_ref[...]
+    unit2 = resid * inv2
+    normed = unit2 * g2_ref[...]
+    narrow = normed.astype(BF16)
+    od = jnp.concatenate([r[...] for r in od_refs], axis=0)
+    slot = lane_iota(TOK_DEV, ROWS)
+    hot0 = jnp.where(slot == slots_ref[:, 0:1], 1.0, 0.0).astype(BF16)
+    hot1 = jnp.where(slot == slots_ref[:, 1:2], 1.0, 0.0).astype(BF16)
+    y0 = mm(hot0, od[:, :width])
+    y1 = mm(hot1, od[:, :width])
+    out_ref[...] = (part_ref[...] + gate0 * y0 + gate1 * y1).astype(BF16)
+    a_n = jnp.sum(g * normed, axis=1, keepdims=True)
+    dg0 = jnp.sum(g * y0, axis=1, keepdims=True)
+    dg1 = jnp.sum(g * y1, axis=1, keepdims=True)
+    r0 = routes_ref[:, 0:1]
+    r1 = routes_ref[:, 1:2]
+    dg0 = jnp.where(r0 == E + 1, a_n, dg0)
+    dg1 = jnp.where(r1 == E + 1, a_n, dg1)
+    g_scale = gate_id
+    dl = jnp.zeros((TOK_DEV, 128), F32)
+    vmix = jnp.zeros((TOK_DEV, 128), F32)
+    for c in range(CONSTS):
+        gate_c, ma, mb = col(4 + 3 * c), col(5 + 3 * c), col(6 + 3 * c)
+        a_v = jnp.sum(g * vc_ref[c : c + 1, :], axis=1, keepdims=True)
+        branch = ma * a_n + mb * a_v
+        dg0 = jnp.where(r0 == E + 2 + c, branch, dg0)
+        dg1 = jnp.where(r1 == E + 2 + c, branch, dg1)
+        g_scale = g_scale + gate_c * ma
+        da = gate_c * a_n
+        db = gate_c * a_v
+        mean = ma * da + mb * db
+        dl = jnp.where(lanes == 16 + 2 * c, ma * (da - mean), dl)
+        dl = jnp.where(lanes == 17 + 2 * c, mb * (db - mean), dl)
+        vmix = jnp.where(lanes == c, gate_c * mb, vmix)
+    probs = probs_ref[...]
+    d_probs = jnp.where(lanes == r0, dg0, 0.0) + jnp.where(lanes == r1, dg1, 0.0)
+    d_logits = probs * (d_probs - jnp.sum(probs * d_probs, axis=1, keepdims=True))
+    dl = jnp.where(lanes < EXPERTS_ALL, d_logits, dl)
+    dl_ref[...] = dl
+    high = dl.astype(BF16)
+    low = (dl - high.astype(F32)).astype(BF16)
+    wr = wr_ref[...]
+    d_normed = g_scale * g + mm(hot0 + hot1, od[:, width:])
+    d_normed = d_normed + mm(high, wr, NT) + mm(low, wr, NT)
+    dw_ref[...] = mm(high, narrow, TN) + mm(low, narrow, TN)
+    vhigh = vmix.astype(BF16)
+    vlow = (vmix - vhigh.astype(F32)).astype(BF16)
+    dv_ref[...] = mm(vhigh, cot_ref[...], TN) + mm(vlow, cot_ref[...], TN)
+    dg2_ref[...] = jnp.broadcast_to(
+        jnp.sum(d_normed * unit2, axis=0, keepdims=True), dg2_ref.shape
+    )
+    n = d_normed * g2_ref[...]
+    dres_ref[...] = g + inv2 * (n - unit2 * jnp.mean(n * unit2, axis=1, keepdims=True))
+
+
+def combine(cot, resid, part, probs, cols, slots, routes, g2, wr, vc, od):
+    width = cot.shape[1]
+    return pl.pallas_call(
+        combine_kernel,
+        out_shape=[
+            sds((TOK_DEV, width), BF16),
+            sds((TOK_DEV, width), F32),
+            sds((TOK_DEV, 128), F32),
+            sds((128, width), F32),
+            sds((128, width), F32),
+            sds((8, width), F32),
+        ],
+        in_specs=whole(10 + E),
+        out_specs=whole(6),
+        compiler_params=params(56),
+        name="combine",
+    )(cot, resid, part, probs, cols, slots, routes, g2, wr, vc, *od)
+
+
+def backward_kernel(
+    dres_ref,
+    wq_ref,
+    wk_ref,
+    wv_ref,
+    wo_ref,
+    q_ref,
+    k_ref,
+    v_ref,
+    n1_ref,
+    inv1_ref,
+    mix_ref,
+    lse_ref,
+    cos_ref,
+    sin_ref,
+    pos_ref,
+    tok_ref,
+    halo_ref,
+    gw_ref,
+    down_ref,
+    dhalo_ref,
+    dg1_ref,
+    dm_ref,
+    dq_ref,
+    dk_ref,
+    dv_ref,
+    dqr_ref,
+    dkr_ref,
+    dvr_ref,
+):
+    scale = HEAD_DIM ** (-0.5)
+    width = dres_ref.shape[1]
+    d_attn = dres_ref[...].astype(BF16)
+    gw_ref[3] = mm(mix_ref[...], d_attn, TN).astype(BF16)
+    dm_ref[...] = mm(d_attn, wo_ref[...], NT).astype(BF16)
+    dk_ref[...] = jnp.zeros_like(dk_ref)
+    dv_ref[...] = jnp.zeros_like(dv_ref)
+
+    def pair(p, _):
+        span = pl.ds(pl.multiple_of(p * 128, 128), 128)
+        for first, count in QBLOCKS:
+            keys = key_span(first)
+            ok = allowed_mask(pos_ref, first, count)[:, :keys]
+            q = q_ref[pl.ds(first, count), span]
+            dm = dm_ref[pl.ds(first, count), span]
+            k = k_ref[pl.ds(first, keys), span]
+            v = v_ref[pl.ds(first, keys), span]
+            lane = lane_iota(count)
+            key_lane = lane_iota(keys)
+            lse = lse_ref[pl.ds(first, count), :]
+            dq = dk = dv = None
+            for h in range(2):
+                mine = (lane < HEAD_DIM) if h == 0 else (lane >= HEAD_DIM)
+                key_mine = (key_lane < HEAD_DIM) if h == 0 else (key_lane >= HEAD_DIM)
+                qh = jnp.where(mine, q, jnp.zeros_like(q))
+                dmh = jnp.where(mine, dm, jnp.zeros_like(dm))
+                s = jnp.where(ok, mm(qh, k, NT) * scale, NEG)
+                probs = jnp.where(ok, jnp.exp(s - pick(lse, lane == 2 * p + h)), 0.0)
+                dp = mm(dmh, v, NT)
+                delta = jnp.sum(probs * dp, axis=1, keepdims=True)
+                ds = (probs * (dp - delta)).astype(BF16)
+                pb = probs.astype(BF16)
+                dqh = mm(ds, k)
+                dkh = mm(ds, q, TN)
+                dvh = mm(pb, dm, TN)
+                dq = dqh if h == 0 else jnp.where(mine, dqh, dq)
+                dk = dkh if h == 0 else jnp.where(key_mine, dkh, dk)
+                dv = dvh if h == 0 else jnp.where(key_mine, dvh, dv)
+            dq_ref[pl.ds(first, count), span] = dq * scale
+            dk_ref[pl.ds(first, keys), span] += dk * scale
+            dv_ref[pl.ds(first, keys), span] += dv
+        return 0
+
+    lax.fori_loop(0, HEADS // 2, pair, 0)
+
+    def finish(i, _):
+        span = pl.ds(pl.multiple_of(i * 256, 256), 256)
+        cos = cos_ref[...]
+        sin = sin_ref[...]
+        dqr_ref[:, span] = turn(dq_ref[:, span], cos[HALO:], -sin[HALO:]).astype(BF16)
+        dkr_ref[:, span] = turn(dk_ref[:, span], cos, -sin).astype(BF16)
+        dvr_ref[:, span] = dv_ref[:, span].astype(BF16)
+        return 0
+
+    lax.fori_loop(0, width // 256, finish, 0)
+    gw_ref[0] = mm(n1_ref[HALO:, :], dqr_ref[...], TN).astype(BF16)
+    gw_ref[1] = mm(n1_ref[...], dkr_ref[...], TN).astype(BF16)
+    gw_ref[2] = mm(n1_ref[...], dvr_ref[...], TN).astype(BF16)
+    d_all = mm(dkr_ref[...], wk_ref[...], NT) + mm(dvr_ref[...], wv_ref[...], NT)
+    d_own = d_all[HALO:] + mm(dqr_ref[...], wq_ref[...], NT)
+    inv1 = inv1_ref[:, 0:1]
+    unit_own = tok_ref[...].astype(F32) * inv1[HALO:]
+    unit_halo = halo_ref[...].astype(F32) * inv1[:HALO]
+    d_halo = d_all[:HALO]
+    dg1 = jnp.sum(d_own * unit_own, axis=0, keepdims=True) + jnp.sum(
+        d_halo * unit_halo, axis=0, keepdims=True
+    )
+    dg1_ref[...] = jnp.broadcast_to(dg1, dg1_ref.shape)
+    down_ref[...] = d_own
+    dhalo_ref[...] = d_halo.astype(BF16)
+
+
+def backward(dres, wq, wk, wv, wo, q, k, v, n1, inv1, mix, lse, cos, sin, pos, tok, halo):
+    width = tok.shape[1]
+    return pl.pallas_call(
+        backward_kernel,
+        out_shape=[
+            sds((4, width, width), BF16),
+            sds((TOK_DEV, width), F32),
+            sds((HALO, width), BF16),
+            sds((8, width), F32),
+        ],
+        in_specs=whole(17),
+        out_specs=whole(4),
+        scratch_shapes=[
+            pltpu.VMEM((TOK_DEV, width), BF16),
+            pltpu.VMEM((TOK_DEV, width), F32),
+            pltpu.VMEM((KEYS, width), F32),
+            pltpu.VMEM((KEYS, width), F32),
+            pltpu.VMEM((TOK_DEV, width), BF16),
+            pltpu.VMEM((KEYS, width), BF16),
+            pltpu.VMEM((KEYS, width), BF16),
+        ],
+        compiler_params=params(60),
+        name="backward",
+    )(dres, wq, wk, wv, wo, q, k, v, n1, inv1, mix, lse, cos, sin, pos, tok, halo)
+
+
+def finish_kernel(dres_ref, down_ref, back_ref, tok_ref, inv1_ref, g1_ref, out_ref):
+    width = tok_ref.shape[1]
+    inv1 = inv1_ref[HALO:, 0:1]
+    unit = tok_ref[...].astype(F32) * inv1
+    back = jnp.concatenate(
+        [jnp.zeros((TOK_DEV - HALO, width), F32), back_ref[...].astype(F32)], axis=0
+    )
+    m = (down_ref[...] + back) * g1_ref[...]
+    d_dealt = inv1 * (m - unit * jnp.mean(m * unit, axis=1, keepdims=True))
+    out_ref[...] = dres_ref[...] + d_dealt.astype(BF16).astype(F32)
+
+
+def finish(dres, down, back, tok, inv1, g1):
+    return pl.pallas_call(
+        finish_kernel,
+        out_shape=sds(dres.shape, F32),
+        in_specs=whole(6),
+        out_specs=pl.BlockSpec(memory_space=pltpu.VMEM),
+        compiler_params=params(40),
+        name="finish",
+    )(dres, down, back, tok, inv1, g1)
+
+
+def store_kernel(own_ref, *refs):
+    t_refs = refs[:E]
+    gate_ref, up_ref, down_ref = refs[E:]
+    own = own_ref[0]
+    for k in range(E):
+        expert = lax.rem(own + k, E)
+        gate_ref[expert] = t_refs[k][0].astype(F32)
+        up_ref[expert] = t_refs[k][1].astype(F32)
+        down_ref[expert] = t_refs[k][2].astype(F32).T
+
+
+def store(own, tiles):
+    rows, cols = tiles[0].shape[1:]
+    return pl.pallas_call(
+        store_kernel,
+        out_shape=[sds((E, rows, cols), F32)] * 2 + [sds((E, cols, rows), F32)],
+        in_specs=[pl.BlockSpec(memory_space=pltpu.SMEM)] + whole(E),
+        out_specs=whole(3),
+        compiler_params=params(40),
+        name="store",
+    )(own, *tiles)
+
+
+def fast_device(
+    tokens,
+    cotangent,
+    prev_logits,
+    lengths,
+    dealing,
+    routes,
+    gain_one,
+    w_query,
+    w_key,
+    w_value,
+    w_out,
+    gain_two,
+    w_router,
+    w_mix,
+    w_const,
+    v_const,
+    w_gate,
+    w_up,
+    w_down,
+):
+    groups = lax.axis_size("grp")
+    ranks = lax.axis_size("fsdp")
+    his = E // ranks
+    lo = groups // his
+    g_id = lax.axis_index("grp")
+    f_id = lax.axis_index("fsdp")
+    width = tokens.shape[1]
+    axes = ("grp", "fsdp")
+    own = (f_id * his + g_id // lo).astype(jnp.int32).reshape(1)
+
+    def member_perm(k):
+        pairs = []
+        for g in range(groups):
+            for f in range(ranks):
+                m = (f * his + g // lo + k) % E
+                pairs.append((g * ranks + f, (m % his * lo + g % lo) * ranks + m // his))
+        return pairs
+
+    def to_member(x, k):
+        return x if k == 0 else lax.ppermute(x, axes, member_perm(k))
+
+    def near_perm(j):
+        return [(g, g ^ j) for g in range(groups)]
+
+    def near(x, j):
+        return x if j == 0 else lax.ppermute(x, "grp", near_perm(j))
+
+    prep = prepare(own, routes, cotangent, w_gate, w_up, w_down)
+    slots, g_rows, w_tiles = prep[0], prep[1 : 1 + E], prep[1 + E :]
+    halo = lax.ppermute(
+        tokens[TOK_DEV - HALO :], "fsdp", [(f, f + 1) for f in range(ranks - 1)]
+    )
+    packed = jnp.stack([w_query, w_key, w_value, w_out])
+    packed = lax.all_gather(packed, axes, axis=0, tiled=False)
+    packed = packed.reshape((groups, ranks) + packed.shape[1:])
+    full = packed.transpose(2, 1, 3, 0, 4).reshape(4, width, width)
+    wq, wk, wv, wo = full[0], full[1], full[2], full[3]
+    per = gain_one.shape[0]
+    small = jnp.concatenate(
+        [gain_one[:, None], gain_two[:, None], v_const, w_router, w_const], axis=1
+    )
+    small = lax.all_gather(small, axes, axis=0, tiled=True)
+    g1 = small[:, 0][None, :].astype(F32)
+    g2 = small[:, 1][None, :].astype(F32)
+    vc = small[:, 2 : 2 + CONSTS].T.astype(F32)
+    wr = jnp.zeros((width, 128), BF16)
+    wr = wr.at[:, :EXPERTS_ALL].set(small[:, 2 + CONSTS : 2 + CONSTS + EXPERTS_ALL])
+    wr = wr.at[:, 16 : 16 + 2 * CONSTS].set(small[:, 2 + CONSTS + EXPERTS_ALL :])
+    tiles = [to_member(w_tiles[k], k) for k in range(E)]
+    g_in = [to_member(g_rows[k], k) for k in range(E)]
+    g_mine = jnp.concatenate(g_in, axis=0)
+    g_all = [near(g_mine, j) for j in range(lo)]
+
+    seq_len = lengths[0]
+    count = seq_len.shape[0]
+    ids = jnp.arange(count, dtype=jnp.int32)
+    ends = jnp.sum(jnp.where(ids[:, None] >= ids[None, :], seq_len[None, :], 0), axis=1)
+    row = f_id * TOK_DEV + jnp.arange(-HALO, TOK_DEV, dtype=jnp.int32)
+    begin = jnp.max(jnp.where(ends[None, :] <= row[:, None], ends[None, :], 0), axis=1)
+    pos = jnp.maximum(row - begin, 0)
+    cos, sin = rotation_tables(pos, HEAD_DIM)
+    cos = jnp.concatenate([cos] * 4, axis=1)
+    sin = jnp.concatenate([-sin, sin, -sin, sin], axis=1)
+    pos_own = jnp.broadcast_to(pos[HALO:, None], (TOK_DEV, 128))
+    mixed_prev = exact_dot(prev_logits, w_mix.astype(F32))
+    mixed_prev = jnp.pad(mixed_prev, ((0, 0), (0, 128 - EXPERTS_ALL)))
+
+    fwd = forward(
+        tokens, halo, g1, g2, cos, sin, pos_own, wq, wk, wv, wo, wr, vc, mixed_prev, routes, slots
+    )
+    q, k, v, n1, inv1, mix, lse, resid, part, probs, cols = fwd[:11]
+    x_in = [to_member(fwd[11 + i], i) for i in range(E)]
+    x_mine = jnp.concatenate(x_in, axis=0)
+    x_all = [near(x_mine, j) for j in range(lo)]
+    done = experts(own, x_all, g_all, tiles, his)
+    od, g_tiles = done[:lo], done[lo:]
+
+    def add(a, b):
+        return (a.astype(F32) + b.astype(F32)).astype(BF16)
+
+    half = near(jnp.concatenate([od[1], od[3]], axis=0), 1)
+    here = add(od[0], half[:ROWS])
+    there = add(od[2], half[ROWS:])
+    od_sum = add(here, near(there, 2))
+
+    def back_perm(i):
+        return [(b, a) for a, b in member_perm(i)]
+
+    od_back = []
+    for i in range(E):
+        rows = od_sum[i * MOST : (i + 1) * MOST]
+        od_back.append(rows if i == 0 else lax.ppermute(rows, axes, back_perm(i)))
+    output, d_resid, dl, dw, dv, dg2 = combine(
+        cotangent, resid, part, probs, cols, slots, routes, g2, wr, vc, od_back
+    )
+    d_logits = dl[:, :EXPERTS_ALL]
+    grad_prev = exact_dot(d_logits, w_mix.astype(F32).T)
+    d_mix = exact_dot(prev_logits.T, d_logits)
+    gw, down, d_halo, dg1 = backward(
+        d_resid, wq, wk, wv, wo, q, k, v, n1, inv1, mix, lse, cos, sin, pos_own, tokens, halo
+    )
+    back = lax.ppermute(d_halo, "fsdp", [(f + 1, f) for f in range(ranks - 1)])
+    grad_tokens = finish(d_resid, down, back, tokens, inv1, g1)
+    tiles_back = [
+        g_tiles[i] if i == 0 else lax.ppermute(g_tiles[i], axes, back_perm(i)) for i in range(E)
+    ]
+    grad_gate, grad_up, grad_down = store(own, tiles_back)
+
+    cols_per = width // groups
+    rows_per = width // ranks
+    gw = gw.reshape(4, width, groups, cols_per).transpose(2, 0, 1, 3)
+    gw = lax.psum_scatter(gw, "grp", scatter_dimension=0, tiled=False)
+    gw = gw.reshape(4, ranks, rows_per, cols_per).transpose(1, 0, 2, 3)
+    gw = lax.psum_scatter(gw, "fsdp", scatter_dimension=0, tiled=False).astype(F32)
+    tiny = jnp.concatenate(
+        [
+            dg1[:1],
+            dg2[:1],
+            dv[:CONSTS],
+            dw[:EXPERTS_ALL],
+            dw[16 : 16 + 2 * CONSTS],
+            jnp.pad(d_mix.reshape(1, -1), ((0, 0), (0, width - EXPERTS_ALL * EXPERTS_ALL))),
+        ],
+        axis=0,
+    )
+    tiny = lax.psum(tiny, axes)
+    grad_mix = tiny[-1, : EXPERTS_ALL * EXPERTS_ALL].reshape(EXPERTS_ALL, EXPERTS_ALL)
+    at = (g_id * ranks + f_id) * per
+    mine = lax.dynamic_slice(tiny, (0, at), (tiny.shape[0], per))
+    n_small = 2 + CONSTS
+    return (
+        output,
+        grad_tokens,
+        grad_prev,
+        mine[0],
+        gw[0],
+        gw[1],
+        gw[2],
+        gw[3],
+        mine[1],
+        mine[n_small : n_small + EXPERTS_ALL].T,
+        grad_mix,
+        mine[n_small + EXPERTS_ALL : n_small + EXPERTS_ALL + 2 * CONSTS].T,
+        mine[2:n_small].T,
+        grad_gate,
+        grad_up,
+        grad_down,
+    )
+
+
+def suits(mesh):
+    ranks, groups = mesh.shape["fsdp"], mesh.shape["grp"]
+    return E % ranks == 0 and groups % (E // ranks) == 0 and groups // (E // ranks) == 4
+
+
 def solution(mesh):
     return jax.shard_map(
-        per_device,
+        fast_device if suits(mesh) else per_device,
         mesh=mesh,
         in_specs=(
             P(("grp", "fsdp"), None),

time: 2890 us -> 715 us (0.25)
  waiting for transfers between devices: 2100 us -> 303 us
  matrix products: 272 us -> 1.51 us
  local copies, waits for them, and re-layouts: 184 us -> 66 us
  other arithmetic: 128 us -> 12.4 us
  Pallas kernels: 0 us -> 102 us
  starting transfers between devices: 2.71 us -> 94.1 us
  blocking collectives: 173 us -> 115 us
    reduce_scatter x12 -> x1, waiting for transfers between devices: 1400 us -> 0.01 us  [fast_device(): lax.psum_scatter(gw, 'fsdp', scatter_dimension=0, tiled=False).astype(F32)]
    all_gather x14 -> x1, waiting for transfers between devices: 529 us -> 0.02 us  [fast_device(): packed = lax.all_gather(packed, axes, axis=0, tiled=False)]
    dot_general x128 -> x0, matrix products: 261 us -> none  [the longest x8 28.5 us: per_device(): up_part = jnp.dot(picked, wup[expert], preferred_element_type=jnp.float32)]
    ppermute x0 -> x45, waiting for transfers between devices: none -> 208 us  [the longest x8 132 us: near(): return x if j == 0 else lax.ppermute(x, 'grp', near_perm(j))]
    pallas_call x0 -> x7, Pallas kernels: none -> 102 us  [the longest x1 35.8 us: experts(): pl.pallas_call(expert_kernel, out_shape=[sds((rows, 2 * width), BF16)] *...]
    ppermute x0 -> x45, starting transfers between devices: none -> 94 us  [the longest x21 64.4 us: to_member(): return x if k == 0 else lax.ppermute(x, axes, member_perm(k))]
    unnamed x40 -> x4, waiting for transfers between devices: 171 us -> 94.2 us
    unnamed x4 -> x0, blocking collectives: 55.2 us -> none
  transfers between devices with their start and end apart: 33 -> 48, of which waited for: 23 -> 17; matrix products, arithmetic and copies ran while one was open for 16% -> 8% of each run, Pallas kernels for 0% -> 4%
where the time goes in v1:
time: 715 us; the launch traced here: 709 us
  waiting for transfers between devices  303 us (42%)
  blocking collectives  115 us (16%)
  Pallas kernels  102 us (14%)
  starting transfers between devices  94.1 us (13%)
  local copies, waits for them, and re-layouts  66 us (9%)
  between operations  15.1 us (2%)
  other arithmetic  12.4 us (2%)
    ppermute x8, waiting for transfers between devices, near(): return x if j == 0 else lax.ppermute(x, 'grp', near_perm(j))  132 us
    unnamed x4, waiting for transfers between devices  94.2 us
    all_gather x1, blocking collectives, fast_device(): small = lax.all_gather(small, axes, axis=0, tiled=True)  74.1 us
    ppermute x21, starting transfers between devices, to_member(): return x if k == 0 else lax.ppermute(x, axes, member_perm(k))  64.4 us
    psum x1, blocking collectives, fast_device(): tiny = lax.psum(tiny, axes)  41.3 us
    ppermute x21, waiting for transfers between devices, to_member(): return x if k == 0 else lax.ppermute(x, axes, member_perm(k))  37.4 us
    ppermute x7, waiting for transfers between devices, fast_device(): od_back.append(rows if i == 0 else lax.ppermute(rows, axes, back_perm(i)))  37 us
    pallas_call x1, Pallas kernels, experts(): pl.pallas_call(expert_kernel, out_shape=[sds((rows, 2 * width), BF16)] *...  35.8 us
  transfers between devices with their start and end apart: 48, of which 17 were waited for; matrix products, arithmetic and copies ran while one was open for 8% of the time, Pallas kernels for 4%

profile of v1, /device:TPU:0, one launch (start us, length us, event | category | flops | bytes accessed | tf_op | source)
XLA Modules:
  0.0 709.3 jit_solution(13988820470238499340)
XLA Ops:
  30.6 74.1 %all_gather.9 = bf16[768,20]{1,0:T(8,128)(2,1)S(1)} all-gather(bf16[24,20]{1,0:T(8,128)(2,1)S(1)} %concatenate.25), channel_id=1, replica_groups=mesh['grp'=8,'fsdp'=4] {'grp','fsdp'}, dimensions={0}, use_global_device_ids=true | all-gather | bytes 31680 | tf_op jit(solution)/shard_map/all_gather | solution.py:1285
  124.7 8.4 %copy.130 = bf16[8,4,4,192,96]{4,0,3,1,2:T(8,128)(2,1)S(1)} copy(bf16[8,4,4,192,96]{4,3,2,1,0:T(8,128)(2,1)} %bitcast.64) | data formatting | bytes 9437184 | tf_op jit(solution)/shard_map/reshape | solution.py:1278
  148.4 22.9 %forward.1 = (bf16[320,768]{1,0:T(8,128)(2,1)}, bf16[576,768]{1,0:T(8,128)(2,1)}, bf16[576,768]{1,0:T(8,128)(2,1)}, bf16[576,768]{1,0:T(8,128)(2,1)}, f32[576,12...) custom-call(bf16[320,768]{1,0:T(8,128)(2,1)} %tok_ref.5, ...), custom_call_target="tpu_custom_call" | custom-call | tf_op jit(solution)/shard_map/forward/pallas_call | solution.py:849
  171.3 5.6 collective-permute-start.1
  188.2 12.1 %collective-permute-done.3 = bf16[80,896]{1,0:T(8,128)(2,1)S(1)} collective-permute-done((bf16[80,896]{1,0:T(8,128)(2,1)}, bf16[80,896]{1,0:T(8,128)(2,1)S(1)}, u32[]{:S(2)}, u32[]{:S(2)}) %collective-permute-start.3) | collective-permute-done | bytes 143392 | tf_op jit(solution)/shard_map/ppermute | solution.py:1263
  200.3 7.6 %collective-permute-start.6 = (bf16[80,896]{1,0:T(8,128)(2,1)}, bf16[80,896]{1,0:T(8,128)(2,1)S(1)}, u32[]{:S(2)}, u32[]{:S(2)}) collective-permute-start(bf16[80,896]{1,0:T(8,128)(2,1)} %get-tuple-element.112), channel_id=1, source_target_pairs={{0,3},{1,0},{2,1},{3,2},{4,7},{5,4},{6,5},{7,6},{8,11},{9,8},{10,9... | collective-permute-start | bytes 430088 | tf_op jit(solution)/shard_map/ppermute | solution.py:1263
  207.8 21.6 %collective-permute-start.7 = (bf16[80,896]{1,0:T(8,128)(2,1)}, bf16[80,896]{1,0:T(8,128)(2,1)S(1)}, u32[]{:S(2)}, u32[]{:S(2)}) collective-permute-start(bf16[80,896]{1,0:T(8,128)(2,1)} %get-tuple-element.113), channel_id=1, source_target_pairs={{0,19},{1,16},{2,17},{3,18},{4,23},{5,20},{6,21},{7,22},{8,27},{9,... | collective-permute-start | bytes 430088 | tf_op jit(solution)/shard_map/ppermute | solution.py:1263
  234.0 5.1 collective-permute-start.27
  239.1 6.2 collective-permute-done.24.refs_12_
  247.8 6.3 collective-permute-done.26.refs_14_
  259.4 59.2 %collective-permute-done.19.refs_6_ = bf16[640,768]{1,0:T(8,128)(2,1)S(1)} collective-permute-done((bf16[640,768]{1,0:T(8,128)(2,1)S(1)}, bf16[640,768]{1,0:T(8,128)(2,1)S(1)}, u32[]{:S(2)}, u32[]{:S(2)}) %collective-permute-start.19) | collective-permute-done | bytes 983072 | tf_op jit(solution)/shard_map/ppermute | solution.py:1269
  318.6 21.0 %collective-permute-done.20.refs_7_ = bf16[640,768]{1,0:T(8,128)(2,1)S(1)} collective-permute-done((bf16[640,768]{1,0:T(8,128)(2,1)S(1)}, bf16[640,768]{1,0:T(8,128)(2,1)S(1)}, u32[]{:S(2)}, u32[]{:S(2)}) %collective-permute-start.20) | collective-permute-done | bytes 983072 | tf_op jit(solution)/shard_map/ppermute | solution.py:1269
  342.0 35.8 %experts.1 = (bf16[640,1536]{1,0:T(8,128)(2,1)}, bf16[640,1536]{1,0:T(8,128)(2,1)}, bf16[640,1536]{1,0:T(8,128)(2,1)}, bf16[640,1536]{1,0:T(8,128)(2,1)}, bf16[3...) custom-call(s32[1]{0:T(128)} %bitcast.10.own_ref, ...), custom_call_target="tpu_custom_call" | custom-call | tf_op jit(solution)/shard_map/experts/pallas_call | solution.py:940
  380.6 6.7 collective-permute-done.28
  387.9 44.8 %collective-permute-done.29 = bf16[640,1536]{1,0:T(8,128)(2,1)S(1)} collective-permute-done((bf16[640,1536]{1,0:T(8,128)(2,1)S(1)}, bf16[640,1536]{1,0:T(8,128)(2,1)S(1)}, u32[]{:S(2)}, u32[]{:S(2)}) %collective-permute-start.29) | collective-permute-done | bytes 1966112 | tf_op jit(solution)/shard_map/ppermute | solution.py:1269
  434.4 6.3 collective-permute-start.31
  445.7 10.1 %collective-permute-done.31.refs_2_ = bf16[80,1536]{1,0:T(8,128)(2,1)S(1)} collective-permute-done((bf16[80,1536]{1,0:T(8,128)(2,1)S(1)}, bf16[80,1536]{1,0:T(8,128)(2,1)S(1)}, u32[]{:S(2)}, u32[]{:S(2)}) %collective-permute-start.31) | collective-permute-done | bytes 245792 | tf_op jit(solution)/shard_map/ppermute | solution.py:1335
  455.8 20.5 %collective-permute-done.33.refs_4_ = bf16[80,1536]{1,0:T(8,128)(2,1)S(1)} collective-permute-done((bf16[80,1536]{1,0:T(8,128)(2,1)S(1)}, bf16[80,1536]{1,0:T(8,128)(2,1)S(1)}, u32[]{:S(2)}, u32[]{:S(2)}) %collective-permute-start.33) | collective-permute-done | bytes 245792 | tf_op jit(solution)/shard_map/ppermute | solution.py:1335
  476.3 6.3 collective-permute-done.34.refs_5_
  483.5 6.5 combine.1
  490.0 28.6 %backward.1 = (bf16[4,768,768]{2,1,0:T(8,128)(2,1)}, f32[320,768]{1,0:T(8,128)}, bf16[256,768]{1,0:T(8,128)(2,1)}, f32[8,768]{1,0:T(8,128)}) custom-call(f32[320,768]{1,0:T(8,128)} %get-tuple-element.135.dres_ref, bf16[768,768]{1,0:T(8,128)(2,1)} %squeeze.30.wq_ref, bf16[768,768]{1,0:T(8,128)(2,1)} %squeeze.31.wk_ref, bf16[768,768]{1,0:T(8,128)(2,1)} %squeeze.32.wv_ref, ...), custom_call_target="tpu_custom_call" | custom-call | tf_op jit(solution)/shard_map/backward/pallas_call | solution.py:1153
  518.7 6.7 copy.121
  541.1 94.2 %all-reduce.6.cloned.1.call-done = bf16[8,4,768,96]{2,3,0,1:T(8,128)(2,1)} async-done(((bf16[8,4,768,96]{2,3,0,1:T(8,128)(2,1)}), bf16[8,4,768,96]{2,3,0,1:T(8,128)(2,1)}) %all-reduce.6.cloned.1.call-update) | async-done | bytes 4718608
  653.8 41.3 %psum.7 = f32[21,768]{1,0:T(8,128)S(1)} all-reduce(f32[21,768]{1,0:T(8,128)S(1)} %concatenate.31), channel_id=1, replica_groups=mesh['grp'=8,'fsdp'=4] {'grp','fsdp'}, use_global_device_ids=true, to_apply=%region_4.5 | all-reduce | flops 16128 | bytes 129024 | tf_op jit(solution)/shard_map/psum | solution.py:1369
  (271 shorter events, 136.2 us)
Async XLA Ops:
  7.2 117.5 %all-gather.3.cloned.1.call-start = ((), (), s32[]{:S(2)}) async-start(), calls=%async_computation.2 | async-start | bytes 6488064 | tf_op jit(solution)/shard_map/all_gather | solution.py:1277
  8.9 626.4 %all-reduce.6.cloned.1.call-start = ((), (), s32[]{:S(2)}) async-start(), calls=%async_computation.3 | async-start | bytes 9437184
  17.7 97.9 %collective-permute-start.11 = (bf16[80,768]{1,0:T(8,128)(2,1)}, bf16[80,768]{1,0:T(8,128)(2,1)S(1)}, u32[]{:S(2)}, u32[]{:S(2)}) collective-permute-start(bf16[80,768]{1,0:T(8,128)(2,1)} %get-tuple-element.115), channel_id=1, source_target_pairs={{0,16},{1,17},{2,18},{3,19},{4,20},{5,21},{6,22},{7,23},{8,24},{9,... | collective-permute-start | bytes 368648 | tf_op jit(solution)/shard_map/ppermute | solution.py:1263
  20.7 95.0 %collective-permute-start.12 = (bf16[80,768]{1,0:T(8,128)(2,1)}, bf16[80,768]{1,0:T(8,128)(2,1)S(1)}, u32[]{:S(2)}, u32[]{:S(2)}) collective-permute-start(bf16[80,768]{1,0:T(8,128)(2,1)} %get-tuple-element.116), channel_id=1, source_target_pairs={{0,1},{1,2},{2,3},{3,0},{4,5},{5,6},{6,7},{7,4},{8,9},{9,10},{10,1... | collective-permute-start | bytes 368648 | tf_op jit(solution)/shard_map/ppermute | solution.py:1263
  22.3 96.0 %collective-permute-start.13 = (bf16[80,768]{1,0:T(8,128)(2,1)}, bf16[80,768]{1,0:T(8,128)(2,1)S(1)}, u32[]{:S(2)}, u32[]{:S(2)}) collective-permute-start(bf16[80,768]{1,0:T(8,128)(2,1)} %get-tuple-element.117), channel_id=1, source_target_pairs={{0,17},{1,18},{2,19},{3,16},{4,21},{5,22},{6,23},{7,20},{8,25},{9,... | collective-permute-start | bytes 368648 | tf_op jit(solution)/shard_map/ppermute | solution.py:1263
  24.8 98.1 %collective-permute-start.14 = (bf16[80,768]{1,0:T(8,128)(2,1)}, bf16[80,768]{1,0:T(8,128)(2,1)S(1)}, u32[]{:S(2)}, u32[]{:S(2)}) collective-permute-start(bf16[80,768]{1,0:T(8,128)(2,1)} %get-tuple-element.118), channel_id=1, source_target_pairs={{0,2},{1,3},{2,0},{3,1},{4,6},{5,7},{6,4},{7,5},{8,10},{9,11},{10,... | collective-permute-start | bytes 368648 | tf_op jit(solution)/shard_map/ppermute | solution.py:1263
  26.0 97.5 %collective-permute-start.15 = (bf16[80,768]{1,0:T(8,128)(2,1)}, bf16[80,768]{1,0:T(8,128)(2,1)S(1)}, u32[]{:S(2)}, u32[]{:S(2)}) collective-permute-start(bf16[80,768]{1,0:T(8,128)(2,1)} %get-tuple-element.119), channel_id=1, source_target_pairs={{0,18},{1,19},{2,16},{3,17},{4,22},{5,23},{6,20},{7,21},{8,26},{9,... | collective-permute-start | bytes 368648 | tf_op jit(solution)/shard_map/ppermute | solution.py:1263
  115.7 61.2 %collective-permute-start.17 = (bf16[80,768]{1,0:T(8,128)(2,1)}, bf16[80,768]{1,0:T(8,128)(2,1)S(1)}, u32[]{:S(2)}, u32[]{:S(2)}) collective-permute-start(bf16[80,768]{1,0:T(8,128)(2,1)} %get-tuple-element.121), channel_id=1, source_target_pairs={{0,19},{1,16},{2,17},{3,18},{4,23},{5,20},{6,21},{7,22},{8,27},{9,... | collective-permute-start | bytes 368648 | tf_op jit(solution)/shard_map/ppermute | solution.py:1263
  122.9 56.9 %collective-permute-start.21 = (bf16[3,192,256]{2,1,0:T(8,128)(2,1)}, bf16[3,192,256]{2,1,0:T(8,128)(2,1)}, u32[]{:S(2)}, u32[]{:S(2)}) collective-permute-start(bf16[3,192,256]{2,1,0:T(8,128)(2,1)} %get-tuple-element.123), channel_id=1, source_target_pairs={{0,16},{1,17},{2,18},{3,19},{4,20},{5,21},{6,22},{7,23},{8,24},{9,... | collective-permute-start | bytes 884744 | tf_op jit(solution)/shard_map/ppermute | solution.py:1263
  123.5 63.6 %collective-permute-start.22 = (bf16[3,192,256]{2,1,0:T(8,128)(2,1)}, bf16[3,192,256]{2,1,0:T(8,128)(2,1)}, u32[]{:S(2)}, u32[]{:S(2)}) collective-permute-start(bf16[3,192,256]{2,1,0:T(8,128)(2,1)} %get-tuple-element.124), channel_id=1, source_target_pairs={{0,1},{1,2},{2,3},{3,0},{4,5},{5,6},{6,7},{7,4},{8,9},{9,10},{10,1... | collective-permute-start | bytes 884744 | tf_op jit(solution)/shard_map/ppermute | solution.py:1263
  176.9 82.3 %collective-permute-start.18 = (bf16[640,768]{1,0:T(8,128)(2,1)S(1)}, bf16[640,768]{1,0:T(8,128)(2,1)S(1)}, u32[]{:S(2)}, u32[]{:S(2)}) collective-permute-start(bf16[640,768]{1,0:T(8,128)(2,1)S(1)} %constant_dynamic-update-slice_fusion.8.refs_4_), channel_id=1, source_target_pairs={{0,4},{4,0},{8,12},{12,8},{16,20},{20,16},{24,28},{28,24},{1,5},{5... | collective-permute-start | bytes 2949128 | tf_op jit(solution)/shard_map/ppermute | solution.py:1269
  179.9 49.6 %collective-permute-start.23 = (bf16[3,192,256]{2,1,0:T(8,128)(2,1)S(1)}, bf16[3,192,256]{2,1,0:T(8,128)(2,1)S(1)}, u32[]{:S(2)}, u32[]{:S(2)}) collective-permute-start(bf16[3,192,256]{2,1,0:T(8,128)(2,1)S(1)} %copy-done.46), channel_id=1, source_target_pairs={{0,17},{1,18},{2,19},{3,16},{4,21},{5,22},{6,23},{7,20},{8,25},{9,... | collective-permute-start | bytes 884744 | tf_op jit(solution)/shard_map/ppermute | solution.py:1263
  245.3 94.3 %collective-permute-start.10 = (bf16[640,896]{1,0:T(8,128)(2,1)S(1)}, bf16[640,896]{1,0:T(8,128)(2,1)S(1)}, u32[]{:S(2)}, u32[]{:S(2)}) collective-permute-start(bf16[640,896]{1,0:T(8,128)(2,1)S(1)} %constant_dynamic-update-slice_fusion.refs_0_), channel_id=1, source_target_pairs={{0,12},{4,8},{8,4},{12,0},{16,28},{20,24},{24,20},{28,16},{1,13},{... | collective-permute-start | bytes 3440648 | tf_op jit(solution)/shard_map/ppermute | solution.py:1269
  247.8 91.8 %collective-permute-start.8 = (bf16[640,896]{1,0:T(8,128)(2,1)S(1)}, bf16[640,896]{1,0:T(8,128)(2,1)S(1)}, u32[]{:S(2)}, u32[]{:S(2)}) collective-permute-start(bf16[640,896]{1,0:T(8,128)(2,1)S(1)} %constant_dynamic-update-slice_fusion.refs_0_), channel_id=1, source_target_pairs={{0,4},{4,0},{8,12},{12,8},{16,20},{20,16},{24,28},{28,24},{1,5},{5... | collective-permute-start | bytes 3440648 | tf_op jit(solution)/shard_map/ppermute | solution.py:1269
  254.1 85.5 %collective-permute-start.9 = (bf16[640,896]{1,0:T(8,128)(2,1)S(1)}, bf16[640,896]{1,0:T(8,128)(2,1)S(1)}, u32[]{:S(2)}, u32[]{:S(2)}) collective-permute-start(bf16[640,896]{1,0:T(8,128)(2,1)S(1)} %constant_dynamic-update-slice_fusion.refs_0_), channel_id=1, source_target_pairs={{0,8},{4,12},{8,0},{12,4},{16,24},{20,28},{24,16},{28,20},{1,9},{5... | collective-permute-start | bytes 3440648 | tf_op jit(solution)/shard_map/ppermute | solution.py:1269
  259.2 59.4 %collective-permute-start.19 = (bf16[640,768]{1,0:T(8,128)(2,1)S(1)}, bf16[640,768]{1,0:T(8,128)(2,1)S(1)}, u32[]{:S(2)}, u32[]{:S(2)}) collective-permute-start(bf16[640,768]{1,0:T(8,128)(2,1)S(1)} %constant_dynamic-update-slice_fusion.8.refs_4_), channel_id=1, source_target_pairs={{0,8},{4,12},{8,0},{12,4},{16,24},{20,28},{24,16},{28,20},{1,9},{5... | collective-permute-start | bytes 2949128 | tf_op jit(solution)/shard_map/ppermute | solution.py:1269
  259.2 80.4 %collective-permute-start.20 = (bf16[640,768]{1,0:T(8,128)(2,1)S(1)}, bf16[640,768]{1,0:T(8,128)(2,1)S(1)}, u32[]{:S(2)}, u32[]{:S(2)}) collective-permute-start(bf16[640,768]{1,0:T(8,128)(2,1)S(1)} %constant_dynamic-update-slice_fusion.8.refs_4_), channel_id=1, source_target_pairs={{0,12},{4,8},{8,4},{12,0},{16,28},{20,24},{24,20},{28,16},{1,13},{... | collective-permute-start | bytes 2949128 | tf_op jit(solution)/shard_map/ppermute | solution.py:1269
  525.4 175.2 %reduce-scatter.5.cloned.1.call-start = ((), (), s32[]{:S(2)}) async-start(), calls=%async_computation.1 | async-start | bytes 983040 | tf_op jit(solution)/shard_map/reduce_scatter | solution.py:1357
  527.3 114.2 %collective-permute-start.40 = (bf16[3,192,256]{2,1,0:T(8,128)(2,1)}, bf16[3,192,256]{2,1,0:T(8,128)(2,1)S(1)}, u32[]{:S(2)}, u32[]{:S(2)}) collective-permute-start(bf16[3,192,256]{2,1,0:T(8,128)(2,1)} %get-tuple-element.154), channel_id=1, source_target_pairs={{17,0},{18,1},{19,2},{16,3},{21,4},{22,5},{23,6},{20,7},{25,8},{26... | collective-permute-start | bytes 884744 | tf_op jit(solution)/shard_map/ppermute | solution.py:1348
  532.1 109.5 %collective-permute-start.41 = (bf16[3,192,256]{2,1,0:T(8,128)(2,1)}, bf16[3,192,256]{2,1,0:T(8,128)(2,1)S(1)}, u32[]{:S(2)}, u32[]{:S(2)}) collective-permute-start(bf16[3,192,256]{2,1,0:T(8,128)(2,1)} %get-tuple-element.155), channel_id=1, source_target_pairs={{2,0},{3,1},{0,2},{1,3},{6,4},{7,5},{4,6},{5,7},{10,8},{11,9},{8,1... | collective-permute-start | bytes 884744 | tf_op jit(solution)/shard_map/ppermute | solution.py:1348
  532.1 109.5 %collective-permute-start.42 = (bf16[3,192,256]{2,1,0:T(8,128)(2,1)}, bf16[3,192,256]{2,1,0:T(8,128)(2,1)S(1)}, u32[]{:S(2)}, u32[]{:S(2)}) collective-permute-start(bf16[3,192,256]{2,1,0:T(8,128)(2,1)} %get-tuple-element.156), channel_id=1, source_target_pairs={{18,0},{19,1},{16,2},{17,3},{22,4},{23,5},{20,6},{21,7},{26,8},{27... | collective-permute-start | bytes 884744 | tf_op jit(solution)/shard_map/ppermute | solution.py:1348
  534.1 107.5 %collective-permute-start.43 = (bf16[3,192,256]{2,1,0:T(8,128)(2,1)}, bf16[3,192,256]{2,1,0:T(8,128)(2,1)S(1)}, u32[]{:S(2)}, u32[]{:S(2)}) collective-permute-start(bf16[3,192,256]{2,1,0:T(8,128)(2,1)} %get-tuple-element.157), channel_id=1, source_target_pairs={{3,0},{0,1},{1,2},{2,3},{7,4},{4,5},{5,6},{6,7},{11,8},{8,9},{9,10... | collective-permute-start | bytes 884744 | tf_op jit(solution)/shard_map/ppermute | solution.py:1348
  540.2 101.4 %collective-permute-start.44 = (bf16[3,192,256]{2,1,0:T(8,128)(2,1)S(1)}, bf16[3,192,256]{2,1,0:T(8,128)(2,1)S(1)}, u32[]{:S(2)}, u32[]{:S(2)}) collective-permute-start(bf16[3,192,256]{2,1,0:T(8,128)(2,1)S(1)} %copy-done.47), channel_id=1, source_target_pairs={{19,0},{16,1},{17,2},{18,3},{23,4},{20,5},{21,6},{22,7},{27,8},{24... | collective-permute-start | bytes 884744 | tf_op jit(solution)/shard_map/ppermute | solution.py:1348
  652.3 46.9 %collective-permute-start.37 = (bf16[256,768]{1,0:T(8,128)(2,1)}, bf16[256,768]{1,0:T(8,128)(2,1)S(1)}, u32[]{:S(2)}, u32[]{:S(2)}) collective-permute-start(bf16[256,768]{1,0:T(8,128)(2,1)} %get-tuple-element.144), channel_id=1, source_target_pairs={{1,0},{2,1},{3,2},{5,4},{6,5},{7,6},{9,8},{10,9},{11,10},{13,12},{... | collective-permute-start | bytes 1179656 | tf_op jit(solution)/shard_map/ppermute | solution.py:1345
  (76 other events, 2614.9 us)
Sparse Core Ops, SparseCore 0:
  11.5 80.8 all-gather.2
  525.5 109.6 all-reduce.5
  641.6 27.9 reduce-scatter.4

commit v2 on v1

--- a/solution.py
+++ b/solution.py
@@ -636,51 +636,71 @@
     return jax.ShapeDtypeStruct(shape, dtype)
 
 
-def prepare_kernel(own_ref, routes_ref, cot_ref, wg_ref, wu_ref, wd_ref, slots_ref, *outs):
-    own = own_ref[0]
-    g_refs, w_refs = outs[:E], outs[E:]
-    lanes = lane_iota(TOK_DEV)
-    r0 = routes_ref[:, 0:1]
-    r1 = routes_ref[:, 1:2]
-    hot0 = lanes == r0
-    hot1 = lanes == r1
-    member = jnp.where(hot0 | hot1, 1.0, 0.0).astype(BF16)
-    earlier = (
-        lax.broadcasted_iota(jnp.int32, (TOK_DEV, TOK_DEV), 1)
-        < lax.broadcasted_iota(jnp.int32, (TOK_DEV, TOK_DEV), 0)
-    )
-    rank = mm(jnp.where(earlier, 1.0, 0.0).astype(BF16), member)
-    c0 = jnp.where(
-        r0 < E, lax.rem(r0 - own + E, E) * MOST + pick(rank, hot0).astype(jnp.int32), -1
-    )
-    c1 = jnp.where(
-        r1 < E, lax.rem(r1 - own + E, E) * MOST + pick(rank, hot1).astype(jnp.int32), -1
-    )
-    slots_ref[...] = jnp.where(lanes == 0, c0, jnp.where(lanes == 1, c1, -1))
-    cols = lane_iota(TOK_DEV, ROWS)
-    spread = jnp.where((cols == c0) | (cols == c1), 1.0, 0.0).astype(BF16)
-    rows = mm(spread, cot_ref[...], TN).astype(BF16)
-    for k in range(E):
-        g_refs[k][...] = rows[k * MOST : (k + 1) * MOST]
-        expert = lax.rem(own + k, E)
-        w_refs[k][0] = wg_ref[expert]
-        w_refs[k][1] = wu_ref[expert]
-        w_refs[k][2] = wd_ref[expert].T
-
-
-def prepare(own, routes, cotangent, w_gate, w_up, w_down):
-    tile = w_gate.shape[1:]
-    width = cotangent.shape[1]
-    return pl.pallas_call(
-        prepare_kernel,
-        out_shape=[sds((TOK_DEV, 128), jnp.int32)]
-        + [sds((MOST, width), BF16)] * E
-        + [sds((3,) + tile, BF16)] * E,
-        in_specs=[pl.BlockSpec(memory_space=pltpu.SMEM)] + whole(5),
-        out_specs=whole(1 + 2 * E),
-        compiler_params=params(56),
-        name="prepare",
-    )(own, routes, cotangent, w_gate, w_up, w_down)
+MESH_ID = pl.DeviceIdType.MESH
+
+
+def send(src, dst, send_sem, recv_sem, device):
+    pltpu.make_async_remote_copy(
+        src_ref=src,
+        dst_ref=dst,
+        send_sem=send_sem,
+        recv_sem=recv_sem,
+        device_id=device,
+        device_id_type=MESH_ID,
+    ).start()
+
+
+def settle(ref, sem):
+    pltpu.make_async_copy(ref, ref, sem).wait()
+
+
+def flip(a, b):
+    return a + b - 2 * a * b
+
+
+def xor4(a, b):
+    return flip(a // 2, b // 2) * 2 + flip(lax.rem(a, 2), lax.rem(b, 2))
+
+
+def aligned(value, to):
+    return pl.multiple_of(value, to)
+
+
+class Place:
+    def __init__(self, his, lo):
+        self.g = lax.axis_index("grp")
+        self.f = lax.axis_index("fsdp")
+        self.his, self.lo = his, lo
+        self.hi = self.g // lo
+        self.l = lax.rem(self.g, lo)
+        self.m = self.f * his + self.hi
+        core = lax.rem(self.g, 2)
+        side = lax.rem(self.g // 2, 2)
+        self.core_peer = self.g + 1 - 2 * core
+        self.side_peer = self.g + 2 - 4 * side
+        self.l1 = lax.rem(self.core_peer, lo)
+        self.l2 = lax.rem(self.side_peer, lo)
+        self.l3 = lo - 1 - self.l
+
+    def member(self, j, hh):
+        f = xor4(self.f, j)
+        hi = flip(self.hi, hh)
+        return f * self.his + hi, (hi * self.lo + self.l, f)
+
+    def others(self):
+        peers = []
+        for j in range(4):
+            for hh in range(self.his):
+                if j or hh:
+                    peers.append(self.member(j, hh)[1])
+        return peers
+
+
+def greet(peers):
+    barrier = pltpu.get_barrier_semaphore()
+    for peer in peers:
+        pl.semaphore_signal(barrier, inc=1, device_id=peer, device_id_type=MESH_ID)
+    pl.semaphore_wait(barrier, len(peers))
 
 
 def turn(values, cos, sin):
@@ -709,22 +729,21 @@
     return min(384, KEYS - first)
 
 
-def forward_kernel(
+def begin_kernel(
+    tile_ref,
     tok_ref,
-    halo_ref,
-    g1_ref,
-    g2_ref,
+    cot_ref,
+    routes_ref,
     cos_ref,
     sin_ref,
     pos_ref,
-    wq_ref,
-    wk_ref,
-    wv_ref,
-    wo_ref,
-    wr_ref,
-    vc_ref,
     mixed_prev_ref,
-    routes_ref,
+    wd_ref,
+    wg_hbm,
+    wu_hbm,
+    wf_ref,
+    s_ref,
+    halo_ref,
     slots_ref,
     q_ref,
     k_ref,
@@ -737,27 +756,195 @@
     part_ref,
     probs_ref,
     cols_ref,
-    *x_refs,
+    x_ref,
+    gates_ref,
+    w_hbm,
+    g_hbm,
+    p_ref,
+    wdt_ref,
+    grow_ref,
+    zs,
+    ps,
+    cs,
+    hs,
+    gs,
+    ws,
+    gas,
+    agr,
+    hr,
+    gr,
+    wr,
+    gqr,
 ):
+    lo, ranks = g_hbm.shape[:2]
+    his = E // ranks
+    at = Place(his, lo)
+    width = tok_ref.shape[1]
+    head_rows = wd_ref.shape[2]
+    ff = wd_ref.shape[1]
+    part_cols = width // p_ref.shape[0]
+    diag = lo * (1 - at.hi) + at.l2
+    upper = lo * (1 - at.hi) + at.l
+    near = [(at.core_peer, at.f), (at.side_peer, at.f), (upper, at.f), (diag, at.f)]
+    greet(at.others() + [near[0], near[1], near[3]])
+
+    p_ref[at.g, at.f] = tile_ref[...]
+    for j in range(1, ranks):
+        f2 = xor4(at.f, j)
+        send(tile_ref, p_ref.at[at.g, at.f], zs.at[j], agr.at[at.g, at.f], (at.g, f2))
+
+    def spread(j, f2, src):
+        for t, peer in enumerate(near):
+            send(src, p_ref.at[at.g, f2], ps.at[j, t], agr.at[at.g, f2], peer)
+
+    spread(0, at.f, tile_ref)
+    halo_rows = halo_ref.shape[0]
+    tail = tok_ref.at[pl.ds(tok_ref.shape[0] - halo_rows, halo_rows)]
+
+    @pl.when(at.f < ranks - 1)
+    def _():
+        send(tail, halo_ref, hs, hr, (at.g, at.f + 1))
+
+    @pl.when(at.f == 0)
+    def _():
+        halo_ref[...] = jnp.zeros_like(halo_ref)
+
+    lanes = lane_iota(TOK_DEV)
+    r0 = routes_ref[:, 0:1]
+    r1 = routes_ref[:, 1:2]
+    hot0 = lanes == r0
+    hot1 = lanes == r1
+    named = jnp.where(hot0 | hot1, 1.0, 0.0).astype(BF16)
+    earlier = (
+        lax.broadcasted_iota(jnp.int32, (TOK_DEV, TOK_DEV), 1)
+        < lax.broadcasted_iota(jnp.int32, (TOK_DEV, TOK_DEV), 0)
+    )
+    rank = mm(jnp.where(earlier, 1.0, 0.0).astype(BF16), named)
+    rank0 = pick(rank, hot0).astype(jnp.int32)
+    rank1 = pick(rank, hot1).astype(jnp.int32)
+    c0 = jnp.where(r0 < E, r0 * MOST + rank0, -1)
+    c1 = jnp.where(r1 < E, r1 * MOST + rank1, -1)
+    slots_ref[...] = jnp.where(lanes == 0, c0, jnp.where(lanes == 1, c1, -1))
+    slot = lane_iota(TOK_DEV, ROWS)
+    spots0 = jnp.where(slot == c0, 1.0, 0.0).astype(BF16)
+    spots1 = jnp.where(slot == c1, 1.0, 0.0).astype(BF16)
+    grow_ref[...] = mm(spots0 + spots1, cot_ref[...], TN).astype(BF16)
+    for e in range(E):
+        wdt_ref[e] = wd_ref[e].T
+
+    for j in range(1, ranks):
+        f2 = xor4(at.f, j)
+        settle(p_ref.at[at.g, f2], agr.at[at.g, f2])
+        spread(j, f2, p_ref.at[at.g, f2])
+
+    own_rows = pl.ds(aligned(at.f * head_rows, 16), head_rows)
+    own_cols = pl.ds(aligned(at.hi * ff, 128), ff)
+    own_spot = pl.ds(aligned(at.hi * MOST, 16), MOST)
+    for j in range(ranks):
+        for hh in range(his):
+            e, peer = at.member(j, hh)
+            rows = grow_ref.at[pl.ds(aligned(e * MOST, 16), MOST)]
+            spot = g_hbm.at[at.l, at.f, own_spot]
+            sources = (wg_hbm.at[e], wu_hbm.at[e], wdt_ref.at[e])
+            if j == 0 and hh == 0:
+                pltpu.make_async_copy(rows, spot, gr.at[at.m]).start()
+                for w in range(3):
+                    pltpu.make_async_copy(
+                        sources[w], w_hbm.at[w, own_rows, own_cols], wr.at[at.m, w]
+                    ).start()
+            else:
+                k = j * his + hh
+                send(rows, spot, gs.at[k], gr.at[at.m], peer)
+                for w in range(3):
+                    send(
+                        sources[w],
+                        w_hbm.at[w, own_rows, own_cols],
+                        ws.at[k, w],
+                        wr.at[at.m, w],
+                        peer,
+                    )
+
+    for j in range(ranks):
+        f2 = xor4(at.f, j)
+        for t in range(1, 4):
+            g2 = near[t][0]
+            settle(p_ref.at[g2, f2], agr.at[g2, f2])
+            send(p_ref.at[g2, f2], p_ref.at[g2, f2], cs.at[t - 1, j], agr.at[g2, f2], near[0])
+    sibling_upper = lo * (1 - at.hi) + at.l1
+    for j in range(ranks):
+        f2 = xor4(at.f, j)
+        for g2 in (
+            at.core_peer,
+            at.hi * lo + at.l3,
+            sibling_upper,
+            lo * (1 - at.hi) + at.l3,
+        ):
+            settle(p_ref.at[g2, f2], agr.at[g2, f2])
+
+    per = (p_ref.shape[2] - head_rows) // 8 * 24
+    groups = p_ref.shape[0]
+    for g2 in range(groups):
+        for f2 in range(ranks):
+            piece = p_ref[g2, f2, head_rows : head_rows + 8, :].astype(F32)
+            for i in range(per // 8):
+                base = (g2 * ranks + f2) * per + 8 * i
+                s_ref[base : base + 8, :] = piece[:, 128 * i : 128 * i + 128]
+
+    def lay(f2, _):
+        rows = pl.ds(aligned(f2 * head_rows, 16), head_rows)
+        for w in range(4):
+            for half in range(2):
+                pieces = [
+                    p_ref[
+                        half * (groups // 2) + i,
+                        f2,
+                        0:head_rows,
+                        w * part_cols : (w + 1) * part_cols,
+                    ]
+                    for i in range(groups // 2)
+                ]
+                wf_ref[w, rows, half * (width // 2) : (half + 1) * (width // 2)] = (
+                    jnp.concatenate(pieces, axis=1)
+                )
+        return 0
+
+    lax.fori_loop(0, ranks, lay, 0)
+
+    @pl.when(at.f > 0)
+    def _():
+        settle(halo_ref, hr)
+
     scale = HEAD_DIM ** (-0.5)
+    flat = s_ref[...].T
+    g1 = flat[SMALL_G1 : SMALL_G1 + 1, :]
+    g2 = flat[SMALL_G1 + 1 : SMALL_G1 + 2, :]
+    vc = flat[SMALL_VC : SMALL_VC + CONSTS, :]
     rows = jnp.concatenate([halo_ref[...], tok_ref[...]], axis=0).astype(F32)
     inv1 = lax.rsqrt(jnp.mean(rows * rows, axis=1, keepdims=True) + NORM_EPS)
     inv1_ref[...] = jnp.broadcast_to(inv1, (KEYS, 128))
-    n1_ref[...] = (rows * inv1 * g1_ref[...]).astype(BF16)
+    n1_ref[...] = (rows * inv1 * g1).astype(BF16)
 
     def project(i, _):
         span = pl.ds(pl.multiple_of(i * 256, 256), 256)
         cos = cos_ref[...]
         sin = sin_ref[...]
-        q = mm(n1_ref[HALO:, :], wq_ref[:, span])
+        q = mm(n1_ref[HALO:, :], wf_ref[0, :, span])
         q_ref[:, span] = turn(q, cos[HALO:], sin[HALO:]).astype(BF16)
-        k = mm(n1_ref[...], wk_ref[:, span])
+        k = mm(n1_ref[...], wf_ref[1, :, span])
         k_ref[:, span] = turn(k, cos, sin).astype(BF16)
-        v_ref[:, span] = mm(n1_ref[...], wv_ref[:, span]).astype(BF16)
+        v_ref[:, span] = mm(n1_ref[...], wf_ref[2, :, span]).astype(BF16)
         return 0
 
-    lax.fori_loop(0, q_ref.shape[1] // 256, project, 0)
+    lax.fori_loop(0, width // 256, project, 0)
     lse_ref[...] = jnp.zeros((TOK_DEV, 128), F32)
+
+    for f2 in range(ranks):
+        for h2 in range(his):
+            settle(
+                g_hbm.at[at.l, f2, h2 * MOST : (h2 + 1) * MOST], gr.at[f2 * his + h2]
+            )
+    send(g_hbm.at[at.l], g_hbm.at[at.l], gas.at[0], gqr.at[0], near[0])
+    send(g_hbm.at[at.l], g_hbm.at[at.l], gas.at[1], gqr.at[1], near[1])
 
     def pair(p, _):
         span = pl.ds(pl.multiple_of(p * 128, 128), 128)
@@ -773,11 +960,11 @@
             for h in range(2):
                 mine = (lane < HEAD_DIM) if h == 0 else (lane >= HEAD_DIM)
                 qh = jnp.where(mine, q, jnp.zeros_like(q))
-                s = jnp.where(ok, mm(qh, k, NT) * scale, NEG)
-                top = jnp.max(s, axis=1, keepdims=True)
-                e = jnp.exp(s - top)
-                total = jnp.sum(e, axis=1, keepdims=True)
-                o = mm((e / total).astype(BF16), v)
+                sc = jnp.where(ok, mm(qh, k, NT) * scale, NEG)
+                top = jnp.max(sc, axis=1, keepdims=True)
+                ex = jnp.exp(sc - top)
+                total = jnp.sum(ex, axis=1, keepdims=True)
+                o = mm((ex / total).astype(BF16), v)
                 out = o if h == 0 else jnp.where(mine, o, out)
                 lse = jnp.where(lane == 2 * p + h, top + jnp.log(total), lse)
             mix_ref[pl.ds(first, count), span] = out.astype(BF16)
@@ -785,23 +972,23 @@
         return 0
 
     lax.fori_loop(0, HEADS // 2, pair, 0)
-    attn_out = mm(mix_ref[...], wo_ref[...]).astype(BF16)
+    settle(g_hbm.at[at.l2], gqr.at[1])
+    send(g_hbm.at[at.l2], g_hbm.at[at.l2], gas.at[2], gqr.at[2], near[0])
+
+    attn_out = mm(mix_ref[...], wf_ref[3]).astype(BF16)
     resid = tok_ref[...].astype(F32) + attn_out.astype(F32)
     resid_ref[...] = resid
     inv2 = lax.rsqrt(jnp.mean(resid * resid, axis=1, keepdims=True) + NORM_EPS)
-    normed = resid * inv2 * g2_ref[...]
+    normed = resid * inv2 * g2
     narrow = normed.astype(BF16)
-    lanes = lane_iota(TOK_DEV)
-    raw = mm(narrow, wr_ref[...])
+    raw = mm(narrow, s_ref[...].astype(BF16))
     logits = jnp.where(lanes < EXPERTS_ALL, raw + mixed_prev_ref[...], NEG)
     top = jnp.max(logits, axis=1, keepdims=True)
-    e = jnp.exp(logits - top)
-    probs = e / jnp.sum(e, axis=1, keepdims=True)
+    ex = jnp.exp(logits - top)
+    probs = ex / jnp.sum(ex, axis=1, keepdims=True)
     probs_ref[...] = probs
-    r0 = routes_ref[:, 0:1]
-    r1 = routes_ref[:, 1:2]
-    gate0 = pick(probs, lanes == r0)
-    gate1 = pick(probs, lanes == r1)
+    gate0 = pick(probs, hot0)
+    gate1 = pick(probs, hot1)
 
     def gate_of(expert):
         return jnp.where(r0 == expert, gate0, 0.0) + jnp.where(r1 == expert, gate1, 0.0)
@@ -813,42 +1000,81 @@
     cols = jnp.where(lanes == 2, gate_id, cols)
     cols = jnp.where(lanes == 3, inv2, cols)
     for c in range(CONSTS):
-        la = pick(raw, lanes == 16 + 2 * c)
-        lb = pick(raw, lanes == 17 + 2 * c)
+        la = pick(raw, lanes == SMALL_C + 2 * c)
+        lb = pick(raw, lanes == SMALL_C + 1 + 2 * c)
         big = jnp.maximum(la, lb)
         ea = jnp.exp(la - big)
         eb = jnp.exp(lb - big)
         ma = ea / (ea + eb)
         mb = eb / (ea + eb)
         gate_c = gate_of(E + 2 + c)
-        part = part + gate_c * (ma * normed + mb * vc_ref[c : c + 1, :])
+        part = part + gate_c * (ma * normed + mb * vc[c : c + 1, :])
         cols = jnp.where(lanes == 4 + 3 * c, gate_c, cols)
         cols = jnp.where(lanes == 5 + 3 * c, ma, cols)
         cols = jnp.where(lanes == 6 + 3 * c, mb, cols)
     part_ref[...] = part
     cols_ref[...] = cols
-    c0 = slots_ref[:, 0:1]
-    c1 = slots_ref[:, 1:2]
-    slot = lane_iota(TOK_DEV, ROWS)
-    hot0 = jnp.where(slot == c0, 1.0, 0.0).astype(BF16)
-    hot1 = jnp.where(slot == c1, 1.0, 0.0).astype(BF16)
-
-    def two_parts(gate):
-        high = gate.astype(BF16).astype(F32)
-        return jnp.where(lanes == 0, high, jnp.where(lanes == 1, gate - high, 0.0)).astype(BF16)
-
-    x = mm(hot0 + hot1, narrow, TN).astype(BF16)
-    gates = (mm(hot0, two_parts(gate0), TN) + mm(hot1, two_parts(gate1), TN)).astype(BF16)
-    for k in range(E):
-        x_refs[k][:, : x.shape[1]] = x[k * MOST : (k + 1) * MOST]
-        x_refs[k][:, x.shape[1] :] = gates[k * MOST : (k + 1) * MOST]
-
-
-def forward(tok, halo, g1, g2, cos, sin, pos, wq, wk, wv, wo, wr, vc, mixed_prev, routes, slots):
+    x_ref[...] = mm(spots0 + spots1, narrow, TN).astype(BF16)
+    wide0 = jnp.where(r0 < E, r0 * 128 + rank0, -1)
+    wide1 = jnp.where(r1 < E, r1 * 128 + rank1, -1)
+    for e in range(E):
+        lane = lanes + e * 128
+        row = jnp.sum(
+            jnp.where(lane == wide0, gate0, 0.0) + jnp.where(lane == wide1, gate1, 0.0),
+            axis=0,
+            keepdims=True,
+        )
+        gates_ref[e] = jnp.broadcast_to(row, (8, 128))
+
+    settle(g_hbm.at[at.l1], gqr.at[0])
+    settle(g_hbm.at[at.l3], gqr.at[2])
+    for f2 in range(ranks):
+        for h2 in range(his):
+            for w in range(3):
+                block = w_hbm.at[
+                    w, f2 * head_rows : (f2 + 1) * head_rows, h2 * ff : (h2 + 1) * ff
+                ]
+                settle(block, wr.at[f2 * his + h2, w])
+    for j in range(1, ranks):
+        settle(tile_ref, zs.at[j])
+    for j in range(ranks):
+        for t in range(4):
+            settle(tile_ref, ps.at[j, t])
+        for t in range(3):
+            settle(tile_ref, cs.at[t, j])
+
+    @pl.when(at.f < ranks - 1)
+    def _():
+        settle(tail, hs)
+
+    for k in range(1, E):
+        settle(grow_ref.at[0:MOST], gs.at[k])
+        for w in range(3):
+            settle(wdt_ref.at[0], ws.at[k, w])
+    for i in range(3):
+        settle(g_hbm.at[at.l], gas.at[i])
+
+
+SMALL_G1 = EXPERTS_ALL
+SMALL_VC = SMALL_G1 + 2
+SMALL_C = SMALL_VC + CONSTS
+
+
+def begin(tile, tok, cot, routes, cos, sin, pos, mixed_prev, w_down, w_gate, w_up, groups, ranks):
     width = tok.shape[1]
+    lo = groups * ranks // E
+    his = E // ranks
+    ff = w_down.shape[1]
+    head_rows = w_down.shape[2]
+    dma = pltpu.SemaphoreType.DMA
+    any_spec = pl.BlockSpec(memory_space=pl.ANY)
     return pl.pallas_call(
-        forward_kernel,
+        begin_kernel,
         out_shape=[
+            sds((4, width, width), BF16),
+            sds((width, 128), F32),
+            sds((HALO, width), BF16),
+            sds((TOK_DEV, 128), jnp.int32),
             sds((TOK_DEV, width), BF16),
             sds((KEYS, width), BF16),
             sds((KEYS, width), BF16),
@@ -860,92 +1086,275 @@
             sds((TOK_DEV, width), F32),
             sds((TOK_DEV, 128), F32),
             sds((TOK_DEV, 128), F32),
-        ]
-        + [sds((MOST, WIDE), BF16)] * E,
-        in_specs=whole(16),
-        out_specs=whole(11 + E),
-        compiler_params=params(56),
-        name="forward",
-    )(tok, halo, g1, g2, cos, sin, pos, wq, wk, wv, wo, wr, vc, mixed_prev, routes, slots)
-
-
-def expert_kernel(own_ref, *refs):
-    lo = 4
-    x_refs = refs[:lo]
-    g_refs = refs[lo : 2 * lo]
-    t_refs = refs[2 * lo : 2 * lo + E]
-    od_refs = refs[2 * lo + E : 3 * lo + E]
-    gt_refs = refs[3 * lo + E : 3 * lo + 2 * E]
-    w_refs = refs[3 * lo + 2 * E : 3 * lo + 2 * E + 3]
-    acc_refs = refs[3 * lo + 2 * E + 3 :]
-    own = own_ref[0]
-    tile = t_refs[0].shape[1:]
-    width = w_refs[0].shape[0]
-    his = w_refs[0].shape[1] // tile[1]
-
-    def place(k):
-        source = lax.rem(own - k + E, E)
-        row = pl.multiple_of(source // his * tile[0], tile[0])
-        col = pl.multiple_of(lax.rem(source, his) * tile[1], tile[1])
-        return pl.ds(row, tile[0]), pl.ds(col, tile[1])
-
+            sds((ROWS, width), BF16),
+            sds((E, 8, 128), F32),
+            sds((3, width, ff * his), BF16),
+            sds((lo, ranks, his * MOST, width), BF16),
+        ],
+        in_specs=whole(9) + [any_spec, any_spec],
+        out_specs=whole(17) + [any_spec, any_spec],
+        scratch_shapes=[
+            pltpu.VMEM((groups, ranks) + tile.shape, BF16),
+            pltpu.VMEM((E, head_rows, ff), BF16),
+            pltpu.VMEM((ROWS, width), BF16),
+            dma((4,)),
+            dma((4, 4)),
+            dma((3, 4)),
+            dma,
+            dma((E,)),
+            dma((E, 3)),
+            dma((3,)),
+            dma((groups, ranks)),
+            dma,
+            dma((E,)),
+            dma((E, 3)),
+            dma((3,)),
+        ],
+        compiler_params=params(60, collective_id=1, has_side_effects=True),
+        name="begin",
+    )(tile, tok, cot, routes, cos, sin, pos, mixed_prev, w_down, w_gate, w_up)
+
+
+def moe_kernel(
+    x_ref,
+    gates_ref,
+    w_ref,
+    g_ref,
+    back_ref,
+    *rest,
+):
+    gt_refs = rest[:E]
+    (
+        xb_ref,
+        gb_ref,
+        od_ref,
+        r1_ref,
+        r2_ref,
+        acc_ref,
+        xs,
+        gs,
+        qs,
+        gqs,
+        d1s,
+        d2s,
+        bs,
+        xr,
+        gr,
+        qr,
+        gqr,
+        d1r,
+        d2r,
+        br,
+    ) = rest[E:]
+    lo, ranks = g_ref.shape[:2]
+    his = E // ranks
+    width = x_ref.shape[1]
+    at = Place(his, lo)
+    core = (at.core_peer, at.f)
+    side = (at.side_peer, at.f)
+    greet(at.others() + [core, side])
+    own_spot = pl.ds(aligned(at.hi * MOST, 16), MOST)
+
+    for j in range(ranks):
+        for hh in range(his):
+            e, peer = at.member(j, hh)
+            k = j * his + hh
+            rows = x_ref.at[pl.ds(aligned(e * MOST, 16), MOST)]
+            spot = xb_ref.at[at.f, at.l, own_spot]
+            if k == 0:
+                pltpu.make_async_copy(rows, spot, xr.at[at.m]).start()
+                pltpu.make_async_copy(
+                    gates_ref.at[e], gb_ref.at[at.f, at.l, at.hi], gr.at[at.m]
+                ).start()
+            else:
+                send(rows, spot, xs.at[k], xr.at[at.m], peer)
+                send(
+                    gates_ref.at[e], gb_ref.at[at.f, at.l, at.hi], gs.at[k], gr.at[at.m], peer
+                )
+    acc_ref[...] = jnp.zeros_like(acc_ref)
+
+    def take(j):
+        fj = xor4(at.f, j)
+        for hh in range(his):
+            hi = flip(at.hi, hh)
+            m = fj * his + hi
+            settle(xb_ref.at[fj, at.l, pl.ds(aligned(hi * MOST, 16), MOST)], xr.at[m])
+            settle(gb_ref.at[fj, at.l, hi], gr.at[m])
+        for i, peer in enumerate((core, side)):
+            send(xb_ref.at[fj, at.l], xb_ref.at[fj, at.l], qs.at[fj, i], qr.at[fj, i], peer)
+            send(gb_ref.at[fj, at.l], gb_ref.at[fj, at.l], gqs.at[fj, i], gqr.at[fj, i], peer)
+
+    def pass_on(j):
+        fj = xor4(at.f, j)
+        settle(xb_ref.at[fj, at.l2], qr.at[fj, 1])
+        settle(gb_ref.at[fj, at.l2], gqr.at[fj, 1])
+        send(xb_ref.at[fj, at.l2], xb_ref.at[fj, at.l2], qs.at[fj, 2], qr.at[fj, 2], core)
+        send(gb_ref.at[fj, at.l2], gb_ref.at[fj, at.l2], gqs.at[fj, 2], gqr.at[fj, 2], core)
+
+    def compute(j):
+        fj = xor4(at.f, j)
+        settle(xb_ref.at[fj, at.l1], qr.at[fj, 0])
+        settle(gb_ref.at[fj, at.l1], gqr.at[fj, 0])
+        settle(xb_ref.at[fj, at.l3], qr.at[fj, 2])
+        settle(gb_ref.at[fj, at.l3], gqr.at[fj, 2])
+        rows = lo * his * MOST
+        x = jnp.concatenate([xb_ref[fj, i] for i in range(lo)], axis=0)
+        g = jnp.concatenate([g_ref[i, fj] for i in range(lo)], axis=0)
+        diagonal = lax.broadcasted_iota(jnp.int32, (MOST, 128), 0) == lane_iota(MOST)
+        gate = jnp.concatenate(
+            [
+                pick(jnp.broadcast_to(gb_ref[fj, i, h][0:1, :], (MOST, 128)), diagonal)
+                for i in range(lo)
+                for h in range(his)
+            ],
+            axis=0,
+        )
+        d_exp = (g.astype(F32) * gate).astype(BF16)
+        wg = w_ref[0]
+        wu = w_ref[1]
+        wd = w_ref[2]
+        a = mm(x, wg)
+        b = mm(x, wu)
+        sig = 1.0 / (1.0 + jnp.exp(-a))
+        hidden = (a * sig * b).astype(BF16)
+        shape = (lo, his * MOST, width)
+        od_ref[fj, :, :, :width] = mm(hidden, wd, NT).astype(BF16).reshape(shape)
+        dh = mm(d_exp, wd)
+        d_up = (dh * a * sig).astype(BF16)
+        d_gate = (dh * b * sig * (1.0 + a * (1.0 - sig))).astype(BF16)
+        od_ref[fj, :, :, width:] = (
+            (mm(d_gate, wg, NT) + mm(d_up, wu, NT)).astype(BF16).reshape(shape)
+        )
+        acc_ref[0] += mm(x, d_gate, TN)
+        acc_ref[1] += mm(x, d_up, TN)
+        acc_ref[2] += mm(d_exp, hidden, TN)
+
+    def to_core(j):
+        fj = xor4(at.f, j)
+        send(od_ref.at[fj, at.l1], r1_ref.at[fj, 0], d1s.at[fj, 0], d1r.at[fj, 0], core)
+        send(od_ref.at[fj, at.l3], r1_ref.at[fj, 1], d1s.at[fj, 1], d1r.at[fj, 1], core)
+
+    def add(ref, other):
+        ref[...] = (ref[...].astype(F32) + other[...].astype(F32)).astype(BF16)
+
+    def to_side(j):
+        fj = xor4(at.f, j)
+        settle(r1_ref.at[fj, 1], d1r.at[fj, 1])
+        add(od_ref.at[fj, at.l2], r1_ref.at[fj, 1])
+        send(od_ref.at[fj, at.l2], r2_ref.at[fj], d2s.at[fj], d2r.at[fj], side)
+        settle(r1_ref.at[fj, 0], d1r.at[fj, 0])
+        add(od_ref.at[fj, at.l], r1_ref.at[fj, 0])
+
+    def to_home(j):
+        fj = xor4(at.f, j)
+        settle(r2_ref.at[fj], d2r.at[fj])
+        add(od_ref.at[fj, at.l], r2_ref.at[fj])
+        for hh in range(his):
+            hi = flip(at.hi, hh)
+            m = fj * his + hi
+            rows = od_ref.at[fj, at.l, pl.ds(aligned(hi * MOST, 16), MOST)]
+            peer = (hi * lo + at.l, fj)
+
+            def away(rows=rows, peer=peer, m=m):
+                send(rows, back_ref.at[at.m], bs.at[m], br.at[at.m], peer)
+
+            if hh:
+                away()
+            else:
+
+                @pl.when(j == 0)
+                def _(rows=rows):
+                    pltpu.make_async_copy(rows, back_ref.at[at.m], br.at[at.m]).start()
+
+                pl.when(j > 0)(away)
+
+    take(0)
+    take(1)
+
+    def step(t, _):
+        @pl.when(t < ranks)
+        def _():
+            pass_on(t)
+            compute(t)
+            to_core(t)
+
+        @pl.when(t + 2 < ranks)
+        def _():
+            take(t + 2)
+
+        @pl.when((t >= 1) & (t <= ranks))
+        def _():
+            to_side(t - 1)
+
+        @pl.when(t >= 2)
+        def _():
+            to_home(t - 2)
+
+        return 0
+
+    lax.fori_loop(0, ranks + 2, step, 0)
+
+    tile = gt_refs[0].shape[1:]
     for k in range(E):
-        at = place(k)
+        source = lax.rem(at.m - k + E, E)
+        rows = pl.ds(aligned(source // his * tile[0], 16), tile[0])
+        cols = pl.ds(aligned(lax.rem(source, his) * tile[1], 128), tile[1])
         for w in range(3):
-            w_refs[w][at] = t_refs[k][w]
-    for w in range(3):
-        acc_refs[w][...] = jnp.zeros_like(acc_refs[w])
-    rows = x_refs[0].shape[0]
-    step = rows // 2
-    for j in range(lo):
-
-        def block(i, _, j=j):
-            at = pl.ds(pl.multiple_of(i * step, step), step)
-            x = x_refs[j][at, :width]
-            gate = (
-                x_refs[j][at, width : width + 1].astype(F32)
-                + x_refs[j][at, width + 1 : width + 2].astype(F32)
-            )
-            d_exp = (g_refs[j][at, :].astype(F32) * gate).astype(BF16)
-            wg = w_refs[0][...]
-            wu = w_refs[1][...]
-            wd = w_refs[2][...]
-            a = mm(x, wg)
-            b = mm(x, wu)
-            sig = 1.0 / (1.0 + jnp.exp(-a))
-            hidden = (a * sig * b).astype(BF16)
-            od_refs[j][at, :width] = mm(hidden, wd, NT).astype(BF16)
-            dh = mm(d_exp, wd)
-            d_up = (dh * a * sig).astype(BF16)
-            d_gate = (dh * b * sig * (1.0 + a * (1.0 - sig))).astype(BF16)
-            od_refs[j][at, width:] = (mm(d_gate, wg, NT) + mm(d_up, wu, NT)).astype(BF16)
-            acc_refs[0][...] += mm(x, d_gate, TN)
-            acc_refs[1][...] += mm(x, d_up, TN)
-            acc_refs[2][...] += mm(d_exp, hidden, TN)
-            return 0
-
-        lax.fori_loop(0, rows // step, block, 0)
-    for k in range(E):
-        at = place(k)
-        for w in range(3):
-            gt_refs[k][w] = acc_refs[w][at].astype(BF16)
-
-
-def experts(own, x, g, tiles, his):
-    tile = tiles[0].shape[1:]
-    width = g[0].shape[1]
-    lo = len(x)
-    rows = x[0].shape[0]
-    full = (width, tile[1] * his)
+            gt_refs[k][w] = acc_ref[w, rows, cols].astype(BF16)
+
+    for m in range(E):
+        settle(back_ref.at[m], br.at[m])
+    for k in range(1, E):
+        settle(x_ref.at[0:MOST], xs.at[k])
+        settle(gates_ref.at[0], gs.at[k])
+    for f2 in range(ranks):
+        for i in range(3):
+            settle(xb_ref.at[0, 0], qs.at[f2, i])
+            settle(gb_ref.at[0, 0], gqs.at[f2, i])
+        for i in range(2):
+            settle(r1_ref.at[0, 0], d1s.at[f2, i])
+        settle(r2_ref.at[0], d2s.at[f2])
+    for j in range(ranks):
+        for hh in range(his):
+            if j or hh:
+                m = at.member(j, hh)[0]
+                settle(back_ref.at[0], bs.at[m])
+
+
+def moe(x, gates, w, g, tile):
+    lo, ranks, block, width = g.shape
+    dma = pltpu.SemaphoreType.DMA
+    his = E // ranks
     return pl.pallas_call(
-        expert_kernel,
-        out_shape=[sds((rows, 2 * width), BF16)] * lo + [sds((3,) + tile, BF16)] * E,
-        in_specs=[pl.BlockSpec(memory_space=pltpu.SMEM)] + whole(2 * lo + E),
-        out_specs=whole(lo + E),
-        scratch_shapes=[pltpu.VMEM(full, BF16)] * 3 + [pltpu.VMEM(full, F32)] * 3,
-        compiler_params=params(60),
-        name="experts",
-    )(own, *x, *g, *tiles)
+        moe_kernel,
+        out_shape=[sds((E, MOST, 2 * width), BF16)] + [sds((3,) + tile, BF16)] * E,
+        in_specs=whole(4),
+        out_specs=whole(1 + E),
+        scratch_shapes=[
+            pltpu.VMEM((ranks, lo, block, width), BF16),
+            pltpu.VMEM((ranks, lo, his, 8, 128), F32),
+            pltpu.VMEM((ranks, lo, block, 2 * width), BF16),
+            pltpu.VMEM((ranks, 2, block, 2 * width), BF16),
+            pltpu.VMEM((ranks, block, 2 * width), BF16),
+            pltpu.VMEM(w.shape, F32),
+            dma((E,)),
+            dma((E,)),
+            dma((4, 3)),
+            dma((4, 3)),
+            dma((4, 2)),
+            dma((4,)),
+            dma((E,)),
+            dma((E,)),
+            dma((E,)),
+            dma((4, 3)),
+            dma((4, 3)),
+            dma((4, 2)),
+            dma((4,)),
+            dma((E,)),
+        ],
+        compiler_params=params(62, collective_id=2, has_side_effects=True),
+        name="moe",
+    )(x, gates, w, g)
 
 
 def combine_kernel(
@@ -956,14 +1365,19 @@
     cols_ref,
     slots_ref,
     routes_ref,
-    g2_ref,
-    wr_ref,
-    vc_ref,
-    *refs,
+    s_ref,
+    od_ref,
+    out_ref,
+    dres_ref,
+    dl_ref,
+    dw_ref,
+    dv_ref,
+    dg2_ref,
 ):
-    od_refs = refs[:E]
-    out_ref, dres_ref, dl_ref, dw_ref, dv_ref, dg2_ref = refs[E:]
     width = cot_ref.shape[1]
+    flat = s_ref[...].T
+    g2 = flat[SMALL_G1 + 1 : SMALL_G1 + 2, :]
+    vc = flat[SMALL_VC : SMALL_VC + CONSTS, :]
     g = cot_ref[...].astype(F32)
     lanes = lane_iota(TOK_DEV)
     cols = cols_ref[...]
@@ -974,9 +1388,9 @@
     gate0, gate1, gate_id, inv2 = col(0), col(1), col(2), col(3)
     resid = resid_ref[...]
     unit2 = resid * inv2
-    normed = unit2 * g2_ref[...]
+    normed = unit2 * g2
     narrow = normed.astype(BF16)
-    od = jnp.concatenate([r[...] for r in od_refs], axis=0)
+    od = od_ref[...].reshape(ROWS, 2 * width)
     slot = lane_iota(TOK_DEV, ROWS)
     hot0 = jnp.where(slot == slots_ref[:, 0:1], 1.0, 0.0).astype(BF16)
     hot1 = jnp.where(slot == slots_ref[:, 1:2], 1.0, 0.0).astype(BF16)
@@ -995,7 +1409,7 @@
     vmix = jnp.zeros((TOK_DEV, 128), F32)
     for c in range(CONSTS):
         gate_c, ma, mb = col(4 + 3 * c), col(5 + 3 * c), col(6 + 3 * c)
-        a_v = jnp.sum(g * vc_ref[c : c + 1, :], axis=1, keepdims=True)
+        a_v = jnp.sum(g * vc[c : c + 1, :], axis=1, keepdims=True)
         branch = ma * a_n + mb * a_v
         dg0 = jnp.where(r0 == E + 2 + c, branch, dg0)
         dg1 = jnp.where(r1 == E + 2 + c, branch, dg1)
@@ -1003,8 +1417,8 @@
         da = gate_c * a_n
         db = gate_c * a_v
         mean = ma * da + mb * db
-        dl = jnp.where(lanes == 16 + 2 * c, ma * (da - mean), dl)
-        dl = jnp.where(lanes == 17 + 2 * c, mb * (db - mean), dl)
+        dl = jnp.where(lanes == SMALL_C + 2 * c, ma * (da - mean), dl)
+        dl = jnp.where(lanes == SMALL_C + 1 + 2 * c, mb * (db - mean), dl)
         vmix = jnp.where(lanes == c, gate_c * mb, vmix)
     probs = probs_ref[...]
     d_probs = jnp.where(lanes == r0, dg0, 0.0) + jnp.where(lanes == r1, dg1, 0.0)
@@ -1013,7 +1427,7 @@
     dl_ref[...] = dl
     high = dl.astype(BF16)
     low = (dl - high.astype(F32)).astype(BF16)
-    wr = wr_ref[...]
+    wr = s_ref[...].astype(BF16)
     d_normed = g_scale * g + mm(hot0 + hot1, od[:, width:])
     d_normed = d_normed + mm(high, wr, NT) + mm(low, wr, NT)
     dw_ref[...] = mm(high, narrow, TN) + mm(low, narrow, TN)
@@ -1023,11 +1437,11 @@
     dg2_ref[...] = jnp.broadcast_to(
         jnp.sum(d_normed * unit2, axis=0, keepdims=True), dg2_ref.shape
     )
-    n = d_normed * g2_ref[...]
+    n = d_normed * g2
     dres_ref[...] = g + inv2 * (n - unit2 * jnp.mean(n * unit2, axis=1, keepdims=True))
 
 
-def combine(cot, resid, part, probs, cols, slots, routes, g2, wr, vc, od):
+def combine(cot, resid, part, probs, cols, slots, routes, small, od):
     width = cot.shape[1]
     return pl.pallas_call(
         combine_kernel,
@@ -1039,19 +1453,16 @@
             sds((128, width), F32),
             sds((8, width), F32),
         ],
-        in_specs=whole(10 + E),
+        in_specs=whole(9),
         out_specs=whole(6),
         compiler_params=params(56),
         name="combine",
-    )(cot, resid, part, probs, cols, slots, routes, g2, wr, vc, *od)
+    )(cot, resid, part, probs, cols, slots, routes, small, od)
 
 
 def backward_kernel(
     dres_ref,
-    wq_ref,
-    wk_ref,
-    wv_ref,
-    wo_ref,
+    wf_ref,
     q_ref,
     k_ref,
     v_ref,
@@ -1080,7 +1491,7 @@
     width = dres_ref.shape[1]
     d_attn = dres_ref[...].astype(BF16)
     gw_ref[3] = mm(mix_ref[...], d_attn, TN).astype(BF16)
-    dm_ref[...] = mm(d_attn, wo_ref[...], NT).astype(BF16)
+    dm_ref[...] = mm(d_attn, wf_ref[3], NT).astype(BF16)
     dk_ref[...] = jnp.zeros_like(dk_ref)
     dv_ref[...] = jnp.zeros_like(dv_ref)
 
@@ -1134,8 +1545,8 @@
     gw_ref[0] = mm(n1_ref[HALO:, :], dqr_ref[...], TN).astype(BF16)
     gw_ref[1] = mm(n1_ref[...], dkr_ref[...], TN).astype(BF16)
     gw_ref[2] = mm(n1_ref[...], dvr_ref[...], TN).astype(BF16)
-    d_all = mm(dkr_ref[...], wk_ref[...], NT) + mm(dvr_ref[...], wv_ref[...], NT)
-    d_own = d_all[HALO:] + mm(dqr_ref[...], wq_ref[...], NT)
+    d_all = mm(dkr_ref[...], wf_ref[1], NT) + mm(dvr_ref[...], wf_ref[2], NT)
+    d_own = d_all[HALO:] + mm(dqr_ref[...], wf_ref[0], NT)
     inv1 = inv1_ref[:, 0:1]
     unit_own = tok_ref[...].astype(F32) * inv1[HALO:]
     unit_halo = halo_ref[...].astype(F32) * inv1[:HALO]
@@ -1148,7 +1559,7 @@
     dhalo_ref[...] = d_halo.astype(BF16)
 
 
-def backward(dres, wq, wk, wv, wo, q, k, v, n1, inv1, mix, lse, cos, sin, pos, tok, halo):
+def backward(dres, wf, q, k, v, n1, inv1, mix, lse, cos, sin, pos, tok, halo):
     width = tok.shape[1]
     return pl.pallas_call(
         backward_kernel,
@@ -1158,7 +1569,7 @@
             sds((HALO, width), BF16),
             sds((8, width), F32),
         ],
-        in_specs=whole(17),
+        in_specs=whole(14),
         out_specs=whole(4),
         scratch_shapes=[
             pltpu.VMEM((TOK_DEV, width), BF16),
@@ -1171,22 +1582,23 @@
         ],
         compiler_params=params(60),
         name="backward",
-    )(dres, wq, wk, wv, wo, q, k, v, n1, inv1, mix, lse, cos, sin, pos, tok, halo)
-
-
-def finish_kernel(dres_ref, down_ref, back_ref, tok_ref, inv1_ref, g1_ref, out_ref):
+    )(dres, wf, q, k, v, n1, inv1, mix, lse, cos, sin, pos, tok, halo)
+
+
+def finish_kernel(dres_ref, down_ref, back_ref, tok_ref, inv1_ref, s_ref, out_ref):
     width = tok_ref.shape[1]
     inv1 = inv1_ref[HALO:, 0:1]
     unit = tok_ref[...].astype(F32) * inv1
     back = jnp.concatenate(
         [jnp.zeros((TOK_DEV - HALO, width), F32), back_ref[...].astype(F32)], axis=0
     )
-    m = (down_ref[...] + back) * g1_ref[...]
+    g1 = s_ref[...].T[SMALL_G1 : SMALL_G1 + 1, :]
+    m = (down_ref[...] + back) * g1
     d_dealt = inv1 * (m - unit * jnp.mean(m * unit, axis=1, keepdims=True))
     out_ref[...] = dres_ref[...] + d_dealt.astype(BF16).astype(F32)
 
 
-def finish(dres, down, back, tok, inv1, g1):
+def finish(dres, down, back, tok, inv1, small):
     return pl.pallas_call(
         finish_kernel,
         out_shape=sds(dres.shape, F32),
@@ -1194,7 +1606,7 @@
         out_specs=pl.BlockSpec(memory_space=pltpu.VMEM),
         compiler_params=params(40),
         name="finish",
-    )(dres, down, back, tok, inv1, g1)
+    )(dres, down, back, tok, inv1, small)
 
 
 def store_kernel(own_ref, *refs):
@@ -1250,57 +1662,23 @@
     width = tokens.shape[1]
     axes = ("grp", "fsdp")
     own = (f_id * his + g_id // lo).astype(jnp.int32).reshape(1)
-
-    def member_perm(k):
-        pairs = []
-        for g in range(groups):
-            for f in range(ranks):
-                m = (f * his + g // lo + k) % E
-                pairs.append((g * ranks + f, (m % his * lo + g % lo) * ranks + m // his))
-        return pairs
-
-    def to_member(x, k):
-        return x if k == 0 else lax.ppermute(x, axes, member_perm(k))
-
-    def near_perm(j):
-        return [(g, g ^ j) for g in range(groups)]
-
-    def near(x, j):
-        return x if j == 0 else lax.ppermute(x, "grp", near_perm(j))
-
-    prep = prepare(own, routes, cotangent, w_gate, w_up, w_down)
-    slots, g_rows, w_tiles = prep[0], prep[1 : 1 + E], prep[1 + E :]
-    halo = lax.ppermute(
-        tokens[TOK_DEV - HALO :], "fsdp", [(f, f + 1) for f in range(ranks - 1)]
-    )
-    packed = jnp.stack([w_query, w_key, w_value, w_out])
-    packed = lax.all_gather(packed, axes, axis=0, tiled=False)
-    packed = packed.reshape((groups, ranks) + packed.shape[1:])
-    full = packed.transpose(2, 1, 3, 0, 4).reshape(4, width, width)
-    wq, wk, wv, wo = full[0], full[1], full[2], full[3]
     per = gain_one.shape[0]
+
     small = jnp.concatenate(
-        [gain_one[:, None], gain_two[:, None], v_const, w_router, w_const], axis=1
-    )
-    small = lax.all_gather(small, axes, axis=0, tiled=True)
-    g1 = small[:, 0][None, :].astype(F32)
-    g2 = small[:, 1][None, :].astype(F32)
-    vc = small[:, 2 : 2 + CONSTS].T.astype(F32)
-    wr = jnp.zeros((width, 128), BF16)
-    wr = wr.at[:, :EXPERTS_ALL].set(small[:, 2 + CONSTS : 2 + CONSTS + EXPERTS_ALL])
-    wr = wr.at[:, 16 : 16 + 2 * CONSTS].set(small[:, 2 + CONSTS + EXPERTS_ALL :])
-    tiles = [to_member(w_tiles[k], k) for k in range(E)]
-    g_in = [to_member(g_rows[k], k) for k in range(E)]
-    g_mine = jnp.concatenate(g_in, axis=0)
-    g_all = [near(g_mine, j) for j in range(lo)]
+        [w_router, gain_one[:, None], gain_two[:, None], v_const, w_const], axis=1
+    )
+    small = jnp.pad(small, ((0, 0), (0, 128 - small.shape[1])))
+    small = small.reshape(per // 8, 8, 128).transpose(1, 0, 2).reshape(8, per // 8 * 128)
+    tile = jnp.concatenate([w_query, w_key, w_value, w_out], axis=1)
+    tile = jnp.concatenate([tile, small], axis=0)
 
     seq_len = lengths[0]
     count = seq_len.shape[0]
     ids = jnp.arange(count, dtype=jnp.int32)
     ends = jnp.sum(jnp.where(ids[:, None] >= ids[None, :], seq_len[None, :], 0), axis=1)
     row = f_id * TOK_DEV + jnp.arange(-HALO, TOK_DEV, dtype=jnp.int32)
-    begin = jnp.max(jnp.where(ends[None, :] <= row[:, None], ends[None, :], 0), axis=1)
-    pos = jnp.maximum(row - begin, 0)
+    start = jnp.max(jnp.where(ends[None, :] <= row[:, None], ends[None, :], 0), axis=1)
+    pos = jnp.maximum(row - start, 0)
     cos, sin = rotation_tables(pos, HEAD_DIM)
     cos = jnp.concatenate([cos] * 4, axis=1)
     sin = jnp.concatenate([-sin, sin, -sin, sin], axis=1)
@@ -1308,42 +1686,45 @@
     mixed_prev = exact_dot(prev_logits, w_mix.astype(F32))
     mixed_prev = jnp.pad(mixed_prev, ((0, 0), (0, 128 - EXPERTS_ALL)))
 
-    fwd = forward(
-        tokens, halo, g1, g2, cos, sin, pos_own, wq, wk, wv, wo, wr, vc, mixed_prev, routes, slots
-    )
-    q, k, v, n1, inv1, mix, lse, resid, part, probs, cols = fwd[:11]
-    x_in = [to_member(fwd[11 + i], i) for i in range(E)]
-    x_mine = jnp.concatenate(x_in, axis=0)
-    x_all = [near(x_mine, j) for j in range(lo)]
-    done = experts(own, x_all, g_all, tiles, his)
-    od, g_tiles = done[:lo], done[lo:]
-
-    def add(a, b):
-        return (a.astype(F32) + b.astype(F32)).astype(BF16)
-
-    half = near(jnp.concatenate([od[1], od[3]], axis=0), 1)
-    here = add(od[0], half[:ROWS])
-    there = add(od[2], half[ROWS:])
-    od_sum = add(here, near(there, 2))
-
-    def back_perm(i):
-        return [(b, a) for a, b in member_perm(i)]
-
-    od_back = []
-    for i in range(E):
-        rows = od_sum[i * MOST : (i + 1) * MOST]
-        od_back.append(rows if i == 0 else lax.ppermute(rows, axes, back_perm(i)))
+    outs = begin(
+        tile,
+        tokens,
+        cotangent,
+        routes,
+        cos,
+        sin,
+        pos_own,
+        mixed_prev,
+        w_down,
+        w_gate,
+        w_up,
+        groups,
+        ranks,
+    )
+    wf, small, halo, slots, q, k, v, n1, inv1, mix, lse, resid, part, probs, cols = outs[:15]
+    x, gates, w_all, g_all = outs[15:]
+    done = moe(x, gates, w_all, g_all, w_gate.shape[1:])
+    od_back, g_tiles = done[0], done[1:]
     output, d_resid, dl, dw, dv, dg2 = combine(
-        cotangent, resid, part, probs, cols, slots, routes, g2, wr, vc, od_back
+        cotangent, resid, part, probs, cols, slots, routes, small, od_back
     )
     d_logits = dl[:, :EXPERTS_ALL]
     grad_prev = exact_dot(d_logits, w_mix.astype(F32).T)
     d_mix = exact_dot(prev_logits.T, d_logits)
     gw, down, d_halo, dg1 = backward(
-        d_resid, wq, wk, wv, wo, q, k, v, n1, inv1, mix, lse, cos, sin, pos_own, tokens, halo
+        d_resid, wf, q, k, v, n1, inv1, mix, lse, cos, sin, pos_own, tokens, halo
     )
     back = lax.ppermute(d_halo, "fsdp", [(f + 1, f) for f in range(ranks - 1)])
-    grad_tokens = finish(d_resid, down, back, tokens, inv1, g1)
+    grad_tokens = finish(d_resid, down, back, tokens, inv1, small)
+
+    def back_perm(k):
+        pairs = []
+        for g in range(groups):
+            for f in range(ranks):
+                m = (f * his + g // lo + k) % E
+                pairs.append(((m % his * lo + g % lo) * ranks + m // his, g * ranks + f))
+        return pairs
+
     tiles_back = [
         g_tiles[i] if i == 0 else lax.ppermute(g_tiles[i], axes, back_perm(i)) for i in range(E)
     ]
@@ -1361,15 +1742,15 @@
             dg2[:1],
             dv[:CONSTS],
             dw[:EXPERTS_ALL],
-            dw[16 : 16 + 2 * CONSTS],
+            dw[SMALL_C : SMALL_C + 2 * CONSTS],
             jnp.pad(d_mix.reshape(1, -1), ((0, 0), (0, width - EXPERTS_ALL * EXPERTS_ALL))),
         ],
         axis=0,
     )
     tiny = lax.psum(tiny, axes)
     grad_mix = tiny[-1, : EXPERTS_ALL * EXPERTS_ALL].reshape(EXPERTS_ALL, EXPERTS_ALL)
-    at = (g_id * ranks + f_id) * per
-    mine = lax.dynamic_slice(tiny, (0, at), (tiny.shape[0], per))
+    first = (g_id * ranks + f_id) * per
+    mine = lax.dynamic_slice(tiny, (0, first), (tiny.shape[0], per))
     n_small = 2 + CONSTS
     return (
         output,
@@ -1392,8 +1773,7 @@
 
 
 def suits(mesh):
-    ranks, groups = mesh.shape["fsdp"], mesh.shape["grp"]
-    return E % ranks == 0 and groups % (E // ranks) == 0 and groups // (E // ranks) == 4
+    return mesh.shape["fsdp"] == 4 and mesh.shape["grp"] == 8
 
 
 def solution(mesh):

time: 715 us -> 536 us (0.75)
  waiting for transfers between devices: 303 us -> 116 us
  Pallas kernels: 102 us -> 277 us
  starting transfers between devices: 94.1 us -> 13.7 us
  blocking collectives: 115 us -> 63.7 us
  local copies, waits for them, and re-layouts: 66 us -> 41.3 us
  other arithmetic: 12.4 us -> 5.1 us
    ppermute x37 -> x0, waiting for transfers between devices: 206 us -> none  [the longest x8 132 us: near(): return x if j == 0 else lax.ppermute(x, 'grp', near_perm(j))]
    pallas_call x3 -> x2, Pallas kernels: 63.6 us -> 236 us  [the longest x1 136 us: moe(): pl.pallas_call(moe_kernel, out_shape=[sds((E, MOST, 2 * width), BF16)] +...]
    ppermute x37 -> x0, starting transfers between devices: 80.8 us -> none  [the longest x21 64.4 us: to_member(): return x if k == 0 else lax.ppermute(x, axes, member_perm(k))]
    all_gather x1 -> x0, blocking collectives: 74.1 us -> none  [fast_device(): small = lax.all_gather(small, axes, axis=0, tiled=True)]
    psum x1, blocking collectives: 41.3 us -> 63.7 us  [fast_device(): tiny = lax.psum(tiny, axes)]
    ppermute x7, waiting for transfers between devices: 2.22 us -> 21.4 us  [fast_device(): lax.ppermute(g_tiles[i], axes, back_perm(i))]
    squeeze x4 -> x0, local copies, waits for them, and re-layouts: 12.3 us -> none  [fast_device(): wq, wk, wv, wo = (full[0], full[1], full[2], full[3])]
    reshape x1, local copies, waits for them, and re-layouts: 8.39 us -> 0.01 us  [fast_device(): small.reshape(per // 8, 8, 128).transpose(1, 0, 2)]
  transfers between devices with their start and end apart: 48 -> 10, of which waited for: 17 -> 2; matrix products, arithmetic and copies ran while one was open for 8% -> 4% of each run, Pallas kernels for 4% -> 1%
where the time goes in v2:
time: 536 us; the launch traced here: 535 us
  Pallas kernels  277 us (52%)
  waiting for transfers between devices  116 us (22%)
  blocking collectives  63.7 us (12%)
  local copies, waits for them, and re-layouts  41.3 us (8%)
  between operations  14.3 us (3%)
  starting transfers between devices  13.7 us (3%)
    pallas_call x1, Pallas kernels, moe(): pl.pallas_call(moe_kernel, out_shape=[sds((E, MOST, 2 * width), BF16)] +...  136 us
    pallas_call x1, Pallas kernels, begin(): pl.pallas_call(begin_kernel, out_shape=[sds((4, width, width), BF16), sds...  100 us
    unnamed x3, waiting for transfers between devices  94.7 us
    psum x1, blocking collectives, fast_device(): tiny = lax.psum(tiny, axes)  63.7 us
    pallas_call x1, Pallas kernels, backward(): pl.pallas_call(backward_kernel, out_shape=[sds((4, width, width), BF16),...  28.4 us
    ppermute x7, waiting for transfers between devices, fast_device(): lax.ppermute(g_tiles[i], axes, back_perm(i))  21.4 us
    unnamed x36, local copies, waits for them, and re-layouts  12.8 us
    ppermute x7, starting transfers between devices, fast_device(): lax.ppermute(g_tiles[i], axes, back_perm(i))  12.1 us
  transfers between devices with their start and end apart: 10, of which 2 were waited for; matrix products, arithmetic and copies ran while one was open for 4% of the time, Pallas kernels for 1%

profile of v2, /device:TPU:0, one launch (start us, length us, event | category | flops | bytes accessed | tf_op | source)
XLA Modules:
  0.0 535.0 jit_solution(1177275644758045256)
XLA Ops:
  8.2 1.5 copy.90.routes_ref
  9.7 2.2 copy.91.wd_ref
  18.6 1.4 pad_maximum_fusion
  21.6 100.3 %begin.1 = (bf16[4,768,768]{2,1,0:T(8,128)(2,1)}, f32[768,128]{1,0:T(8,128)}, bf16[256,768]{1,0:T(8,128)(2,1)}, s32[320,128]{1,0:T(8,128)}, bf16[320,768]{1,0:T(...) custom-call(bf16[200,384]{1,0:T(8,128)(2,1)} %pad_maximum_fusion.2.t, ...), custom_call_target="tpu_custom_call" | custom-call | tf_op jit(solution)/shard_map/begin/pallas_call | solution.py:1071
  121.8 135.5 %moe.1 = (bf16[8,80,1536]{2,1,0:T(8,128)(2,1)}, bf16[3,192,256]{2,1,0:T(8,128)(2,1)}, bf16[3,192,256]{2,1,0:T(8,128)(2,1)}, bf16[3,192,256]{2,1,0:T(8,128)(2,1)}...) custom-call(bf16[640,768]{1,0:T(8,128)(2,1)} %get-tuple-element.63.x, ...), custom_call_target="tpu_custom_call" | custom-call | tf_op jit(solution)/shard_map/moe/pallas_call | solution.py:1328
  257.4 6.7 %combine.1 = (bf16[320,768]{1,0:T(8,128)(2,1)}, f32[320,768]{1,0:T(8,128)}, f32[320,128]{1,0:T(8,128)}, f32[128,768]{1,0:T(8,128)}, f32[128,768]{1,0:T(8,128)}, /*index=5*/f32[8,768]{1,0:T(8,128)}) custom-call(bf16[320,768]{1,0:T(8,128)(2,1)} %cot_ref.3, f32[320,768]{1,0:T(8,128)} %get-tuple-element.57.resid_ref, f32[320,768]{1,0:T(8,128)} %get-tuple-element.58.part_ref, ...), custom_call_target="tpu_custom_call" | custom-call | tf_op jit(solution)/shard_map/combine/pallas_call | solution.py:1446
  264.1 28.4 %backward.1 = (bf16[4,768,768]{2,1,0:T(8,128)(2,1)}, f32[320,768]{1,0:T(8,128)}, bf16[256,768]{1,0:T(8,128)(2,1)}, f32[8,768]{1,0:T(8,128)}) custom-call(f32[320,768]{1,0:T(8,128)} %get-tuple-element.69.dres_ref, bf16[4,768,768]{2,1,0:T(8,128)(2,1)} %get-tuple-element.70.wf_ref, bf16[320,768]{1,0:T(8,128)(2,1)} %get-tuple-element.71.q_ref, ...), custom_call_target="tpu_custom_call" | custom-call | tf_op jit(solution)/shard_map/backward/pallas_call | solution.py:1564
  292.5 6.7 %copy.94 = bf16[4,768,768]{1,2,0:T(8,128)(2,1)} copy(bf16[4,768,768]{2,1,0:T(8,128)(2,1)} %get-tuple-element.86) | data formatting | bytes 9437184 | tf_op jit(solution)/shard_map/backward/pallas_call | solution.py:1564
  300.4 94.6 %all-reduce.6.cloned.1.call-done = bf16[8,4,768,96]{2,3,0,1:T(8,128)(2,1)} async-done(((bf16[8,4,768,96]{2,3,0,1:T(8,128)(2,1)}), bf16[8,4,768,96]{2,3,0,1:T(8,128)(2,1)}) %all-reduce.6.cloned.1.call-update) | async-done | bytes 4718608
  395.0 1.8 constant_dynamic-slice_fusion
  398.8 4.1 collective-permute-start.1
  403.5 3.1 collective-permute-start.4
  407.9 1.4 slice.60
  416.1 2.3 concatenate.23
  418.4 63.7 %psum.7 = f32[21,768]{1,0:T(8,128)} all-reduce(f32[21,768]{1,0:T(8,128)S(1)} %concatenate.23), channel_id=1, replica_groups=mesh['grp'=8,'fsdp'=4] {'grp','fsdp'}, use_global_device_ids=true, to_apply=%region_2.3 | all-reduce | flops 16128 | bytes 129024 | tf_op jit(solution)/shard_map/psum | solution.py:1750
  482.2 1.4 dynamic-slice_bitcast_fusion
  487.7 1.6 collective-permute-start.5
  489.2 1.5 collective-permute-start.6
  492.0 1.4 dynamic-slice_bitcast_fusion.3
  493.4 1.7 fusion.1
  495.1 21.4 %collective-permute-done.5.refs_5_ = bf16[3,192,256]{2,1,0:T(8,128)(2,1)S(1)} collective-permute-done((bf16[3,192,256]{2,1,0:T(8,128)(2,1)}, bf16[3,192,256]{2,1,0:T(8,128)(2,1)S(1)}, u32[]{:S(2)}, u32[]{:S(2)}) %collective-permute-start.5) | collective-permute-done | bytes 294944 | tf_op jit(solution)/shard_map/ppermute | solution.py:1729
  516.5 3.3 store.1
  521.2 2.8 copy.96
  524.0 2.5 finish.1
  (79 shorter events, 29.5 us)
Async XLA Ops:
  7.2 9.7 %copy-start = (f32[320,12]{0,1:T(8,128)S(1)}, f32[320,12]{0,1:T(8,128)}, u32[]{:S(2)}) copy-start(f32[320,12]{0,1:T(8,128)} %param.21) | copy-start | bytes 46084
  7.2 12.8 %copy-start.11 = (bf16[192,96]{1,0:T(8,128)(2,1)S(1)}, bf16[192,96]{1,0:T(8,128)(2,1)}, u32[]{:S(2)}) copy-start(bf16[192,96]{1,0:T(8,128)(2,1)} %param.25) | copy-start | bytes 110596
  7.2 12.8 %copy-start.10 = (bf16[192,96]{1,0:T(8,128)(2,1)S(1)}, bf16[192,96]{1,0:T(8,128)(2,1)}, u32[]{:S(2)}) copy-start(bf16[192,96]{1,0:T(8,128)(2,1)} %param.26) | copy-start | bytes 110596
  7.2 12.8 %copy-start.9 = (bf16[192,96]{1,0:T(8,128)(2,1)S(1)}, bf16[192,96]{1,0:T(8,128)(2,1)}, u32[]{:S(2)}) copy-start(bf16[192,96]{1,0:T(8,128)(2,1)} %param.27) | copy-start | bytes 110596
  7.2 12.8 %copy-start.8 = (bf16[192,96]{1,0:T(8,128)(2,1)S(1)}, bf16[192,96]{1,0:T(8,128)(2,1)}, u32[]{:S(2)}) copy-start(bf16[192,96]{1,0:T(8,128)(2,1)} %param.28) | copy-start | bytes 110596
  7.2 387.8 %all-reduce.6.cloned.1.call-start = ((), (), s32[]{:S(2)}) async-start(), calls=%async_computation.2 | async-start | bytes 9437184
  299.1 0.7 copy-start.13
  299.1 194.2 %copy-start.12 = (bf16[12,12]{1,0:T(8,128)(2,1)S(1)}, bf16[12,12]{1,0:T(8,128)(2,1)}, u32[]{:S(2)}) copy-start(bf16[12,12]{1,0:T(8,128)(2,1)} %param.31) | copy-start | bytes 868
  299.2 217.4 %copy-start.7 = (bf16[3,192,256]{2,1,0:T(8,128)(2,1)S(1)}, bf16[3,192,256]{2,1,0:T(8,128)(2,1)}, u32[]{:S(2)}) copy-start(bf16[3,192,256]{2,1,0:T(8,128)(2,1)} %get-tuple-element.87.refs_0_) | copy-start | bytes 884740
  299.2 227.3 %reduce-scatter.5.cloned.1.call-start = ((), (), s32[]{:S(2)}) async-start(), calls=%async_computation.1 | async-start | bytes 983040 | tf_op jit(solution)/shard_map/reduce_scatter | solution.py:1738
  398.7 125.2 %copy-start.1 = (bf16[320,768]{1,0:T(8,128)(2,1)S(1)}, bf16[320,768]{1,0:T(8,128)(2,1)}, u32[]{:S(2)}) copy-start(bf16[320,768]{1,0:T(8,128)(2,1)} %tok_ref.5) | copy-start | bytes 1474564
  398.7 125.2 %copy-start.2 = (f32[320,768]{1,0:T(8,128)S(1)}, f32[320,768]{1,0:T(8,128)}, u32[]{:S(2)}) copy-start(f32[320,768]{1,0:T(8,128)} %get-tuple-element.69.dres_ref) | copy-start | bytes 2949124
  398.8 125.2 %copy-start.4 = (f32[768,128]{1,0:T(8,128)S(1)}, f32[768,128]{1,0:T(8,128)}, u32[]{:S(2)}) copy-start(f32[768,128]{1,0:T(8,128)} %get-tuple-element.62.s_ref) | copy-start | bytes 1179652
  398.8 125.2 %copy-start.5 = (f32[576,128]{1,0:T(8,128)S(1)}, f32[576,128]{1,0:T(8,128)}, u32[]{:S(2)}) copy-start(f32[576,128]{1,0:T(8,128)} %get-tuple-element.75.inv1_ref) | copy-start | bytes 884740
  398.8 125.2 %copy-start.6 = (f32[320,768]{1,0:T(8,128)S(1)}, f32[320,768]{1,0:T(8,128)}, u32[]{:S(2)}) copy-start(f32[320,768]{1,0:T(8,128)} %get-tuple-element.79.down_ref) | copy-start | bytes 2949124
  398.8 88.9 %collective-permute-start.1 = (bf16[3,192,256]{2,1,0:T(8,128)(2,1)}, bf16[3,192,256]{2,1,0:T(8,128)(2,1)}, u32[]{:S(2)}, u32[]{:S(2)}) collective-permute-start(bf16[3,192,256]{2,1,0:T(8,128)(2,1)} %get-tuple-element.88), channel_id=1, source_target_pairs={{16,0},{17,1},{18,2},{19,3},{20,4},{21,5},{22,6},{23,7},{24,8},{25... | collective-permute-start | bytes 884744 | tf_op jit(solution)/shard_map/ppermute | solution.py:1729
  402.9 86.3 %collective-permute-start.2 = (bf16[3,192,256]{2,1,0:T(8,128)(2,1)}, bf16[3,192,256]{2,1,0:T(8,128)(2,1)}, u32[]{:S(2)}, u32[]{:S(2)}) collective-permute-start(bf16[3,192,256]{2,1,0:T(8,128)(2,1)} %get-tuple-element.89), channel_id=1, source_target_pairs={{1,0},{2,1},{3,2},{0,3},{5,4},{6,5},{7,6},{4,7},{9,8},{10,9},{11,1... | collective-permute-start | bytes 884744 | tf_op jit(solution)/shard_map/ppermute | solution.py:1729
  403.5 87.2 %collective-permute-start.3 = (bf16[3,192,256]{2,1,0:T(8,128)(2,1)}, bf16[3,192,256]{2,1,0:T(8,128)(2,1)}, u32[]{:S(2)}, u32[]{:S(2)}) collective-permute-start(bf16[3,192,256]{2,1,0:T(8,128)(2,1)} %get-tuple-element.90), channel_id=1, source_target_pairs={{17,0},{18,1},{19,2},{16,3},{21,4},{22,5},{23,6},{20,7},{25,8},{26... | collective-permute-start | bytes 884744 | tf_op jit(solution)/shard_map/ppermute | solution.py:1729
  403.5 91.6 %collective-permute-start.4 = (bf16[3,192,256]{2,1,0:T(8,128)(2,1)}, bf16[3,192,256]{2,1,0:T(8,128)(2,1)}, u32[]{:S(2)}, u32[]{:S(2)}) collective-permute-start(bf16[3,192,256]{2,1,0:T(8,128)(2,1)} %get-tuple-element.91), channel_id=1, source_target_pairs={{2,0},{3,1},{0,2},{1,3},{6,4},{7,5},{4,6},{5,7},{10,8},{11,9},{8,1... | collective-permute-start | bytes 884744 | tf_op jit(solution)/shard_map/ppermute | solution.py:1729
  406.6 117.4 %collective-permute-start = (bf16[256,768]{1,0:T(8,128)(2,1)}, bf16[256,768]{1,0:T(8,128)(2,1)}, u32[]{:S(2)}, u32[]{:S(2)}) collective-permute-start(bf16[256,768]{1,0:T(8,128)(2,1)} %get-tuple-element.80), channel_id=1, source_target_pairs={{1,0},{2,1},{3,2},{5,4},{6,5},{7,6},{9,8},{10,9},{11,10},{13,12},{... | collective-permute-start | bytes 1179656 | tf_op jit(solution)/shard_map/ppermute | solution.py:1717
  487.7 28.9 %collective-permute-start.5 = (bf16[3,192,256]{2,1,0:T(8,128)(2,1)}, bf16[3,192,256]{2,1,0:T(8,128)(2,1)S(1)}, u32[]{:S(2)}, u32[]{:S(2)}) collective-permute-start(bf16[3,192,256]{2,1,0:T(8,128)(2,1)} %get-tuple-element.92), channel_id=1, source_target_pairs={{18,0},{19,1},{16,2},{17,3},{22,4},{23,5},{20,6},{21,7},{26,8},{27... | collective-permute-start | bytes 884744 | tf_op jit(solution)/shard_map/ppermute | solution.py:1729
  489.2 27.3 %collective-permute-start.6 = (bf16[3,192,256]{2,1,0:T(8,128)(2,1)}, bf16[3,192,256]{2,1,0:T(8,128)(2,1)S(1)}, u32[]{:S(2)}, u32[]{:S(2)}) collective-permute-start(bf16[3,192,256]{2,1,0:T(8,128)(2,1)} %get-tuple-element.93), channel_id=1, source_target_pairs={{3,0},{0,1},{1,2},{2,3},{7,4},{4,5},{5,6},{6,7},{11,8},{8,9},{9,10... | collective-permute-start | bytes 884744 | tf_op jit(solution)/shard_map/ppermute | solution.py:1729
  490.7 25.8 %collective-permute-start.7 = (bf16[3,192,256]{2,1,0:T(8,128)(2,1)}, bf16[3,192,256]{2,1,0:T(8,128)(2,1)S(1)}, u32[]{:S(2)}, u32[]{:S(2)}) collective-permute-start(bf16[3,192,256]{2,1,0:T(8,128)(2,1)} %get-tuple-element.94), channel_id=1, source_target_pairs={{19,0},{16,1},{17,2},{18,3},{23,4},{20,5},{21,6},{22,7},{27,8},{24... | collective-permute-start | bytes 884744 | tf_op jit(solution)/shard_map/ppermute | solution.py:1729
  519.8 1.3 copy-start.3
Sparse Core Ops, SparseCore 0:
  299.3 95.6 all-reduce.5
  398.9 49.8 reduce-scatter.4

commit v3 on v2

--- a/solution.py
+++ b/solution.py
@@ -618,12 +618,6 @@
     return jnp.sum(jnp.where(lane_mask, values, 0.0), axis=1, keepdims=True)
 
 
-def split_mm(mat, wide, dims):
-    high = wide.astype(BF16)
-    low = (wide - high.astype(F32)).astype(BF16)
-    return mm(mat, high, dims) + mm(mat, low, dims)
-
-
 def params(mb, **kw):
     return pltpu.CompilerParams(vmem_limit_bytes=mb << 20, **kw)
 
@@ -737,7 +731,8 @@
     cos_ref,
     sin_ref,
     pos_ref,
-    mixed_prev_ref,
+    prev_ref,
+    wmix_ref,
     wd_ref,
     wg_hbm,
     wu_hbm,
@@ -982,7 +977,14 @@
     normed = resid * inv2 * g2
     narrow = normed.astype(BF16)
     raw = mm(narrow, s_ref[...].astype(BF16))
-    logits = jnp.where(lanes < EXPERTS_ALL, raw + mixed_prev_ref[...], NEG)
+    prev = prev_ref[...]
+    wmix = wmix_ref[...]
+    phigh = prev.astype(BF16)
+    prest = prev - phigh.astype(F32)
+    pmid = prest.astype(BF16)
+    plow = (prest - pmid.astype(F32)).astype(BF16)
+    mixed_prev = mm(phigh, wmix) + (mm(pmid, wmix) + mm(plow, wmix))
+    logits = jnp.where(lanes < EXPERTS_ALL, raw + mixed_prev, NEG)
     top = jnp.max(logits, axis=1, keepdims=True)
     ex = jnp.exp(logits - top)
     probs = ex / jnp.sum(ex, axis=1, keepdims=True)
@@ -1060,7 +1062,9 @@
 SMALL_C = SMALL_VC + CONSTS
 
 
-def begin(tile, tok, cot, routes, cos, sin, pos, mixed_prev, w_down, w_gate, w_up, groups, ranks):
+def begin(
+    tile, tok, cot, routes, cos, sin, pos, prev, wmix, w_down, w_gate, w_up, groups, ranks
+):
     width = tok.shape[1]
     lo = groups * ranks // E
     his = E // ranks
@@ -1091,7 +1095,7 @@
             sds((3, width, ff * his), BF16),
             sds((lo, ranks, his * MOST, width), BF16),
         ],
-        in_specs=whole(9) + [any_spec, any_spec],
+        in_specs=whole(10) + [any_spec, any_spec],
         out_specs=whole(17) + [any_spec, any_spec],
         scratch_shapes=[
             pltpu.VMEM((groups, ranks) + tile.shape, BF16),
@@ -1112,7 +1116,7 @@
         ],
         compiler_params=params(60, collective_id=1, has_side_effects=True),
         name="begin",
-    )(tile, tok, cot, routes, cos, sin, pos, mixed_prev, w_down, w_gate, w_up)
+    )(tile, tok, cot, routes, cos, sin, pos, prev, wmix, w_down, w_gate, w_up)
 
 
 def moe_kernel(
@@ -1121,31 +1125,28 @@
     w_ref,
     g_ref,
     back_ref,
-    *rest,
+    gw_ref,
+    xb_ref,
+    gb_ref,
+    od_ref,
+    r1_ref,
+    r2_ref,
+    acc_ref,
+    xs,
+    gs,
+    qs,
+    gqs,
+    d1s,
+    d2s,
+    bs,
+    xr,
+    gr,
+    qr,
+    gqr,
+    d1r,
+    d2r,
+    br,
 ):
-    gt_refs = rest[:E]
-    (
-        xb_ref,
-        gb_ref,
-        od_ref,
-        r1_ref,
-        r2_ref,
-        acc_ref,
-        xs,
-        gs,
-        qs,
-        gqs,
-        d1s,
-        d2s,
-        bs,
-        xr,
-        gr,
-        qr,
-        gqr,
-        d1r,
-        d2r,
-        br,
-    ) = rest[E:]
     lo, ranks = g_ref.shape[:2]
     his = E // ranks
     width = x_ref.shape[1]
@@ -1294,14 +1295,7 @@
 
     lax.fori_loop(0, ranks + 2, step, 0)
 
-    tile = gt_refs[0].shape[1:]
-    for k in range(E):
-        source = lax.rem(at.m - k + E, E)
-        rows = pl.ds(aligned(source // his * tile[0], 16), tile[0])
-        cols = pl.ds(aligned(lax.rem(source, his) * tile[1], 128), tile[1])
-        for w in range(3):
-            gt_refs[k][w] = acc_ref[w, rows, cols].astype(BF16)
-
+    gw_ref[...] = acc_ref[...].astype(BF16)
     for m in range(E):
         settle(back_ref.at[m], br.at[m])
     for k in range(1, E):
@@ -1321,15 +1315,15 @@
                 settle(back_ref.at[0], bs.at[m])
 
 
-def moe(x, gates, w, g, tile):
+def moe(x, gates, w, g):
     lo, ranks, block, width = g.shape
     dma = pltpu.SemaphoreType.DMA
     his = E // ranks
     return pl.pallas_call(
         moe_kernel,
-        out_shape=[sds((E, MOST, 2 * width), BF16)] + [sds((3,) + tile, BF16)] * E,
+        out_shape=[sds((E, MOST, 2 * width), BF16), sds(w.shape, BF16)],
         in_specs=whole(4),
-        out_specs=whole(1 + E),
+        out_specs=whole(2),
         scratch_shapes=[
             pltpu.VMEM((ranks, lo, block, width), BF16),
             pltpu.VMEM((ranks, lo, his, 8, 128), F32),
@@ -1357,7 +1351,7 @@
     )(x, gates, w, g)
 
 
-def combine_kernel(
+def end_kernel(
     cot_ref,
     resid_ref,
     part_ref,
@@ -1365,18 +1359,95 @@
     cols_ref,
     slots_ref,
     routes_ref,
+    prev_ref,
+    wmix_ref,
     s_ref,
     od_ref,
+    gw_ref,
+    wf_ref,
+    q_ref,
+    k_ref,
+    v_ref,
+    n1_ref,
+    inv1_ref,
+    mix_ref,
+    lse_ref,
+    cos_ref,
+    sin_ref,
+    pos_ref,
+    tok_ref,
+    halo_ref,
     out_ref,
     dres_ref,
-    dl_ref,
-    dw_ref,
+    gprev_ref,
+    down_ref,
+    back_ref,
+    t_ref,
+    fin_ref,
+    gmix_ref,
+    flat_ref,
+    dhalo_ref,
+    dm_ref,
+    dq_ref,
+    dk_ref,
     dv_ref,
-    dg2_ref,
+    dqr_ref,
+    dkr_ref,
+    dvr_ref,
+    full_ref,
+    p_ref,
+    r1_ref,
+    r2_ref,
+    r3_ref,
+    r4_ref,
+    mx_ref,
+    mr_ref,
+    mz_ref,
+    ts,
+    tr,
+    hs,
+    hr,
+    s1,
+    e1,
+    s2,
+    e2,
+    s3,
+    e3,
+    s4,
+    e4,
+    ms,
+    me,
+    zs,
+    ze,
 ):
+    ranks = p_ref.shape[1]
+    his = E // ranks
+    groups = p_ref.shape[0]
+    lo = groups // his
+    at = Place(his, lo)
     width = cot_ref.shape[1]
+    tile = t_ref.shape[2:]
+    core = (at.core_peer, at.f)
+    side = (at.side_peer, at.f)
+    upper = (lo * (1 - at.hi) + at.l, at.f)
+    greet(at.others() + [core, side])
+
+    for j in range(ranks):
+        for hh in range(his):
+            e, peer = at.member(j, hh)
+            rows = pl.ds(aligned(e // his * tile[0], 16), tile[0])
+            lanes_at = pl.ds(aligned(lax.rem(e, his) * tile[1], 128), tile[1])
+            n = j * his + hh
+            for w in range(3):
+                block = gw_ref.at[w, rows, lanes_at]
+                if n == 0:
+                    pltpu.make_async_copy(block, t_ref.at[at.m, w], tr.at[at.m, w]).start()
+                else:
+                    send(block, t_ref.at[at.m, w], ts.at[n, w], tr.at[at.m, w], peer)
+
     flat = s_ref[...].T
-    g2 = flat[SMALL_G1 + 1 : SMALL_G1 + 2, :]
+    gain1 = flat[SMALL_G1 : SMALL_G1 + 1, :]
+    gain2 = flat[SMALL_G1 + 1 : SMALL_G1 + 2, :]
     vc = flat[SMALL_VC : SMALL_VC + CONSTS, :]
     g = cot_ref[...].astype(F32)
     lanes = lane_iota(TOK_DEV)
@@ -1388,7 +1459,7 @@
     gate0, gate1, gate_id, inv2 = col(0), col(1), col(2), col(3)
     resid = resid_ref[...]
     unit2 = resid * inv2
-    normed = unit2 * g2
+    normed = unit2 * gain2
     narrow = normed.astype(BF16)
     od = od_ref[...].reshape(ROWS, 2 * width)
     slot = lane_iota(TOK_DEV, ROWS)
@@ -1419,78 +1490,37 @@
         mean = ma * da + mb * db
         dl = jnp.where(lanes == SMALL_C + 2 * c, ma * (da - mean), dl)
         dl = jnp.where(lanes == SMALL_C + 1 + 2 * c, mb * (db - mean), dl)
-        vmix = jnp.where(lanes == c, gate_c * mb, vmix)
+        vmix = jnp.where(lanes == SMALL_VC + c, gate_c * mb, vmix)
     probs = probs_ref[...]
     d_probs = jnp.where(lanes == r0, dg0, 0.0) + jnp.where(lanes == r1, dg1, 0.0)
     d_logits = probs * (d_probs - jnp.sum(probs * d_probs, axis=1, keepdims=True))
     dl = jnp.where(lanes < EXPERTS_ALL, d_logits, dl)
-    dl_ref[...] = dl
     high = dl.astype(BF16)
     low = (dl - high.astype(F32)).astype(BF16)
     wr = s_ref[...].astype(BF16)
     d_normed = g_scale * g + mm(hot0 + hot1, od[:, width:])
     d_normed = d_normed + mm(high, wr, NT) + mm(low, wr, NT)
-    dw_ref[...] = mm(high, narrow, TN) + mm(low, narrow, TN)
     vhigh = vmix.astype(BF16)
     vlow = (vmix - vhigh.astype(F32)).astype(BF16)
-    dv_ref[...] = mm(vhigh, cot_ref[...], TN) + mm(vlow, cot_ref[...], TN)
-    dg2_ref[...] = jnp.broadcast_to(
-        jnp.sum(d_normed * unit2, axis=0, keepdims=True), dg2_ref.shape
-    )
-    n = d_normed * g2
+    tiny = mm(high, narrow, TN) + mm(low, narrow, TN)
+    tiny = tiny + mm(vhigh, cot_ref[...], TN) + mm(vlow, cot_ref[...], TN)
+    row_id = lax.broadcasted_iota(jnp.int32, (128, width), 0)
+    dg2 = jnp.sum(d_normed * unit2, axis=0, keepdims=True)
+    flat_ref[...] = jnp.where(row_id == SMALL_G1 + 1, dg2, tiny)
+    n = d_normed * gain2
     dres_ref[...] = g + inv2 * (n - unit2 * jnp.mean(n * unit2, axis=1, keepdims=True))
-
-
-def combine(cot, resid, part, probs, cols, slots, routes, small, od):
-    width = cot.shape[1]
-    return pl.pallas_call(
-        combine_kernel,
-        out_shape=[
-            sds((TOK_DEV, width), BF16),
-            sds((TOK_DEV, width), F32),
-            sds((TOK_DEV, 128), F32),
-            sds((128, width), F32),
-            sds((128, width), F32),
-            sds((8, width), F32),
-        ],
-        in_specs=whole(9),
-        out_specs=whole(6),
-        compiler_params=params(56),
-        name="combine",
-    )(cot, resid, part, probs, cols, slots, routes, small, od)
-
-
-def backward_kernel(
-    dres_ref,
-    wf_ref,
-    q_ref,
-    k_ref,
-    v_ref,
-    n1_ref,
-    inv1_ref,
-    mix_ref,
-    lse_ref,
-    cos_ref,
-    sin_ref,
-    pos_ref,
-    tok_ref,
-    halo_ref,
-    gw_ref,
-    down_ref,
-    dhalo_ref,
-    dg1_ref,
-    dm_ref,
-    dq_ref,
-    dk_ref,
-    dv_ref,
-    dqr_ref,
-    dkr_ref,
-    dvr_ref,
-):
+    wmix = wmix_ref[...]
+    gprev_ref[...] = mm(high, wmix, NT) + mm(low, wmix, NT)
+    prev = prev_ref[...]
+    phigh = prev.astype(BF16)
+    plow = (prev - phigh.astype(F32)).astype(BF16)
+    d_mix = mm(phigh, high, TN) + mm(phigh, low, TN) + mm(plow, high, TN)
+    mx_ref[0] = d_mix[0:16]
+    send(mx_ref.at[0], mr_ref.at[0], ms.at[0], me.at[0], core)
+
     scale = HEAD_DIM ** (-0.5)
-    width = dres_ref.shape[1]
     d_attn = dres_ref[...].astype(BF16)
-    gw_ref[3] = mm(mix_ref[...], d_attn, TN).astype(BF16)
+    full_ref[3] = mm(mix_ref[...], d_attn, TN).astype(BF16)
     dm_ref[...] = mm(d_attn, wf_ref[3], NT).astype(BF16)
     dk_ref[...] = jnp.zeros_like(dk_ref)
     dv_ref[...] = jnp.zeros_like(dv_ref)
@@ -1514,11 +1544,11 @@
                 qh = jnp.where(mine, q, jnp.zeros_like(q))
                 dmh = jnp.where(mine, dm, jnp.zeros_like(dm))
                 s = jnp.where(ok, mm(qh, k, NT) * scale, NEG)
-                probs = jnp.where(ok, jnp.exp(s - pick(lse, lane == 2 * p + h)), 0.0)
+                pr = jnp.where(ok, jnp.exp(s - pick(lse, lane == 2 * p + h)), 0.0)
                 dp = mm(dmh, v, NT)
-                delta = jnp.sum(probs * dp, axis=1, keepdims=True)
-                ds = (probs * (dp - delta)).astype(BF16)
-                pb = probs.astype(BF16)
+                delta = jnp.sum(pr * dp, axis=1, keepdims=True)
+                ds = (pr * (dp - delta)).astype(BF16)
+                pb = pr.astype(BF16)
                 dqh = mm(ds, k)
                 dkh = mm(ds, q, TN)
                 dvh = mm(pb, dm, TN)
@@ -1532,7 +1562,7 @@
 
     lax.fori_loop(0, HEADS // 2, pair, 0)
 
-    def finish(i, _):
+    def unturn(i, _):
         span = pl.ds(pl.multiple_of(i * 256, 256), 256)
         cos = cos_ref[...]
         sin = sin_ref[...]
@@ -1541,95 +1571,264 @@
         dvr_ref[:, span] = dv_ref[:, span].astype(BF16)
         return 0
 
-    lax.fori_loop(0, width // 256, finish, 0)
-    gw_ref[0] = mm(n1_ref[HALO:, :], dqr_ref[...], TN).astype(BF16)
-    gw_ref[1] = mm(n1_ref[...], dkr_ref[...], TN).astype(BF16)
-    gw_ref[2] = mm(n1_ref[...], dvr_ref[...], TN).astype(BF16)
+    lax.fori_loop(0, width // 256, unturn, 0)
     d_all = mm(dkr_ref[...], wf_ref[1], NT) + mm(dvr_ref[...], wf_ref[2], NT)
+    dhalo_ref[...] = (d_all[:HALO] * gain1).astype(BF16)
+
+    @pl.when(at.f > 0)
+    def _():
+        send(dhalo_ref, back_ref, hs, hr, (at.g, at.f - 1))
+
+    @pl.when(at.f == ranks - 1)
+    def _():
+        back_ref[...] = jnp.zeros_like(back_ref)
+
+    full_ref[0] = mm(n1_ref[HALO:, :], dqr_ref[...], TN).astype(BF16)
+    full_ref[1] = mm(n1_ref[...], dkr_ref[...], TN).astype(BF16)
+    full_ref[2] = mm(n1_ref[...], dvr_ref[...], TN).astype(BF16)
     d_own = d_all[HALO:] + mm(dqr_ref[...], wf_ref[0], NT)
     inv1 = inv1_ref[:, 0:1]
     unit_own = tok_ref[...].astype(F32) * inv1[HALO:]
     unit_halo = halo_ref[...].astype(F32) * inv1[:HALO]
-    d_halo = d_all[:HALO]
     dg1 = jnp.sum(d_own * unit_own, axis=0, keepdims=True) + jnp.sum(
-        d_halo * unit_halo, axis=0, keepdims=True
-    )
-    dg1_ref[...] = jnp.broadcast_to(dg1, dg1_ref.shape)
-    down_ref[...] = d_own
-    dhalo_ref[...] = d_halo.astype(BF16)
-
-
-def backward(dres, wf, q, k, v, n1, inv1, mix, lse, cos, sin, pos, tok, halo):
-    width = tok.shape[1]
+        d_all[:HALO] * unit_halo, axis=0, keepdims=True
+    )
+    down_ref[...] = d_own * gain1
+    flat_ref[...] = jnp.where(row_id == SMALL_G1, dg1, flat_ref[...])
+
+    part_cols = width // groups
+    head_rows = width // ranks
+
+    def pack(f2, _):
+        rows = pl.ds(aligned(f2 * head_rows, 16), head_rows)
+        for g2 in range(groups):
+            pieces = [
+                full_ref[w, rows, g2 * part_cols : (g2 + 1) * part_cols] for w in range(4)
+            ]
+            p_ref[g2, f2, 0:head_rows, :] = jnp.concatenate(pieces, axis=1)
+        return 0
+
+    lax.fori_loop(0, ranks, pack, 0)
+    column = flat_ref[...].T
+    per = width // (groups * ranks)
+    for g2 in range(groups):
+        for f2 in range(ranks):
+            base = (g2 * ranks + f2) * per
+            pieces = [column[base + 8 * i : base + 8 * i + 8, :] for i in range(per // 8)]
+            p_ref[g2, f2, head_rows : head_rows + 8, :] = jnp.concatenate(
+                pieces, axis=1
+            ).astype(BF16)
+
+    def add(ref, other):
+        ref[...] = (ref[...].astype(F32) + other[...].astype(F32)).astype(BF16)
+
+    c = lax.rem(at.g, 2)
+    x = lax.rem(at.g // 2, 2)
+    y = at.hi
+
+    def block(y2, x2, c2):
+        return (y2 * 2 + x2) * 2 + c2
+
+    half = ranks // 2
+    quads = [(1 - y, 1 - x), (y, 1 - x), (1 - y, x), (y, x)]
+    for i, (y2, x2) in enumerate(quads):
+        spot = y2 * 2 + x2
+        send(p_ref.at[block(y2, x2, 1 - c)], r1_ref.at[spot], s1.at[i], e1.at[spot], core)
+    settle(mr_ref.at[0], me.at[0])
+    mx_ref[1] = mx_ref[0] + mr_ref[0]
+    send(mx_ref.at[1], mr_ref.at[1], ms.at[1], me.at[1], side)
+    for i, (y2, x2) in enumerate(quads):
+        spot = y2 * 2 + x2
+        settle(r1_ref.at[spot], e1.at[spot])
+        add(p_ref.at[block(y2, x2, c)], r1_ref.at[spot])
+        if i == 0:
+            here = p_ref.at[block(1 - y, 1 - x, c)]
+            send(here.at[0:half], r2_ref.at[0, 1 - y], s2.at[0, 0], e2.at[0, 1 - y], side)
+            send(here.at[half:], r2_ref.at[1, 1 - x], s2.at[1, 0], e2.at[1, 1 - x], upper)
+        if i == 1:
+            here = p_ref.at[block(y, 1 - x, c)]
+            send(here.at[0:half], r2_ref.at[0, y], s2.at[0, 1], e2.at[0, y], side)
+        if i == 2:
+            here = p_ref.at[block(1 - y, x, c)]
+            send(here.at[half:], r2_ref.at[1, x], s2.at[1, 1], e2.at[1, x], upper)
+    settle(mr_ref.at[1], me.at[1])
+    mx_ref[2] = mx_ref[1] + mr_ref[1]
+    send(mx_ref.at[2], mr_ref.at[2], ms.at[2], me.at[2], upper)
+    settle(r2_ref.at[0, 1 - y], e2.at[0, 1 - y])
+    add(p_ref.at[block(1 - y, x, c), 0:half], r2_ref.at[0, 1 - y])
+    send(
+        p_ref.at[block(1 - y, x, c), 0:half], r3_ref.at[0], s3.at[0], e3.at[0], upper
+    )
+    settle(r2_ref.at[1, 1 - x], e2.at[1, 1 - x])
+    add(p_ref.at[block(y, 1 - x, c), half:], r2_ref.at[1, 1 - x])
+    send(p_ref.at[block(y, 1 - x, c), half:], r3_ref.at[1], s3.at[1], e3.at[1], side)
+    settle(r2_ref.at[0, y], e2.at[0, y])
+    add(p_ref.at[at.g, 0:half], r2_ref.at[0, y])
+    settle(r2_ref.at[1, x], e2.at[1, x])
+    add(p_ref.at[at.g, half:], r2_ref.at[1, x])
+    settle(mr_ref.at[2], me.at[2])
+    mx_ref[3] = mx_ref[2] + mr_ref[2]
+    mz_ref[at.f] = mx_ref[3]
+    for i in range(2):
+        settle(r3_ref.at[i], e3.at[i])
+        add(p_ref.at[at.g, i * half : (i + 1) * half], r3_ref.at[i])
+    for j in range(1, ranks):
+        f2 = xor4(at.f, j)
+        send(p_ref.at[at.g, f2], r4_ref.at[at.f], s4.at[j], e4.at[at.f], (at.g, f2))
+        send(mx_ref.at[3], mz_ref.at[at.f], zs.at[j], ze.at[at.f], (at.g, f2))
+    total = p_ref[at.g, at.f].astype(F32)
+    for j in range(1, ranks):
+        f2 = xor4(at.f, j)
+        settle(r4_ref.at[f2], e4.at[f2])
+        total = total + r4_ref[f2].astype(F32)
+        settle(mz_ref.at[f2], ze.at[f2])
+    fin_ref[...] = total
+    gmix_ref[...] = (mz_ref[0] + mz_ref[1]) + (mz_ref[2] + mz_ref[3])
+
+    for m in range(E):
+        for w in range(3):
+            settle(t_ref.at[m, w], tr.at[m, w])
+    for i in range(1, E):
+        for w in range(3):
+            settle(t_ref.at[0, w], ts.at[i, w])
+
+    @pl.when(at.f > 0)
+    def _():
+        settle(dhalo_ref, hs)
+
+    @pl.when(at.f < ranks - 1)
+    def _():
+        settle(back_ref, hr)
+
+    for i in range(4):
+        settle(r1_ref.at[0], s1.at[i])
+    for i in range(2):
+        for n2 in range(2):
+            settle(r2_ref.at[0, 0], s2.at[i, n2])
+        settle(r3_ref.at[0], s3.at[i])
+    for i in range(3):
+        settle(mr_ref.at[0], ms.at[i])
+    for j in range(1, ranks):
+        settle(r4_ref.at[0], s4.at[j])
+        settle(mz_ref.at[0], zs.at[j])
+
+
+def end(groups, ranks, tile, *args):
+    cot = args[0]
+    width = cot.shape[1]
+    dma = pltpu.SemaphoreType.DMA
+    vm = pltpu.VMEM
+    block = (width // ranks + 8, 4 * (width // groups))
+    half = ranks // 2
     return pl.pallas_call(
-        backward_kernel,
+        end_kernel,
         out_shape=[
-            sds((4, width, width), BF16),
+            sds((TOK_DEV, width), BF16),
+            sds((TOK_DEV, width), F32),
+            sds((TOK_DEV, 128), F32),
             sds((TOK_DEV, width), F32),
             sds((HALO, width), BF16),
-            sds((8, width), F32),
+            sds((E, 3) + tile, BF16),
+            sds(block, F32),
+            sds((16, 128), F32),
         ],
-        in_specs=whole(14),
-        out_specs=whole(4),
+        in_specs=whole(25),
+        out_specs=whole(8),
         scratch_shapes=[
-            pltpu.VMEM((TOK_DEV, width), BF16),
-            pltpu.VMEM((TOK_DEV, width), F32),
-            pltpu.VMEM((KEYS, width), F32),
-            pltpu.VMEM((KEYS, width), F32),
-            pltpu.VMEM((TOK_DEV, width), BF16),
-            pltpu.VMEM((KEYS, width), BF16),
-            pltpu.VMEM((KEYS, width), BF16),
+            vm((128, width), F32),
+            vm((HALO, width), BF16),
+            vm((TOK_DEV, width), BF16),
+            vm((TOK_DEV, width), F32),
+            vm((KEYS, width), F32),
+            vm((KEYS, width), F32),
+            vm((TOK_DEV, width), BF16),
+            vm((KEYS, width), BF16),
+            vm((KEYS, width), BF16),
+            vm((4, width, width), BF16),
+            vm((groups, ranks) + block, BF16),
+            vm((4, ranks) + block, BF16),
+            vm((2, 2, half) + block, BF16),
+            vm((2, half) + block, BF16),
+            vm((ranks,) + block, BF16),
+            vm((4, 16, 128), F32),
+            vm((3, 16, 128), F32),
+            vm((ranks, 16, 128), F32),
+            dma((E, 3)),
+            dma((E, 3)),
+            dma,
+            dma,
+            dma((4,)),
+            dma((4,)),
+            dma((2, 2)),
+            dma((2, 2)),
+            dma((2,)),
+            dma((2,)),
+            dma((4,)),
+            dma((4,)),
+            dma((3,)),
+            dma((3,)),
+            dma((4,)),
+            dma((4,)),
         ],
-        compiler_params=params(60),
-        name="backward",
-    )(dres, wf, q, k, v, n1, inv1, mix, lse, cos, sin, pos, tok, halo)
-
-
-def finish_kernel(dres_ref, down_ref, back_ref, tok_ref, inv1_ref, s_ref, out_ref):
+        compiler_params=params(63, collective_id=3, has_side_effects=True),
+        name="end",
+    )(*args)
+
+
+def store_kernel(
+    t_ref,
+    fin_ref,
+    dres_ref,
+    down_ref,
+    back_ref,
+    tok_ref,
+    inv1_ref,
+    gate_ref,
+    up_ref,
+    downw_ref,
+    gq_ref,
+    gk_ref,
+    gv_ref,
+    go_ref,
+    small_ref,
+    gtok_ref,
+):
+    for e in range(E):
+        gate_ref[e] = t_ref[e, 0].astype(F32)
+        up_ref[e] = t_ref[e, 1].astype(F32)
+        downw_ref[e] = t_ref[e, 2].astype(F32).T
+    head_rows, part_cols = gq_ref.shape
+    for w, ref in enumerate((gq_ref, gk_ref, gv_ref, go_ref)):
+        ref[...] = fin_ref[0:head_rows, w * part_cols : (w + 1) * part_cols]
+    for i in range(small_ref.shape[0] // 8):
+        small_ref[8 * i : 8 * i + 8, :] = fin_ref[
+            head_rows : head_rows + 8, 128 * i : 128 * i + 128
+        ]
     width = tok_ref.shape[1]
     inv1 = inv1_ref[HALO:, 0:1]
     unit = tok_ref[...].astype(F32) * inv1
-    back = jnp.concatenate(
-        [jnp.zeros((TOK_DEV - HALO, width), F32), back_ref[...].astype(F32)], axis=0
-    )
-    g1 = s_ref[...].T[SMALL_G1 : SMALL_G1 + 1, :]
-    m = (down_ref[...] + back) * g1
+    m = jnp.concatenate(
+        [down_ref[: TOK_DEV - HALO, :], down_ref[TOK_DEV - HALO :, :] + back_ref[...]], axis=0
+    )
     d_dealt = inv1 * (m - unit * jnp.mean(m * unit, axis=1, keepdims=True))
-    out_ref[...] = dres_ref[...] + d_dealt.astype(BF16).astype(F32)
-
-
-def finish(dres, down, back, tok, inv1, small):
-    return pl.pallas_call(
-        finish_kernel,
-        out_shape=sds(dres.shape, F32),
-        in_specs=whole(6),
-        out_specs=pl.BlockSpec(memory_space=pltpu.VMEM),
-        compiler_params=params(40),
-        name="finish",
-    )(dres, down, back, tok, inv1, small)
-
-
-def store_kernel(own_ref, *refs):
-    t_refs = refs[:E]
-    gate_ref, up_ref, down_ref = refs[E:]
-    own = own_ref[0]
-    for k in range(E):
-        expert = lax.rem(own + k, E)
-        gate_ref[expert] = t_refs[k][0].astype(F32)
-        up_ref[expert] = t_refs[k][1].astype(F32)
-        down_ref[expert] = t_refs[k][2].astype(F32).T
-
-
-def store(own, tiles):
-    rows, cols = tiles[0].shape[1:]
+    gtok_ref[...] = dres_ref[...] + d_dealt.astype(BF16).astype(F32)
+
+
+def store(t, fin, dres, down, back, tok, inv1, groups, ranks):
+    width = tok.shape[1]
+    rows, cols = t.shape[2:]
+    per = width // (groups * ranks)
     return pl.pallas_call(
         store_kernel,
-        out_shape=[sds((E, rows, cols), F32)] * 2 + [sds((E, cols, rows), F32)],
-        in_specs=[pl.BlockSpec(memory_space=pltpu.SMEM)] + whole(E),
-        out_specs=whole(3),
-        compiler_params=params(40),
+        out_shape=[sds((E, rows, cols), F32)] * 2
+        + [sds((E, cols, rows), F32)]
+        + [sds((width // ranks, width // groups), F32)] * 4
+        + [sds((per, 128), F32), sds(tok.shape, F32)],
+        in_specs=whole(7),
+        out_specs=whole(9),
+        compiler_params=params(48),
         name="store",
-    )(own, *tiles)
+    )(t, fin, dres, down, back, tok, inv1)
 
 
 def fast_device(
@@ -1655,13 +1854,8 @@
 ):
     groups = lax.axis_size("grp")
     ranks = lax.axis_size("fsdp")
-    his = E // ranks
-    lo = groups // his
-    g_id = lax.axis_index("grp")
     f_id = lax.axis_index("fsdp")
     width = tokens.shape[1]
-    axes = ("grp", "fsdp")
-    own = (f_id * his + g_id // lo).astype(jnp.int32).reshape(1)
     per = gain_one.shape[0]
 
     small = jnp.concatenate(
@@ -1683,8 +1877,8 @@
     cos = jnp.concatenate([cos] * 4, axis=1)
     sin = jnp.concatenate([-sin, sin, -sin, sin], axis=1)
     pos_own = jnp.broadcast_to(pos[HALO:, None], (TOK_DEV, 128))
-    mixed_prev = exact_dot(prev_logits, w_mix.astype(F32))
-    mixed_prev = jnp.pad(mixed_prev, ((0, 0), (0, 128 - EXPERTS_ALL)))
+    prev = jnp.pad(prev_logits, ((0, 0), (0, 128 - EXPERTS_ALL)))
+    wmix = jnp.pad(w_mix, ((0, 128 - EXPERTS_ALL), (0, 128 - EXPERTS_ALL)))
 
     outs = begin(
         tile,
@@ -1694,7 +1888,8 @@
         cos,
         sin,
         pos_own,
-        mixed_prev,
+        prev,
+        wmix,
         w_down,
         w_gate,
         w_up,
@@ -1703,69 +1898,54 @@
     )
     wf, small, halo, slots, q, k, v, n1, inv1, mix, lse, resid, part, probs, cols = outs[:15]
     x, gates, w_all, g_all = outs[15:]
-    done = moe(x, gates, w_all, g_all, w_gate.shape[1:])
-    od_back, g_tiles = done[0], done[1:]
-    output, d_resid, dl, dw, dv, dg2 = combine(
-        cotangent, resid, part, probs, cols, slots, routes, small, od_back
-    )
-    d_logits = dl[:, :EXPERTS_ALL]
-    grad_prev = exact_dot(d_logits, w_mix.astype(F32).T)
-    d_mix = exact_dot(prev_logits.T, d_logits)
-    gw, down, d_halo, dg1 = backward(
-        d_resid, wf, q, k, v, n1, inv1, mix, lse, cos, sin, pos_own, tokens, halo
-    )
-    back = lax.ppermute(d_halo, "fsdp", [(f + 1, f) for f in range(ranks - 1)])
-    grad_tokens = finish(d_resid, down, back, tokens, inv1, small)
-
-    def back_perm(k):
-        pairs = []
-        for g in range(groups):
-            for f in range(ranks):
-                m = (f * his + g // lo + k) % E
-                pairs.append(((m % his * lo + g % lo) * ranks + m // his, g * ranks + f))
-        return pairs
-
-    tiles_back = [
-        g_tiles[i] if i == 0 else lax.ppermute(g_tiles[i], axes, back_perm(i)) for i in range(E)
-    ]
-    grad_gate, grad_up, grad_down = store(own, tiles_back)
-
-    cols_per = width // groups
-    rows_per = width // ranks
-    gw = gw.reshape(4, width, groups, cols_per).transpose(2, 0, 1, 3)
-    gw = lax.psum_scatter(gw, "grp", scatter_dimension=0, tiled=False)
-    gw = gw.reshape(4, ranks, rows_per, cols_per).transpose(1, 0, 2, 3)
-    gw = lax.psum_scatter(gw, "fsdp", scatter_dimension=0, tiled=False).astype(F32)
-    tiny = jnp.concatenate(
-        [
-            dg1[:1],
-            dg2[:1],
-            dv[:CONSTS],
-            dw[:EXPERTS_ALL],
-            dw[SMALL_C : SMALL_C + 2 * CONSTS],
-            jnp.pad(d_mix.reshape(1, -1), ((0, 0), (0, width - EXPERTS_ALL * EXPERTS_ALL))),
-        ],
-        axis=0,
-    )
-    tiny = lax.psum(tiny, axes)
-    grad_mix = tiny[-1, : EXPERTS_ALL * EXPERTS_ALL].reshape(EXPERTS_ALL, EXPERTS_ALL)
-    first = (g_id * ranks + f_id) * per
-    mine = lax.dynamic_slice(tiny, (0, first), (tiny.shape[0], per))
-    n_small = 2 + CONSTS
+    od_back, gw = moe(x, gates, w_all, g_all)
+    output, dres, gprev, down, back, tiles, fin, gmix = end(
+        groups,
+        ranks,
+        w_gate.shape[1:],
+        cotangent,
+        resid,
+        part,
+        probs,
+        cols,
+        slots,
+        routes,
+        prev,
+        wmix,
+        small,
+        od_back,
+        gw,
+        wf,
+        q,
+        k,
+        v,
+        n1,
+        inv1,
+        mix,
+        lse,
+        cos,
+        sin,
+        pos_own,
+        tokens,
+        halo,
+    )
+    grad_gate, grad_up, grad_down, gq, gk, gv, go, tiny, grad_tokens = store(
+        tiles, fin, dres, down, back, tokens, inv1, groups, ranks
+    )
     return (
         output,
         grad_tokens,
-        grad_prev,
-        mine[0],
-        gw[0],
-        gw[1],
-        gw[2],
-        gw[3],
-        mine[1],
-        mine[n_small : n_small + EXPERTS_ALL].T,
-        grad_mix,
-        mine[n_small + EXPERTS_ALL : n_small + EXPERTS_ALL + 2 * CONSTS].T,
-        mine[2:n_small].T,
+        gprev[:, :EXPERTS_ALL],
+        tiny[:, SMALL_G1],
+        gq,
+        gk,
+        gv,
+        go,
+        tiny[:, SMALL_G1 + 1],
+        tiny[:, :EXPERTS_ALL],
+        gmix[:EXPERTS_ALL, :EXPERTS_ALL],
+        tiny[:, SMALL_C : SMALL_C + 2 * CONSTS],
+        tiny[:, SMALL_VC : SMALL_VC + CONSTS],
         grad_gate,
         grad_up,
         grad_down,

time: 536 us -> 365 us (0.68)
  waiting for transfers between devices: 116 us -> 0 us
  blocking collectives: 63.7 us -> 0 us
  Pallas kernels: 277 us -> 336 us
  local copies, waits for them, and re-layouts: 41.3 us -> 22.2 us
  starting transfers between devices: 13.7 us -> 0 us
  between operations: 14.3 us -> 0.76 us
    unnamed x3 -> x0, waiting for transfers between devices: 94.7 us -> none
    psum x1 -> x0, blocking collectives: 63.7 us -> none  [fast_device(): tiny = lax.psum(tiny, axes)]
    pallas_call x4 -> x2, Pallas kernels: 173 us -> 232 us  [the longest x1 136 us: moe(): pl.pallas_call(moe_kernel, out_shape=[sds((E, MOST, 2 * width), BF16), sd...]
    ppermute x8 -> x0, waiting for transfers between devices: 21.4 us -> none  [the longest x7 21.4 us: fast_device(): lax.ppermute(g_tiles[i], axes, back_perm(i))]
    ppermute x8 -> x0, starting transfers between devices: 13.4 us -> none  [the longest x7 12.1 us: fast_device(): lax.ppermute(g_tiles[i], axes, back_perm(i))]
    pallas_call x1 -> x0, local copies, waits for them, and re-layouts: 6.66 us -> none  [backward(): pl.pallas_call(backward_kernel, out_shape=[sds((4, width, width), BF16),...]
    slice x6 -> x3, local copies, waits for them, and re-layouts: 6.84 us -> 0.84 us  [the longest x1 0.7 us: fast_device(): tiny[:, SMALL_G1 + 1]]
    transpose x4 -> x0, local copies, waits for them, and re-layouts: 5.42 us -> none  [the longest x1 1.41 us: fast_device(): mine[n_small:n_small + EXPERTS_ALL]]
  transfers between devices with their start and end apart: 10 -> 0, of which waited for: 2 -> 0; matrix products, arithmetic and copies ran while one was open for 4% -> 0% of each run, Pallas kernels for 1% -> 0%
where the time goes in v3:
time: 365 us; the launch traced here: 364 us
  Pallas kernels  336 us (92%)
  local copies, waits for them, and re-layouts  22.2 us (6%)
  other arithmetic  5.06 us (1%)
    pallas_call x1, Pallas kernels, moe(): pl.pallas_call(moe_kernel, out_shape=[sds((E, MOST, 2 * width), BF16), sd...  136 us
    pallas_call x1, Pallas kernels, begin(): pl.pallas_call(begin_kernel, out_shape=[sds((4, width, width), BF16), sds...  100 us
    pallas_call x1, Pallas kernels, end(): pl.pallas_call(end_kernel, out_shape=[sds((TOK_DEV, width), BF16), sds((T...  95.9 us
    unnamed x31, local copies, waits for them, and re-layouts  17 us

profile of v3, /device:TPU:0, one launch (start us, length us, event | category | flops | bytes accessed | tf_op | source)
XLA Modules:
  0.0 364.3 jit_solution(2412404494479643702)
XLA Ops:
  0.7 0.8 select_reduce_fusion.1
  1.6 0.7 copy.73
  2.4 0.7 copy.74
  3.1 0.8 copy.72
  3.9 0.8 copy.76
  5.5 1.3 pad.14.wmix_ref
  6.9 1.7 pad_maximum_fusion.2.tile_ref
  8.5 0.8 broadcast_in_dim.49.pos_ref
  9.3 1.5 copy.79.routes_ref
  10.8 0.8 copy.78
  12.3 1.1 fusion
  13.4 1.3 pad_maximum_fusion
  14.8 1.3 copy.80.wd_ref
  16.1 100.3 %begin.1 = (bf16[4,768,768]{2,1,0:T(8,128)(2,1)}, f32[768,128]{1,0:T(8,128)}, bf16[256,768]{1,0:T(8,128)(2,1)}, s32[320,128]{1,0:T(8,128)}, bf16[320,768]{1,0:T(...) custom-call(bf16[200,384]{1,0:T(8,128)(2,1)} %pad_maximum_fusion.2.t, ...), custom_call_target="tpu_custom_call" | custom-call | tf_op jit(solution)/shard_map/begin/pallas_call | solution.py:1075
  116.3 135.7 %moe.1 = (bf16[8,80,1536]{2,1,0:T(8,128)(2,1)}, bf16[3,768,512]{2,1,0:T(8,128)(2,1)}) custom-call(bf16[640,768]{1,0:T(8,128)(2,1)} %get-tuple-element.60.x_ref, f32[8,8,128]{2,1,0:T(8,128)} %get-tuple-element.61.gates_ref, bf16[3,768,512]{2,1,0:T(8,128)(2,1)} %get-tuple-element.62.w_ref, bf16[4,4,160,768]{3,2,1,0:T(8,128)(2,1)} %get-tuple-element.63.g_ref), custom_call_target="tpu_custom_call" | custom-call | tf_op jit(solution)/shard_map/moe/pallas_call | solution.py:1322
  252.0 95.9 %end.1 = (bf16[320,768]{1,0:T(8,128)(2,1)}, f32[320,768]{1,0:T(8,128)}, f32[320,128]{1,0:T(8,128)}, f32[320,768]{1,0:T(8,128)}, bf16[256,768]{1,0:T(8,128)(2,1)}...) custom-call(bf16[320,768]{1,0:T(8,128)(2,1)} %cot_ref.3, ...), custom_call_target="tpu_custom_call" | custom-call | tf_op jit(solution)/shard_map/end/pallas_call | solution.py:1723
  347.9 1.6 copy.82
  349.5 1.2 copy-done.2
  350.7 1.2 copy-done.3
  351.9 1.0 copy-done.4
  352.9 1.0 copy-done.5
  353.9 4.5 %store.1 = (f32[8,192,256]{2,1,0:T(8,128)}, f32[8,192,256]{2,1,0:T(8,128)}, f32[8,256,192]{2,1,0:T(8,128)S(1)}, f32[192,96]{1,0:T(8,128)}, f32[192,96]{1,0:T(8,1...) custom-call(bf16[8,3,192,256]{3,2,1,0:T(8,128)(2,1)} %get-tuple-element.76.t_ref, ...), custom_call_target="tpu_custom_call" | custom-call | tf_op jit(solution)/shard_map/store/pallas_call | solution.py:1821
  361.2 1.7 copy.86
  362.9 0.8 copy.89
  (30 shorter events, 5.1 us)
Async XLA Ops:
  0.6 14.1 %copy-start.6 = (bf16[8,256,192]{1,2,0:T(8,128)(2,1)S(1)}, bf16[8,256,192]{1,2,0:T(8,128)(2,1)}, u32[]{:S(2)}) copy-start(bf16[8,256,192]{1,2,0:T(8,128)(2,1)} %param.36) | copy-start | bytes 2359300
  252.0 97.5 %copy-start = (bf16[320,768]{1,0:T(8,128)(2,1)S(1)}, bf16[320,768]{1,0:T(8,128)(2,1)}, u32[]{:S(2)}) copy-start(bf16[320,768]{1,0:T(8,128)(2,1)} %tok_ref.5) | copy-start | bytes 1474564
  252.0 97.5 %copy-start.1 = (f32[576,128]{1,0:T(8,128)S(1)}, f32[576,128]{1,0:T(8,128)}, u32[]{:S(2)}) copy-start(f32[576,128]{1,0:T(8,128)} %get-tuple-element.71.inv1_ref) | copy-start | bytes 884740
  349.5 1.2 copy-start.2
  350.7 1.2 copy-start.3
  351.9 1.0 copy-start.4
  352.9 1.0 copy-start.5
  358.4 4.5 %copy-start.7 = (bf16[320,768]{1,0:T(8,128)(2,1)S(1)}, bf16[320,768]{1,0:T(8,128)(2,1)}, u32[]{:S(2)}) copy-start(bf16[320,768]{1,0:T(8,128)(2,1)} %get-tuple-element.181) | copy-start | bytes 1474564
  359.8 3.9 %copy-start.8 = (f32[16,128]{1,0:T(8,128)S(1)}, f32[16,128]{1,0:T(8,128)}, u32[]{:S(2)}) copy-start(f32[16,128]{1,0:T(8,128)} %get-tuple-element.88) | copy-start | bytes 24580

commit v4 on v3

--- a/solution.py
+++ b/solution.py
@@ -597,7 +597,6 @@
 HALO = 256
 KEYS = HALO + TOK_DEV
 ROWS = E * MOST
-WIDE = 896
 NEG = -1e30
 F32 = jnp.float32
 BF16 = jnp.bfloat16
@@ -690,11 +689,14 @@
         return peers
 
 
-def greet(peers):
+def call(peers):
     barrier = pltpu.get_barrier_semaphore()
     for peer in peers:
         pl.semaphore_signal(barrier, inc=1, device_id=peer, device_id_type=MESH_ID)
-    pl.semaphore_wait(barrier, len(peers))
+
+
+def answer(peers):
+    pl.semaphore_wait(pltpu.get_barrier_semaphore(), len(peers))
 
 
 def turn(values, cos, sin):
@@ -713,75 +715,173 @@
 QBLOCKS = [(0, 128), (128, 128), (256, 64)]
 
 
-def allowed_mask(pos_ref, first, count):
+def allowed_mask(pos_ref, first, count, lane):
     ii = lax.broadcasted_iota(jnp.int32, (count, 384), 0) + HALO
     jj = lax.broadcasted_iota(jnp.int32, (count, 384), 1)
-    return (jj <= ii) & (jj >= ii - pos_ref[pl.ds(first, count), 0:1])
+    pos = pos_ref[pl.ds(first, count), lane : lane + 1].astype(jnp.int32)
+    return (jj <= ii) & (jj >= ii - pos)
 
 
 def key_span(first):
     return min(384, KEYS - first)
 
 
-def begin_kernel(
-    tile_ref,
+KEPT = (
+    ("wf", (4, None, None), BF16),
+    ("s", (None, 128), F32),
+    ("halo", (HALO, None), BF16),
+    ("q", (TOK_DEV, None), BF16),
+    ("k", (KEYS, None), BF16),
+    ("v", (KEYS, None), BF16),
+    ("n1", (KEYS, None), BF16),
+    ("inv1", (KEYS, 128), F32),
+    ("mix", (TOK_DEV, None), BF16),
+    ("lse", (TOK_DEV, 128), F32),
+    ("resid", (TOK_DEV, None), F32),
+    ("part", (TOK_DEV, None), F32),
+    ("probs", (TOK_DEV, 128), F32),
+    ("cols", (TOK_DEV, 128), F32),
+    ("cos", (KEYS, 128), F32),
+    ("sin", (KEYS, 128), F32),
+)
+
+
+def kept_shape(dims, width):
+    return tuple(width if d is None else d for d in dims)
+
+
+def by_name(refs):
+    return {name: ref for (name, _, _), ref in zip(KEPT, refs)}
+
+
+def token_places(len_ref, at):
+    row = lax.broadcasted_iota(jnp.int32, (KEYS, 128), 0) + (at.f * TOK_DEV - HALO)
+    first = jnp.zeros((KEYS, 128), jnp.int32)
+    reached = jnp.int32(0)
+    for i in range(len_ref.shape[1]):
+        reached = reached + len_ref[0, i]
+        first = jnp.where(row >= reached, reached, first)
+    return jnp.maximum(row - first, 0)
+
+
+def ahead_kernel(
+    len_ref,
+    routes_ref,
+    prev_ref,
+    wmix_ref,
+    router_ref,
+    gain1_ref,
+    gain2_ref,
+    const_ref,
+    vconst_ref,
+    wq_ref,
+    wk_ref,
+    wv_ref,
+    wo_ref,
     tok_ref,
     cot_ref,
-    routes_ref,
-    cos_ref,
-    sin_ref,
-    pos_ref,
-    prev_ref,
-    wmix_ref,
-    wd_ref,
     wg_hbm,
     wu_hbm,
-    wf_ref,
-    s_ref,
-    halo_ref,
-    slots_ref,
-    q_ref,
-    k_ref,
-    v_ref,
-    n1_ref,
-    inv1_ref,
-    mix_ref,
-    lse_ref,
-    resid_ref,
-    part_ref,
-    probs_ref,
-    cols_ref,
-    x_ref,
-    gates_ref,
-    w_hbm,
-    g_hbm,
-    p_ref,
-    wdt_ref,
-    grow_ref,
-    zs,
-    ps,
-    cs,
-    hs,
-    gs,
-    ws,
-    gas,
-    agr,
-    hr,
-    gr,
-    wr,
-    gqr,
+    wd_hbm,
+    *rest,
 ):
-    lo, ranks = g_hbm.shape[:2]
+    n = len(KEPT)
+    kept_hbm = by_name(rest[:n])
+    op_hbm, gw_hbm, back_hbm, dgb_hbm = rest[n : n + 4]
+    kept = by_name(rest[n + 4 : 2 * n + 4])
+    (
+        tile_ref,
+        small_ref,
+        p_ref,
+        grow_ref,
+        x_ref,
+        gates_ref,
+        w_ref,
+        g_ref,
+        xb_ref,
+        gb_ref,
+        od_ref,
+        op_ref,
+        r1_ref,
+        r2_ref,
+        dgp_ref,
+        dr1_ref,
+        dr2_ref,
+        acc_ref,
+        gw_ref,
+        back_ref,
+        dgb_ref,
+        keep_sem,
+        last_sem,
+        zs,
+        ps,
+        cs,
+        hs,
+        gs,
+        ws,
+        gas,
+        agr,
+        hr,
+        gr,
+        wr,
+        gqr,
+        xs,
+        ts,
+        qs,
+        tqs,
+        d1s,
+        t1s,
+        d2s,
+        t2s,
+        bs,
+        tbs,
+        xr,
+        tr,
+        qr,
+        tqr,
+        d1r,
+        t1r,
+        d2r,
+        t2r,
+        br,
+        tbr,
+    ) = rest[2 * n + 4 :]
+    wf_ref, s_ref, halo_ref = kept["wf"], kept["s"], kept["halo"]
+    q_ref, k_ref, v_ref, n1_ref = kept["q"], kept["k"], kept["v"], kept["n1"]
+    mix_ref, lse_ref = kept["mix"], kept["lse"]
+    lo, ranks = g_ref.shape[:2]
     his = E // ranks
     at = Place(his, lo)
     width = tok_ref.shape[1]
-    head_rows = wd_ref.shape[2]
-    ff = wd_ref.shape[1]
-    part_cols = width // p_ref.shape[0]
+    head_rows, part_cols = wq_ref.shape
+    ff = wg_hbm.shape[2]
     diag = lo * (1 - at.hi) + at.l2
     upper = lo * (1 - at.hi) + at.l
     near = [(at.core_peer, at.f), (at.side_peer, at.f), (upper, at.f), (diag, at.f)]
-    greet(at.others() + [near[0], near[1], near[3]])
+    core, side = near[0], near[1]
+    peers = at.others() + [near[0], near[1], near[3]]
+    call(peers)
+
+    def keep(*names):
+        for name in names:
+            i = [k[0] for k in KEPT].index(name)
+            pltpu.make_async_copy(kept[name], kept_hbm[name], keep_sem.at[i]).start()
+
+    tile_ref[0:head_rows, :] = jnp.concatenate(
+        [wq_ref[...], wk_ref[...], wv_ref[...], wo_ref[...]], axis=1
+    )
+    small_ref[...] = jnp.zeros_like(small_ref)
+    per = router_ref.shape[1]
+    small_ref[0:EXPERTS_ALL, 0:per] = router_ref[...].astype(F32)
+    small_ref[SMALL_G1 : SMALL_G1 + 1, 0:per] = gain1_ref[...].astype(F32)
+    small_ref[SMALL_G1 + 1 : SMALL_G1 + 2, 0:per] = gain2_ref[...].astype(F32)
+    small_ref[SMALL_VC : SMALL_VC + CONSTS, 0:per] = vconst_ref[...].astype(F32)
+    small_ref[SMALL_C : SMALL_C + 2 * CONSTS, 0:per] = const_ref[...].astype(F32)
+    turned = small_ref[...].T
+    tile_ref[head_rows : head_rows + 8, :] = jnp.concatenate(
+        [turned[8 * i : 8 * i + 8, :] for i in range(per // 8)], axis=1
+    ).astype(BF16)
+    answer(peers)
 
     p_ref[at.g, at.f] = tile_ref[...]
     for j in range(1, ranks):
@@ -805,8 +905,15 @@
         halo_ref[...] = jnp.zeros_like(halo_ref)
 
     lanes = lane_iota(TOK_DEV)
-    r0 = routes_ref[:, 0:1]
-    r1 = routes_ref[:, 1:2]
+    routes = jnp.concatenate(
+        [
+            jnp.broadcast_to(routes_ref[0:1, :], (8, TOK_DEV)),
+            jnp.broadcast_to(routes_ref[1:2, :], (8, TOK_DEV)),
+        ],
+        axis=0,
+    ).T
+    r0 = routes[:, 0:1]
+    r1 = routes[:, 8:9]
     hot0 = lanes == r0
     hot1 = lanes == r1
     named = jnp.where(hot0 | hot1, 1.0, 0.0).astype(BF16)
@@ -819,13 +926,10 @@
     rank1 = pick(rank, hot1).astype(jnp.int32)
     c0 = jnp.where(r0 < E, r0 * MOST + rank0, -1)
     c1 = jnp.where(r1 < E, r1 * MOST + rank1, -1)
-    slots_ref[...] = jnp.where(lanes == 0, c0, jnp.where(lanes == 1, c1, -1))
     slot = lane_iota(TOK_DEV, ROWS)
     spots0 = jnp.where(slot == c0, 1.0, 0.0).astype(BF16)
     spots1 = jnp.where(slot == c1, 1.0, 0.0).astype(BF16)
     grow_ref[...] = mm(spots0 + spots1, cot_ref[...], TN).astype(BF16)
-    for e in range(E):
-        wdt_ref[e] = wd_ref[e].T
 
     for j in range(1, ranks):
         f2 = xor4(at.f, j)
@@ -839,13 +943,13 @@
         for hh in range(his):
             e, peer = at.member(j, hh)
             rows = grow_ref.at[pl.ds(aligned(e * MOST, 16), MOST)]
-            spot = g_hbm.at[at.l, at.f, own_spot]
-            sources = (wg_hbm.at[e], wu_hbm.at[e], wdt_ref.at[e])
+            spot = g_ref.at[at.l, at.f, own_spot]
+            sources = (wg_hbm.at[e], wu_hbm.at[e], wd_hbm.at[e])
             if j == 0 and hh == 0:
                 pltpu.make_async_copy(rows, spot, gr.at[at.m]).start()
                 for w in range(3):
                     pltpu.make_async_copy(
-                        sources[w], w_hbm.at[w, own_rows, own_cols], wr.at[at.m, w]
+                        sources[w], w_ref.at[w, own_rows, own_cols], wr.at[at.m, w]
                     ).start()
             else:
                 k = j * his + hh
@@ -853,11 +957,24 @@
                 for w in range(3):
                     send(
                         sources[w],
-                        w_hbm.at[w, own_rows, own_cols],
+                        w_ref.at[w, own_rows, own_cols],
                         ws.at[k, w],
                         wr.at[at.m, w],
                         peer,
                     )
+
+    pos = token_places(len_ref, at).astype(F32)
+    half_dim = HEAD_DIM // 2
+    lane_k = lane_iota(KEYS)
+    freq = jnp.exp(
+        lax.rem(lane_k, half_dim).astype(F32) * (-2.0 * math.log(10000.0) / HEAD_DIM)
+    )
+    kept["cos"][...] = jnp.cos(pos * freq)
+    sine = jnp.sin(pos * freq)
+    kept["sin"][...] = jnp.where(lax.rem(lane_k, HEAD_DIM) < half_dim, -sine, sine)
+    pos_own = pos[HALO:]
+    pos_ref = kept["cols"]
+    pos_ref[...] = pos_own
 
     for j in range(ranks):
         f2 = xor4(at.f, j)
@@ -876,7 +993,6 @@
         ):
             settle(p_ref.at[g2, f2], agr.at[g2, f2])
 
-    per = (p_ref.shape[2] - head_rows) // 8 * 24
     groups = p_ref.shape[0]
     for g2 in range(groups):
         for f2 in range(ranks):
@@ -914,15 +1030,16 @@
     g1 = flat[SMALL_G1 : SMALL_G1 + 1, :]
     g2 = flat[SMALL_G1 + 1 : SMALL_G1 + 2, :]
     vc = flat[SMALL_VC : SMALL_VC + CONSTS, :]
+    keep("wf", "s", "halo")
     rows = jnp.concatenate([halo_ref[...], tok_ref[...]], axis=0).astype(F32)
     inv1 = lax.rsqrt(jnp.mean(rows * rows, axis=1, keepdims=True) + NORM_EPS)
-    inv1_ref[...] = jnp.broadcast_to(inv1, (KEYS, 128))
+    kept["inv1"][...] = jnp.broadcast_to(inv1, (KEYS, 128))
     n1_ref[...] = (rows * inv1 * g1).astype(BF16)
 
     def project(i, _):
         span = pl.ds(pl.multiple_of(i * 256, 256), 256)
-        cos = cos_ref[...]
-        sin = sin_ref[...]
+        cos = kept["cos"][...]
+        sin = kept["sin"][...]
         q = mm(n1_ref[HALO:, :], wf_ref[0, :, span])
         q_ref[:, span] = turn(q, cos[HALO:], sin[HALO:]).astype(BF16)
         k = mm(n1_ref[...], wf_ref[1, :, span])
@@ -931,21 +1048,22 @@
         return 0
 
     lax.fori_loop(0, width // 256, project, 0)
+    keep("q", "k", "v", "n1", "inv1", "cos", "sin")
     lse_ref[...] = jnp.zeros((TOK_DEV, 128), F32)
 
     for f2 in range(ranks):
         for h2 in range(his):
             settle(
-                g_hbm.at[at.l, f2, h2 * MOST : (h2 + 1) * MOST], gr.at[f2 * his + h2]
+                g_ref.at[at.l, f2, h2 * MOST : (h2 + 1) * MOST], gr.at[f2 * his + h2]
             )
-    send(g_hbm.at[at.l], g_hbm.at[at.l], gas.at[0], gqr.at[0], near[0])
-    send(g_hbm.at[at.l], g_hbm.at[at.l], gas.at[1], gqr.at[1], near[1])
+    send(g_ref.at[at.l], g_ref.at[at.l], gas.at[0], gqr.at[0], near[0])
+    send(g_ref.at[at.l], g_ref.at[at.l], gas.at[1], gqr.at[1], near[1])
 
     def pair(p, _):
         span = pl.ds(pl.multiple_of(p * 128, 128), 128)
         for first, count in QBLOCKS:
             keys = key_span(first)
-            ok = allowed_mask(pos_ref, first, count)[:, :keys]
+            ok = allowed_mask(pos_ref, first, count, 0)[:, :keys]
             q = q_ref[pl.ds(first, count), span]
             k = k_ref[pl.ds(first, keys), span]
             v = v_ref[pl.ds(first, keys), span]
@@ -967,28 +1085,30 @@
         return 0
 
     lax.fori_loop(0, HEADS // 2, pair, 0)
-    settle(g_hbm.at[at.l2], gqr.at[1])
-    send(g_hbm.at[at.l2], g_hbm.at[at.l2], gas.at[2], gqr.at[2], near[0])
+    settle(g_ref.at[at.l2], gqr.at[1])
+    send(g_ref.at[at.l2], g_ref.at[at.l2], gas.at[2], gqr.at[2], near[0])
 
     attn_out = mm(mix_ref[...], wf_ref[3]).astype(BF16)
     resid = tok_ref[...].astype(F32) + attn_out.astype(F32)
-    resid_ref[...] = resid
+    kept["resid"][...] = resid
     inv2 = lax.rsqrt(jnp.mean(resid * resid, axis=1, keepdims=True) + NORM_EPS)
     normed = resid * inv2 * g2
     narrow = normed.astype(BF16)
     raw = mm(narrow, s_ref[...].astype(BF16))
     prev = prev_ref[...]
-    wmix = wmix_ref[...]
+    wmix = jnp.concatenate(
+        [wmix_ref[...].astype(F32), jnp.zeros((EXPERTS_ALL, 128 - EXPERTS_ALL), F32)], axis=1
+    ).astype(BF16)
     phigh = prev.astype(BF16)
     prest = prev - phigh.astype(F32)
     pmid = prest.astype(BF16)
     plow = (prest - pmid.astype(F32)).astype(BF16)
-    mixed_prev = mm(phigh, wmix) + (mm(pmid, wmix) + mm(plow, wmix))
+    mixed_prev = mm(phigh, wmix, TN) + (mm(pmid, wmix, TN) + mm(plow, wmix, TN))
     logits = jnp.where(lanes < EXPERTS_ALL, raw + mixed_prev, NEG)
     top = jnp.max(logits, axis=1, keepdims=True)
     ex = jnp.exp(logits - top)
     probs = ex / jnp.sum(ex, axis=1, keepdims=True)
-    probs_ref[...] = probs
+    kept["probs"][...] = probs
     gate0 = pick(probs, hot0)
     gate1 = pick(probs, hot1)
 
@@ -1014,11 +1134,15 @@
         cols = jnp.where(lanes == 4 + 3 * c, gate_c, cols)
         cols = jnp.where(lanes == 5 + 3 * c, ma, cols)
         cols = jnp.where(lanes == 6 + 3 * c, mb, cols)
-    part_ref[...] = part
-    cols_ref[...] = cols
-    x_ref[...] = mm(spots0 + spots1, narrow, TN).astype(BF16)
+    kept["part"][...] = part
     wide0 = jnp.where(r0 < E, r0 * 128 + rank0, -1)
     wide1 = jnp.where(r1 < E, r1 * 128 + rank1, -1)
+    more = (pos_own[:, 0:1], c0, c1, r0, r1, wide0, wide1)
+    for i, value in enumerate(more):
+        cols = jnp.where(lanes == COL_POS + i, value.astype(F32), cols)
+    kept["cols"][...] = cols
+    keep("mix", "lse", "resid", "part", "probs", "cols")
+    x_ref[...] = mm(spots0 + spots1, narrow, TN).astype(BF16)
     for e in range(E):
         lane = lanes + e * 128
         row = jnp.sum(
@@ -1028,15 +1152,195 @@
         )
         gates_ref[e] = jnp.broadcast_to(row, (8, 128))
 
-    settle(g_hbm.at[at.l1], gqr.at[0])
-    settle(g_hbm.at[at.l3], gqr.at[2])
+
+    for j in range(ranks):
+        for hh in range(his):
+            e, peer = at.member(j, hh)
+            k = j * his + hh
+            rows = x_ref.at[pl.ds(aligned(e * MOST, 16), MOST)]
+            spot = xb_ref.at[at.f, at.l, own_spot]
+            if k == 0:
+                pltpu.make_async_copy(rows, spot, xr.at[at.m]).start()
+                pltpu.make_async_copy(
+                    gates_ref.at[e], gb_ref.at[at.f, at.l, at.hi], tr.at[at.m]
+                ).start()
+            else:
+                send(rows, spot, xs.at[k], xr.at[at.m], peer)
+                send(
+                    gates_ref.at[e], gb_ref.at[at.f, at.l, at.hi], ts.at[k], tr.at[at.m], peer
+                )
+    acc_ref[...] = jnp.zeros_like(acc_ref)
+
+    def take(j):
+        fj = xor4(at.f, j)
+        for hh in range(his):
+            hi = flip(at.hi, hh)
+            m = fj * his + hi
+            settle(xb_ref.at[fj, at.l, pl.ds(aligned(hi * MOST, 16), MOST)], xr.at[m])
+            settle(gb_ref.at[fj, at.l, hi], tr.at[m])
+        for i, peer in enumerate((core, side)):
+            send(xb_ref.at[fj, at.l], xb_ref.at[fj, at.l], qs.at[fj, i], qr.at[fj, i], peer)
+            send(gb_ref.at[fj, at.l], gb_ref.at[fj, at.l], tqs.at[fj, i], tqr.at[fj, i], peer)
+
+    def pass_on(j):
+        fj = xor4(at.f, j)
+        settle(xb_ref.at[fj, at.l2], qr.at[fj, 1])
+        settle(gb_ref.at[fj, at.l2], tqr.at[fj, 1])
+        send(xb_ref.at[fj, at.l2], xb_ref.at[fj, at.l2], qs.at[fj, 2], qr.at[fj, 2], core)
+        send(gb_ref.at[fj, at.l2], gb_ref.at[fj, at.l2], tqs.at[fj, 2], tqr.at[fj, 2], core)
+
+    def compute(j):
+        fj = xor4(at.f, j)
+        settle(xb_ref.at[fj, at.l1], qr.at[fj, 0])
+        settle(gb_ref.at[fj, at.l1], tqr.at[fj, 0])
+        settle(xb_ref.at[fj, at.l3], qr.at[fj, 2])
+        settle(gb_ref.at[fj, at.l3], tqr.at[fj, 2])
+        diagonal = lax.broadcasted_iota(jnp.int32, (MOST, 128), 0) == lane_iota(MOST)
+        pair_rows = 2 * his * MOST
+
+        def rows_of(i, _):
+            l2 = pl.ds(2 * i, 2)
+            x = xb_ref[fj, l2].reshape(pair_rows, width)
+            g = g_ref[l2, fj].reshape(pair_rows, width)
+            gate = jnp.concatenate(
+                [
+                    pick(
+                        jnp.broadcast_to(gb_ref[fj, 2 * i + i2, h][0:1, :], (MOST, 128)), diagonal
+                    )
+                    for i2 in range(2)
+                    for h in range(his)
+                ],
+                axis=0,
+            )
+            d_exp = (g.astype(F32) * gate).astype(BF16)
+            wg = w_ref[0]
+            wu = w_ref[1]
+            wd = w_ref[2]
+            a = mm(x, wg)
+            b = mm(x, wu)
+            sig = 1.0 / (1.0 + jnp.exp(-a))
+            hidden = (a * sig * b).astype(BF16)
+            shape = (2, his * MOST, width)
+            op_ref[fj, l2] = mm(hidden, wd, NT).astype(BF16).reshape(shape)
+            dh_raw = mm(g, wd)
+            d_route = jnp.sum(hidden.astype(F32) * dh_raw, axis=1, keepdims=True)
+            for i2 in range(2):
+                for h in range(his):
+                    first = (i2 * his + h) * MOST
+                    line = jnp.sum(
+                        jnp.where(diagonal, d_route[first : first + MOST], 0.0),
+                        axis=0,
+                        keepdims=True,
+                    )
+                    dgp_ref[fj, 2 * i + i2, h] = jnp.broadcast_to(line, (8, 128))
+            dh = dh_raw * gate
+            d_up = (dh * a * sig).astype(BF16)
+            d_gate = (dh * b * sig * (1.0 + a * (1.0 - sig))).astype(BF16)
+            od_ref[fj, l2] = (mm(d_gate, wg, NT) + mm(d_up, wu, NT)).astype(BF16).reshape(shape)
+            acc_ref[0] += mm(x, d_gate, TN)
+            acc_ref[1] += mm(x, d_up, TN)
+            acc_ref[2] += mm(d_exp, hidden, TN)
+            return 0
+
+        lax.fori_loop(0, lo // 2, rows_of, 0)
+        pltpu.make_async_copy(op_ref.at[fj], op_hbm.at[fj], last_sem.at[fj]).start()
+
+    def to_core(j):
+        fj = xor4(at.f, j)
+        send(od_ref.at[fj, at.l1], r1_ref.at[fj, 0], d1s.at[fj, 0], d1r.at[fj, 0], core)
+        send(od_ref.at[fj, at.l3], r1_ref.at[fj, 1], d1s.at[fj, 1], d1r.at[fj, 1], core)
+        send(dgp_ref.at[fj, at.l1], dr1_ref.at[fj, 0], t1s.at[fj, 0], t1r.at[fj, 0], core)
+        send(dgp_ref.at[fj, at.l3], dr1_ref.at[fj, 1], t1s.at[fj, 1], t1r.at[fj, 1], core)
+
+    def add(ref, other):
+        ref[...] = (ref[...].astype(F32) + other[...].astype(F32)).astype(BF16)
+
+    def to_side(j):
+        fj = xor4(at.f, j)
+        settle(r1_ref.at[fj, 1], d1r.at[fj, 1])
+        add(od_ref.at[fj, at.l2], r1_ref.at[fj, 1])
+        send(od_ref.at[fj, at.l2], r2_ref.at[fj], d2s.at[fj], d2r.at[fj], side)
+        settle(dr1_ref.at[fj, 1], t1r.at[fj, 1])
+        dgp_ref[fj, at.l2] += dr1_ref[fj, 1]
+        send(dgp_ref.at[fj, at.l2], dr2_ref.at[fj], t2s.at[fj], t2r.at[fj], side)
+        settle(r1_ref.at[fj, 0], d1r.at[fj, 0])
+        add(od_ref.at[fj, at.l], r1_ref.at[fj, 0])
+        settle(dr1_ref.at[fj, 0], t1r.at[fj, 0])
+        dgp_ref[fj, at.l] += dr1_ref[fj, 0]
+
+    def to_home(j):
+        fj = xor4(at.f, j)
+        settle(r2_ref.at[fj], d2r.at[fj])
+        add(od_ref.at[fj, at.l], r2_ref.at[fj])
+        settle(dr2_ref.at[fj], t2r.at[fj])
+        dgp_ref[fj, at.l] += dr2_ref[fj]
+        for hh in range(his):
+            hi = flip(at.hi, hh)
+            m = fj * his + hi
+            rows = od_ref.at[fj, at.l, pl.ds(aligned(hi * MOST, 16), MOST)]
+            peer = (hi * lo + at.l, fj)
+
+            line = dgp_ref.at[fj, at.l, hi]
+
+            def away(rows=rows, line=line, peer=peer, m=m):
+                send(rows, back_ref.at[at.m], bs.at[m], br.at[at.m], peer)
+                send(line, dgb_ref.at[at.m], tbs.at[m], tbr.at[at.m], peer)
+
+            if hh:
+                away()
+            else:
+
+                @pl.when(j == 0)
+                def _(rows=rows, line=line):
+                    pltpu.make_async_copy(rows, back_ref.at[at.m], br.at[at.m]).start()
+                    pltpu.make_async_copy(line, dgb_ref.at[at.m], tbr.at[at.m]).start()
+
+                pl.when(j > 0)(away)
+
+    take(0)
+    take(1)
+    settle(g_ref.at[at.l1], gqr.at[0])
+    settle(g_ref.at[at.l3], gqr.at[2])
     for f2 in range(ranks):
         for h2 in range(his):
             for w in range(3):
-                block = w_hbm.at[
+                block = w_ref.at[
                     w, f2 * head_rows : (f2 + 1) * head_rows, h2 * ff : (h2 + 1) * ff
                 ]
                 settle(block, wr.at[f2 * his + h2, w])
+
+    def step(t, _):
+        @pl.when(t < ranks)
+        def _():
+            pass_on(t)
+            compute(t)
+            to_core(t)
+
+        @pl.when(t + 2 < ranks)
+        def _():
+            take(t + 2)
+
+        @pl.when((t >= 1) & (t <= ranks))
+        def _():
+            to_side(t - 1)
+
+        @pl.when(t >= 2)
+        def _():
+            to_home(t - 2)
+
+        return 0
+
+    lax.fori_loop(0, ranks + 2, step, 0)
+
+    gw_ref[...] = acc_ref[...].astype(BF16)
+    pltpu.make_async_copy(gw_ref, gw_hbm, last_sem.at[4]).start()
+
+    for m in range(E):
+        settle(back_ref.at[m], br.at[m])
+        settle(dgb_ref.at[m], tbr.at[m])
+    pltpu.make_async_copy(back_ref, back_hbm, last_sem.at[5]).start()
+    pltpu.make_async_copy(dgb_ref, dgb_hbm, last_sem.at[6]).start()
+
     for j in range(1, ranks):
         settle(tile_ref, zs.at[j])
     for j in range(ranks):
@@ -1051,56 +1355,90 @@
 
     for k in range(1, E):
         settle(grow_ref.at[0:MOST], gs.at[k])
+        settle(x_ref.at[0:MOST], xs.at[k])
+        settle(gates_ref.at[0], ts.at[k])
         for w in range(3):
-            settle(wdt_ref.at[0], ws.at[k, w])
+            settle(w_ref.at[0, 0:head_rows, 0:ff], ws.at[k, w])
     for i in range(3):
-        settle(g_hbm.at[at.l], gas.at[i])
+        settle(g_ref.at[0], gas.at[i])
+    for f2 in range(ranks):
+        for i in range(3):
+            settle(xb_ref.at[0, 0], qs.at[f2, i])
+            settle(gb_ref.at[0, 0], tqs.at[f2, i])
+        for i in range(2):
+            settle(r1_ref.at[0, 0], d1s.at[f2, i])
+            settle(dr1_ref.at[0, 0], t1s.at[f2, i])
+        settle(r2_ref.at[0], d2s.at[f2])
+        settle(dr2_ref.at[0], t2s.at[f2])
+        settle(op_ref.at[0], last_sem.at[f2])
+    for j in range(ranks):
+        for hh in range(his):
+            if j or hh:
+                m = at.member(j, hh)[0]
+                settle(back_ref.at[0], bs.at[m])
+                settle(dgb_ref.at[0], tbs.at[m])
+    settle(gw_ref, last_sem.at[4])
+    settle(back_ref, last_sem.at[5])
+    settle(dgb_ref, last_sem.at[6])
+    for i, (name, _, _) in enumerate(KEPT):
+        settle(kept[name], keep_sem.at[i])
 
 
 SMALL_G1 = EXPERTS_ALL
 SMALL_VC = SMALL_G1 + 2
 SMALL_C = SMALL_VC + CONSTS
-
-
-def begin(
-    tile, tok, cot, routes, cos, sin, pos, prev, wmix, w_down, w_gate, w_up, groups, ranks
-):
+COL_POS, COL_C0, COL_C1, COL_R0, COL_R1, COL_W0, COL_W1 = range(16, 23)
+
+
+def ahead(groups, ranks, *args):
+    tok = args[13]
+    w_gate = args[15]
     width = tok.shape[1]
-    lo = groups * ranks // E
     his = E // ranks
-    ff = w_down.shape[1]
-    head_rows = w_down.shape[2]
+    lo = groups // his
+    ff = w_gate.shape[2]
     dma = pltpu.SemaphoreType.DMA
+    vm = pltpu.VMEM
     any_spec = pl.BlockSpec(memory_space=pl.ANY)
+    block = (width // ranks + 8, 4 * (width // groups))
+    rows = (his * MOST, width)
+    kept = [(kept_shape(dims, width), dtype) for _, dims, dtype in KEPT]
+    results = [
+        ((ranks, lo) + rows, BF16),
+        ((3, width, ff * his), BF16),
+        ((E, MOST, width), BF16),
+        ((E, 8, 128), F32),
+    ]
     return pl.pallas_call(
-        begin_kernel,
-        out_shape=[
-            sds((4, width, width), BF16),
-            sds((width, 128), F32),
-            sds((HALO, width), BF16),
-            sds((TOK_DEV, 128), jnp.int32),
-            sds((TOK_DEV, width), BF16),
-            sds((KEYS, width), BF16),
-            sds((KEYS, width), BF16),
-            sds((KEYS, width), BF16),
-            sds((KEYS, 128), F32),
-            sds((TOK_DEV, width), BF16),
-            sds((TOK_DEV, 128), F32),
-            sds((TOK_DEV, width), F32),
-            sds((TOK_DEV, width), F32),
-            sds((TOK_DEV, 128), F32),
-            sds((TOK_DEV, 128), F32),
-            sds((ROWS, width), BF16),
-            sds((E, 8, 128), F32),
-            sds((3, width, ff * his), BF16),
-            sds((lo, ranks, his * MOST, width), BF16),
-        ],
-        in_specs=whole(10) + [any_spec, any_spec],
-        out_specs=whole(17) + [any_spec, any_spec],
-        scratch_shapes=[
-            pltpu.VMEM((groups, ranks) + tile.shape, BF16),
-            pltpu.VMEM((E, head_rows, ff), BF16),
-            pltpu.VMEM((ROWS, width), BF16),
+        ahead_kernel,
+        out_shape=[sds(*k) for k in kept + results],
+        in_specs=[pl.BlockSpec(memory_space=pltpu.SMEM)] + whole(14) + [any_spec] * 3,
+        out_specs=[any_spec] * (len(kept) + len(results)),
+        scratch_shapes=[vm(*k) for k in kept]
+        + [
+            vm(block, BF16),
+            vm((128, 128), F32),
+            vm((groups, ranks) + block, BF16),
+            vm((ROWS, width), BF16),
+            vm((ROWS, width), BF16),
+            vm((E, 8, 128), F32),
+            vm((3, width, ff * his), BF16),
+            vm((lo, ranks) + rows, BF16),
+            vm((ranks, lo) + rows, BF16),
+            vm((ranks, lo, his, 8, 128), F32),
+            vm((ranks, lo) + rows, BF16),
+            vm((ranks, lo) + rows, BF16),
+            vm((ranks, 2) + rows, BF16),
+            vm((ranks,) + rows, BF16),
+            vm((ranks, lo, his, 8, 128), F32),
+            vm((ranks, 2, his, 8, 128), F32),
+            vm((ranks, his, 8, 128), F32),
+            vm((3, width, ff * his), F32),
+            vm((3, width, ff * his), BF16),
+            vm((E, MOST, width), BF16),
+            vm((E, 8, 128), F32),
+            dma((len(kept),)),
+            dma((8,)),
             dma((4,)),
             dma((4, 4)),
             dma((3, 4)),
@@ -1113,313 +1451,121 @@
             dma((E,)),
             dma((E, 3)),
             dma((3,)),
-        ],
-        compiler_params=params(60, collective_id=1, has_side_effects=True),
-        name="begin",
-    )(tile, tok, cot, routes, cos, sin, pos, prev, wmix, w_down, w_gate, w_up)
-
-
-def moe_kernel(
-    x_ref,
-    gates_ref,
-    w_ref,
-    g_ref,
-    back_ref,
-    gw_ref,
-    xb_ref,
-    gb_ref,
-    od_ref,
-    r1_ref,
-    r2_ref,
-    acc_ref,
-    xs,
-    gs,
-    qs,
-    gqs,
-    d1s,
-    d2s,
-    bs,
-    xr,
-    gr,
-    qr,
-    gqr,
-    d1r,
-    d2r,
-    br,
-):
-    lo, ranks = g_ref.shape[:2]
-    his = E // ranks
-    width = x_ref.shape[1]
-    at = Place(his, lo)
-    core = (at.core_peer, at.f)
-    side = (at.side_peer, at.f)
-    greet(at.others() + [core, side])
-    own_spot = pl.ds(aligned(at.hi * MOST, 16), MOST)
-
-    for j in range(ranks):
-        for hh in range(his):
-            e, peer = at.member(j, hh)
-            k = j * his + hh
-            rows = x_ref.at[pl.ds(aligned(e * MOST, 16), MOST)]
-            spot = xb_ref.at[at.f, at.l, own_spot]
-            if k == 0:
-                pltpu.make_async_copy(rows, spot, xr.at[at.m]).start()
-                pltpu.make_async_copy(
-                    gates_ref.at[e], gb_ref.at[at.f, at.l, at.hi], gr.at[at.m]
-                ).start()
-            else:
-                send(rows, spot, xs.at[k], xr.at[at.m], peer)
-                send(
-                    gates_ref.at[e], gb_ref.at[at.f, at.l, at.hi], gs.at[k], gr.at[at.m], peer
-                )
-    acc_ref[...] = jnp.zeros_like(acc_ref)
-
-    def take(j):
-        fj = xor4(at.f, j)
-        for hh in range(his):
-            hi = flip(at.hi, hh)
-            m = fj * his + hi
-            settle(xb_ref.at[fj, at.l, pl.ds(aligned(hi * MOST, 16), MOST)], xr.at[m])
-            settle(gb_ref.at[fj, at.l, hi], gr.at[m])
-        for i, peer in enumerate((core, side)):
-            send(xb_ref.at[fj, at.l], xb_ref.at[fj, at.l], qs.at[fj, i], qr.at[fj, i], peer)
-            send(gb_ref.at[fj, at.l], gb_ref.at[fj, at.l], gqs.at[fj, i], gqr.at[fj, i], peer)
-
-    def pass_on(j):
-        fj = xor4(at.f, j)
-        settle(xb_ref.at[fj, at.l2], qr.at[fj, 1])
-        settle(gb_ref.at[fj, at.l2], gqr.at[fj, 1])
-        send(xb_ref.at[fj, at.l2], xb_ref.at[fj, at.l2], qs.at[fj, 2], qr.at[fj, 2], core)
-        send(gb_ref.at[fj, at.l2], gb_ref.at[fj, at.l2], gqs.at[fj, 2], gqr.at[fj, 2], core)
-
-    def compute(j):
-        fj = xor4(at.f, j)
-        settle(xb_ref.at[fj, at.l1], qr.at[fj, 0])
-        settle(gb_ref.at[fj, at.l1], gqr.at[fj, 0])
-        settle(xb_ref.at[fj, at.l3], qr.at[fj, 2])
-        settle(gb_ref.at[fj, at.l3], gqr.at[fj, 2])
-        rows = lo * his * MOST
-        x = jnp.concatenate([xb_ref[fj, i] for i in range(lo)], axis=0)
-        g = jnp.concatenate([g_ref[i, fj] for i in range(lo)], axis=0)
-        diagonal = lax.broadcasted_iota(jnp.int32, (MOST, 128), 0) == lane_iota(MOST)
-        gate = jnp.concatenate(
-            [
-                pick(jnp.broadcast_to(gb_ref[fj, i, h][0:1, :], (MOST, 128)), diagonal)
-                for i in range(lo)
-                for h in range(his)
-            ],
-            axis=0,
-        )
-        d_exp = (g.astype(F32) * gate).astype(BF16)
-        wg = w_ref[0]
-        wu = w_ref[1]
-        wd = w_ref[2]
-        a = mm(x, wg)
-        b = mm(x, wu)
-        sig = 1.0 / (1.0 + jnp.exp(-a))
-        hidden = (a * sig * b).astype(BF16)
-        shape = (lo, his * MOST, width)
-        od_ref[fj, :, :, :width] = mm(hidden, wd, NT).astype(BF16).reshape(shape)
-        dh = mm(d_exp, wd)
-        d_up = (dh * a * sig).astype(BF16)
-        d_gate = (dh * b * sig * (1.0 + a * (1.0 - sig))).astype(BF16)
-        od_ref[fj, :, :, width:] = (
-            (mm(d_gate, wg, NT) + mm(d_up, wu, NT)).astype(BF16).reshape(shape)
-        )
-        acc_ref[0] += mm(x, d_gate, TN)
-        acc_ref[1] += mm(x, d_up, TN)
-        acc_ref[2] += mm(d_exp, hidden, TN)
-
-    def to_core(j):
-        fj = xor4(at.f, j)
-        send(od_ref.at[fj, at.l1], r1_ref.at[fj, 0], d1s.at[fj, 0], d1r.at[fj, 0], core)
-        send(od_ref.at[fj, at.l3], r1_ref.at[fj, 1], d1s.at[fj, 1], d1r.at[fj, 1], core)
-
-    def add(ref, other):
-        ref[...] = (ref[...].astype(F32) + other[...].astype(F32)).astype(BF16)
-
-    def to_side(j):
-        fj = xor4(at.f, j)
-        settle(r1_ref.at[fj, 1], d1r.at[fj, 1])
-        add(od_ref.at[fj, at.l2], r1_ref.at[fj, 1])
-        send(od_ref.at[fj, at.l2], r2_ref.at[fj], d2s.at[fj], d2r.at[fj], side)
-        settle(r1_ref.at[fj, 0], d1r.at[fj, 0])
-        add(od_ref.at[fj, at.l], r1_ref.at[fj, 0])
-
-    def to_home(j):
-        fj = xor4(at.f, j)
-        settle(r2_ref.at[fj], d2r.at[fj])
-        add(od_ref.at[fj, at.l], r2_ref.at[fj])
-        for hh in range(his):
-            hi = flip(at.hi, hh)
-            m = fj * his + hi
-            rows = od_ref.at[fj, at.l, pl.ds(aligned(hi * MOST, 16), MOST)]
-            peer = (hi * lo + at.l, fj)
-
-            def away(rows=rows, peer=peer, m=m):
-                send(rows, back_ref.at[at.m], bs.at[m], br.at[at.m], peer)
-
-            if hh:
-                away()
-            else:
-
-                @pl.when(j == 0)
-                def _(rows=rows):
-                    pltpu.make_async_copy(rows, back_ref.at[at.m], br.at[at.m]).start()
-
-                pl.when(j > 0)(away)
-
-    take(0)
-    take(1)
-
-    def step(t, _):
-        @pl.when(t < ranks)
-        def _():
-            pass_on(t)
-            compute(t)
-            to_core(t)
-
-        @pl.when(t + 2 < ranks)
-        def _():
-            take(t + 2)
-
-        @pl.when((t >= 1) & (t <= ranks))
-        def _():
-            to_side(t - 1)
-
-        @pl.when(t >= 2)
-        def _():
-            to_home(t - 2)
-
-        return 0
-
-    lax.fori_loop(0, ranks + 2, step, 0)
-
-    gw_ref[...] = acc_ref[...].astype(BF16)
-    for m in range(E):
-        settle(back_ref.at[m], br.at[m])
-    for k in range(1, E):
-        settle(x_ref.at[0:MOST], xs.at[k])
-        settle(gates_ref.at[0], gs.at[k])
-    for f2 in range(ranks):
-        for i in range(3):
-            settle(xb_ref.at[0, 0], qs.at[f2, i])
-            settle(gb_ref.at[0, 0], gqs.at[f2, i])
-        for i in range(2):
-            settle(r1_ref.at[0, 0], d1s.at[f2, i])
-        settle(r2_ref.at[0], d2s.at[f2])
-    for j in range(ranks):
-        for hh in range(his):
-            if j or hh:
-                m = at.member(j, hh)[0]
-                settle(back_ref.at[0], bs.at[m])
-
-
-def moe(x, gates, w, g):
-    lo, ranks, block, width = g.shape
-    dma = pltpu.SemaphoreType.DMA
-    his = E // ranks
-    return pl.pallas_call(
-        moe_kernel,
-        out_shape=[sds((E, MOST, 2 * width), BF16), sds(w.shape, BF16)],
-        in_specs=whole(4),
-        out_specs=whole(2),
-        scratch_shapes=[
-            pltpu.VMEM((ranks, lo, block, width), BF16),
-            pltpu.VMEM((ranks, lo, his, 8, 128), F32),
-            pltpu.VMEM((ranks, lo, block, 2 * width), BF16),
-            pltpu.VMEM((ranks, 2, block, 2 * width), BF16),
-            pltpu.VMEM((ranks, block, 2 * width), BF16),
-            pltpu.VMEM(w.shape, F32),
             dma((E,)),
             dma((E,)),
             dma((4, 3)),
             dma((4, 3)),
             dma((4, 2)),
+            dma((4, 2)),
             dma((4,)),
+            dma((4,)),
+            dma((E,)),
             dma((E,)),
             dma((E,)),
             dma((E,)),
             dma((4, 3)),
             dma((4, 3)),
             dma((4, 2)),
+            dma((4, 2)),
+            dma((4,)),
             dma((4,)),
             dma((E,)),
+            dma((E,)),
         ],
-        compiler_params=params(62, collective_id=2, has_side_effects=True),
-        name="moe",
-    )(x, gates, w, g)
+        compiler_params=params(63, collective_id=1, has_side_effects=True),
+        name="ahead",
+    )(*args)
 
 
 def end_kernel(
     cot_ref,
-    resid_ref,
-    part_ref,
-    probs_ref,
-    cols_ref,
-    slots_ref,
-    routes_ref,
+    tok_ref,
     prev_ref,
     wmix_ref,
-    s_ref,
-    od_ref,
-    gw_ref,
-    wf_ref,
-    q_ref,
-    k_ref,
-    v_ref,
-    n1_ref,
-    inv1_ref,
-    mix_ref,
-    lse_ref,
-    cos_ref,
-    sin_ref,
-    pos_ref,
-    tok_ref,
-    halo_ref,
-    out_ref,
-    dres_ref,
-    gprev_ref,
-    down_ref,
-    back_ref,
-    t_ref,
-    fin_ref,
-    gmix_ref,
-    flat_ref,
-    dhalo_ref,
-    dm_ref,
-    dq_ref,
-    dk_ref,
-    dv_ref,
-    dqr_ref,
-    dkr_ref,
-    dvr_ref,
-    full_ref,
-    p_ref,
-    r1_ref,
-    r2_ref,
-    r3_ref,
-    r4_ref,
-    mx_ref,
-    mr_ref,
-    mz_ref,
-    ts,
-    tr,
-    hs,
-    hr,
-    s1,
-    e1,
-    s2,
-    e2,
-    s3,
-    e3,
-    s4,
-    e4,
-    ms,
-    me,
-    zs,
-    ze,
+    back_hbm,
+    dgb_hbm,
+    op_hbm,
+    gw_hbm,
+    *rest,
 ):
+    n = len(KEPT)
+    kept_hbm = by_name(rest[:n])
+    (
+        out_ref,
+        dres_ref,
+        gprev_ref,
+        down_ref,
+        back_ref,
+        fin_ref,
+        gmix_ref,
+        t_ref,
+    ) = rest[n : n + 8]
+    kept = by_name(rest[n + 8 : 2 * n + 8])
+    (
+        dx_ref,
+        dgb_ref,
+        opl_ref,
+        r1o_ref,
+        r2o_ref,
+        outb_ref,
+        flat_ref,
+        dhalo_ref,
+        dm_ref,
+        dq_ref,
+        dk_ref,
+        dv_ref,
+        dqr_ref,
+        dkr_ref,
+        dvr_ref,
+        full_ref,
+        p_ref,
+        r1_ref,
+        r2_ref,
+        r3_ref,
+        r4_ref,
+        mx_ref,
+        mr_ref,
+        mz_ref,
+        load_sem,
+        more_sem,
+        o1s,
+        o1r,
+        o2s,
+        o2r,
+        obs,
+        obr,
+        ts,
+        tr,
+        hs,
+        hr,
+        s1,
+        e1,
+        s2,
+        e2,
+        s3,
+        e3,
+        s4,
+        e4,
+        ms,
+        me,
+        zs,
+        ze,
+    ) = rest[2 * n + 8 :]
+    wf_ref, s_ref, halo_ref, cols_ref = kept["wf"], kept["s"], kept["halo"], kept["cols"]
+    q_ref, k_ref, v_ref, n1_ref = kept["q"], kept["k"], kept["v"], kept["n1"]
+    mix_ref, lse_ref = kept["mix"], kept["lse"]
+    names = [item[0] for item in KEPT]
+
+    def load(*which):
+        for name in which:
+            pltpu.make_async_copy(
+                kept_hbm[name], kept[name], load_sem.at[names.index(name)]
+            ).start()
+
+    def ready(*which):
+        for name in which:
+            settle(kept[name], load_sem.at[names.index(name)])
+
     ranks = p_ref.shape[1]
     his = E // ranks
     groups = p_ref.shape[0]
@@ -1430,7 +1576,22 @@
     core = (at.core_peer, at.f)
     side = (at.side_peer, at.f)
     upper = (lo * (1 - at.hi) + at.l, at.f)
-    greet(at.others() + [core, side])
+    peers = at.others() + [core, side]
+    call(peers)
+    pltpu.make_async_copy(back_hbm, dx_ref, more_sem.at[0]).start()
+    pltpu.make_async_copy(dgb_hbm, dgb_ref, more_sem.at[1]).start()
+    load("cols", "s", "resid", "probs", "mix", "wf", "q", "k", "v", "lse")
+    for f2 in range(ranks):
+        for i, l2 in enumerate((at.l, at.l2)):
+            pltpu.make_async_copy(
+                op_hbm.at[f2, l2], opl_ref.at[f2, i], more_sem.at[2 + 2 * f2 + i]
+            ).start()
+    load("cos", "sin", "n1", "inv1", "halo", "part")
+    answer(peers)
+
+    for f2 in range(ranks):
+        send(op_hbm.at[f2, at.l1], r1o_ref.at[f2, 0], o1s.at[f2, 0], o1r.at[f2, 0], core)
+        send(op_hbm.at[f2, at.l3], r1o_ref.at[f2, 1], o1s.at[f2, 1], o1r.at[f2, 1], core)
 
     for j in range(ranks):
         for hh in range(his):
@@ -1439,12 +1600,18 @@
             lanes_at = pl.ds(aligned(lax.rem(e, his) * tile[1], 128), tile[1])
             n = j * his + hh
             for w in range(3):
-                block = gw_ref.at[w, rows, lanes_at]
+                block = gw_hbm.at[w, rows, lanes_at]
                 if n == 0:
                     pltpu.make_async_copy(block, t_ref.at[at.m, w], tr.at[at.m, w]).start()
                 else:
                     send(block, t_ref.at[at.m, w], ts.at[n, w], tr.at[at.m, w], peer)
 
+    def add(ref, other):
+        ref[...] = (ref[...].astype(F32) + other[...].astype(F32)).astype(BF16)
+
+    ready("cols", "s", "resid", "probs")
+    settle(dx_ref, more_sem.at[0])
+    settle(dgb_ref, more_sem.at[1])
     flat = s_ref[...].T
     gain1 = flat[SMALL_G1 : SMALL_G1 + 1, :]
     gain2 = flat[SMALL_G1 + 1 : SMALL_G1 + 2, :]
@@ -1457,22 +1624,23 @@
         return pick(cols, lanes == i)
 
     gate0, gate1, gate_id, inv2 = col(0), col(1), col(2), col(3)
-    resid = resid_ref[...]
+    resid = kept["resid"][...]
     unit2 = resid * inv2
     normed = unit2 * gain2
     narrow = normed.astype(BF16)
-    od = od_ref[...].reshape(ROWS, 2 * width)
+    c0, c1, r0, r1, wide0, wide1 = (
+        col(COL_POS + 1 + i).astype(jnp.int32) for i in range(6)
+    )
     slot = lane_iota(TOK_DEV, ROWS)
-    hot0 = jnp.where(slot == slots_ref[:, 0:1], 1.0, 0.0).astype(BF16)
-    hot1 = jnp.where(slot == slots_ref[:, 1:2], 1.0, 0.0).astype(BF16)
-    y0 = mm(hot0, od[:, :width])
-    y1 = mm(hot1, od[:, :width])
-    out_ref[...] = (part_ref[...] + gate0 * y0 + gate1 * y1).astype(BF16)
+    hot0 = jnp.where(slot == c0, 1.0, 0.0).astype(BF16)
+    hot1 = jnp.where(slot == c1, 1.0, 0.0).astype(BF16)
+    dg0 = jnp.zeros((TOK_DEV, 1), F32)
+    dg1 = jnp.zeros((TOK_DEV, 1), F32)
+    for e in range(E):
+        line = jnp.broadcast_to(dgb_ref[e][0:1, :], (TOK_DEV, 128))
+        dg0 = dg0 + pick(line, lanes + e * 128 == wide0)
+        dg1 = dg1 + pick(line, lanes + e * 128 == wide1)
     a_n = jnp.sum(g * normed, axis=1, keepdims=True)
-    dg0 = jnp.sum(g * y0, axis=1, keepdims=True)
-    dg1 = jnp.sum(g * y1, axis=1, keepdims=True)
-    r0 = routes_ref[:, 0:1]
-    r1 = routes_ref[:, 1:2]
     dg0 = jnp.where(r0 == E + 1, a_n, dg0)
     dg1 = jnp.where(r1 == E + 1, a_n, dg1)
     g_scale = gate_id
@@ -1491,14 +1659,14 @@
         dl = jnp.where(lanes == SMALL_C + 2 * c, ma * (da - mean), dl)
         dl = jnp.where(lanes == SMALL_C + 1 + 2 * c, mb * (db - mean), dl)
         vmix = jnp.where(lanes == SMALL_VC + c, gate_c * mb, vmix)
-    probs = probs_ref[...]
+    probs = kept["probs"][...]
     d_probs = jnp.where(lanes == r0, dg0, 0.0) + jnp.where(lanes == r1, dg1, 0.0)
     d_logits = probs * (d_probs - jnp.sum(probs * d_probs, axis=1, keepdims=True))
     dl = jnp.where(lanes < EXPERTS_ALL, d_logits, dl)
     high = dl.astype(BF16)
     low = (dl - high.astype(F32)).astype(BF16)
     wr = s_ref[...].astype(BF16)
-    d_normed = g_scale * g + mm(hot0 + hot1, od[:, width:])
+    d_normed = g_scale * g + mm(hot0 + hot1, dx_ref[...].reshape(ROWS, width))
     d_normed = d_normed + mm(high, wr, NT) + mm(low, wr, NT)
     vhigh = vmix.astype(BF16)
     vlow = (vmix - vhigh.astype(F32)).astype(BF16)
@@ -1509,15 +1677,27 @@
     flat_ref[...] = jnp.where(row_id == SMALL_G1 + 1, dg2, tiny)
     n = d_normed * gain2
     dres_ref[...] = g + inv2 * (n - unit2 * jnp.mean(n * unit2, axis=1, keepdims=True))
-    wmix = wmix_ref[...]
-    gprev_ref[...] = mm(high, wmix, NT) + mm(low, wmix, NT)
+    wmix = jnp.concatenate(
+        [wmix_ref[...].astype(F32), jnp.zeros((EXPERTS_ALL, 128 - EXPERTS_ALL), F32)], axis=1
+    ).astype(BF16)
+    gprev_ref[...] = mm(wmix, high, NT) + mm(wmix, low, NT)
     prev = prev_ref[...]
     phigh = prev.astype(BF16)
     plow = (prev - phigh.astype(F32)).astype(BF16)
-    d_mix = mm(phigh, high, TN) + mm(phigh, low, TN) + mm(plow, high, TN)
-    mx_ref[0] = d_mix[0:16]
+    mx_ref[0] = jnp.zeros(mx_ref.shape[1:], F32)
+    mx_ref[0, 0:EXPERTS_ALL, :] = mm(phigh, high) + mm(phigh, low) + mm(plow, high)
     send(mx_ref.at[0], mr_ref.at[0], ms.at[0], me.at[0], core)
 
+    for f2 in range(ranks):
+        settle(opl_ref.at[f2, 1], more_sem.at[3 + 2 * f2])
+        settle(r1o_ref.at[f2, 1], o1r.at[f2, 1])
+        add(opl_ref.at[f2, 1], r1o_ref.at[f2, 1])
+        send(opl_ref.at[f2, 1], r2o_ref.at[f2], o2s.at[f2], o2r.at[f2], side)
+        settle(opl_ref.at[f2, 0], more_sem.at[2 + 2 * f2])
+        settle(r1o_ref.at[f2, 0], o1r.at[f2, 0])
+        add(opl_ref.at[f2, 0], r1o_ref.at[f2, 0])
+
+    ready("mix", "wf", "q", "k", "v", "lse")
     scale = HEAD_DIM ** (-0.5)
     d_attn = dres_ref[...].astype(BF16)
     full_ref[3] = mm(mix_ref[...], d_attn, TN).astype(BF16)
@@ -1529,7 +1709,7 @@
         span = pl.ds(pl.multiple_of(p * 128, 128), 128)
         for first, count in QBLOCKS:
             keys = key_span(first)
-            ok = allowed_mask(pos_ref, first, count)[:, :keys]
+            ok = allowed_mask(cols_ref, first, count, COL_POS)[:, :keys]
             q = q_ref[pl.ds(first, count), span]
             dm = dm_ref[pl.ds(first, count), span]
             k = k_ref[pl.ds(first, keys), span]
@@ -1558,14 +1738,32 @@
             dq_ref[pl.ds(first, count), span] = dq * scale
             dk_ref[pl.ds(first, keys), span] += dk * scale
             dv_ref[pl.ds(first, keys), span] += dv
+
+        @pl.when(p == 2)
+        def _():
+            for j in range(ranks):
+                fj = xor4(at.f, j)
+                settle(r2o_ref.at[fj], o2r.at[fj])
+                add(opl_ref.at[fj, 0], r2o_ref.at[fj])
+                for hh in range(his):
+                    m, peer = at.member(j, hh)
+                    hi = flip(at.hi, hh)
+                    rows = opl_ref.at[fj, 0, pl.ds(aligned(hi * MOST, 16), MOST)]
+                    if j or hh:
+                        send(rows, outb_ref.at[at.m], obs.at[m], obr.at[at.m], peer)
+                    else:
+                        pltpu.make_async_copy(rows, outb_ref.at[at.m], obr.at[at.m]).start()
+
         return 0
 
     lax.fori_loop(0, HEADS // 2, pair, 0)
+
+    ready("cos", "sin", "n1", "inv1", "halo", "part")
 
     def unturn(i, _):
         span = pl.ds(pl.multiple_of(i * 256, 256), 256)
-        cos = cos_ref[...]
-        sin = sin_ref[...]
+        cos = kept["cos"][...]
+        sin = kept["sin"][...]
         dqr_ref[:, span] = turn(dq_ref[:, span], cos[HALO:], -sin[HALO:]).astype(BF16)
         dkr_ref[:, span] = turn(dk_ref[:, span], cos, -sin).astype(BF16)
         dvr_ref[:, span] = dv_ref[:, span].astype(BF16)
@@ -1587,7 +1785,7 @@
     full_ref[1] = mm(n1_ref[...], dkr_ref[...], TN).astype(BF16)
     full_ref[2] = mm(n1_ref[...], dvr_ref[...], TN).astype(BF16)
     d_own = d_all[HALO:] + mm(dqr_ref[...], wf_ref[0], NT)
-    inv1 = inv1_ref[:, 0:1]
+    inv1 = kept["inv1"][:, 0:1]
     unit_own = tok_ref[...].astype(F32) * inv1[HALO:]
     unit_halo = halo_ref[...].astype(F32) * inv1[:HALO]
     dg1 = jnp.sum(d_own * unit_own, axis=0, keepdims=True) + jnp.sum(
@@ -1618,9 +1816,6 @@
             p_ref[g2, f2, head_rows : head_rows + 8, :] = jnp.concatenate(
                 pieces, axis=1
             ).astype(BF16)
-
-    def add(ref, other):
-        ref[...] = (ref[...].astype(F32) + other[...].astype(F32)).astype(BF16)
 
     c = lax.rem(at.g, 2)
     x = lax.rem(at.g // 2, 2)
@@ -1676,6 +1871,18 @@
         f2 = xor4(at.f, j)
         send(p_ref.at[at.g, f2], r4_ref.at[at.f], s4.at[j], e4.at[at.f], (at.g, f2))
         send(mx_ref.at[3], mz_ref.at[at.f], zs.at[j], ze.at[at.f], (at.g, f2))
+    for m in range(E):
+        settle(outb_ref.at[m], obr.at[m])
+    rows = outb_ref[...].reshape(ROWS, width)
+    cols = cols_ref[...]
+    c0 = pick(cols, lanes == COL_C0).astype(jnp.int32)
+    c1 = pick(cols, lanes == COL_C1).astype(jnp.int32)
+    y0 = mm(jnp.where(slot == c0, 1.0, 0.0).astype(BF16), rows)
+    y1 = mm(jnp.where(slot == c1, 1.0, 0.0).astype(BF16), rows)
+    gate0 = pick(cols, lanes == 0)
+    gate1 = pick(cols, lanes == 1)
+    out_ref[...] = (kept["part"][...] + gate0 * y0 + gate1 * y1).astype(BF16)
+
     total = p_ref[at.g, at.f].astype(F32)
     for j in range(1, ranks):
         f2 = xor4(at.f, j)
@@ -1685,6 +1892,14 @@
     fin_ref[...] = total
     gmix_ref[...] = (mz_ref[0] + mz_ref[1]) + (mz_ref[2] + mz_ref[3])
 
+    for f2 in range(ranks):
+        for i in range(2):
+            settle(r1o_ref.at[0, 0], o1s.at[f2, i])
+        settle(r2o_ref.at[0], o2s.at[f2])
+    for j in range(ranks):
+        for hh in range(his):
+            if j or hh:
+                settle(outb_ref.at[0], obs.at[at.member(j, hh)[0]])
     for m in range(E):
         for w in range(3):
             settle(t_ref.at[m, w], tr.at[m, w])
@@ -1720,21 +1935,31 @@
     vm = pltpu.VMEM
     block = (width // ranks + 8, 4 * (width // groups))
     half = ranks // 2
+    rows = (E // ranks * MOST, width)
+    kept = [(kept_shape(dims, width), dtype) for _, dims, dtype in KEPT]
+    any_spec = pl.BlockSpec(memory_space=pl.ANY)
     return pl.pallas_call(
         end_kernel,
         out_shape=[
             sds((TOK_DEV, width), BF16),
             sds((TOK_DEV, width), F32),
-            sds((TOK_DEV, 128), F32),
+            sds((EXPERTS_ALL, TOK_DEV), F32),
             sds((TOK_DEV, width), F32),
             sds((HALO, width), BF16),
-            sds((E, 3) + tile, BF16),
             sds(block, F32),
             sds((16, 128), F32),
+            sds((E, 3) + tile, BF16),
         ],
-        in_specs=whole(25),
-        out_specs=whole(8),
-        scratch_shapes=[
+        in_specs=whole(4) + [any_spec] * (4 + len(kept)),
+        out_specs=whole(7) + [any_spec],
+        scratch_shapes=[vm(*k) for k in kept]
+        + [
+            vm((E, MOST, width), BF16),
+            vm((E, 8, 128), F32),
+            vm((ranks, 2) + rows, BF16),
+            vm((ranks, 2) + rows, BF16),
+            vm((ranks,) + rows, BF16),
+            vm((E, MOST, width), BF16),
             vm((128, width), F32),
             vm((HALO, width), BF16),
             vm((TOK_DEV, width), BF16),
@@ -1753,6 +1978,14 @@
             vm((4, 16, 128), F32),
             vm((3, 16, 128), F32),
             vm((ranks, 16, 128), F32),
+            dma((len(kept),)),
+            dma((2 + 2 * ranks,)),
+            dma((ranks, 2)),
+            dma((ranks, 2)),
+            dma((ranks,)),
+            dma((ranks,)),
+            dma((E,)),
+            dma((E,)),
             dma((E, 3)),
             dma((E, 3)),
             dma,
@@ -1790,20 +2023,35 @@
     gk_ref,
     gv_ref,
     go_ref,
-    small_ref,
+    router_ref,
+    const_ref,
+    vconst_ref,
+    gain1_ref,
+    gain2_ref,
     gtok_ref,
 ):
     for e in range(E):
         gate_ref[e] = t_ref[e, 0].astype(F32)
         up_ref[e] = t_ref[e, 1].astype(F32)
-        downw_ref[e] = t_ref[e, 2].astype(F32).T
+        downw_ref[e] = t_ref[e, 2].astype(F32)
     head_rows, part_cols = gq_ref.shape
     for w, ref in enumerate((gq_ref, gk_ref, gv_ref, go_ref)):
         ref[...] = fin_ref[0:head_rows, w * part_cols : (w + 1) * part_cols]
-    for i in range(small_ref.shape[0] // 8):
-        small_ref[8 * i : 8 * i + 8, :] = fin_ref[
-            head_rows : head_rows + 8, 128 * i : 128 * i + 128
+    per = router_ref.shape[1]
+    column = jnp.concatenate(
+        [
+            fin_ref[head_rows : head_rows + 8, 128 * i : 128 * i + 128]
+            for i in range(per // 8)
         ]
+        + [jnp.zeros((128 - per, 128), F32)],
+        axis=0,
+    )
+    flat = column.T[:, 0:per]
+    router_ref[...] = flat[0:EXPERTS_ALL]
+    gain1_ref[...] = flat[SMALL_G1 : SMALL_G1 + 1]
+    gain2_ref[...] = flat[SMALL_G1 + 1 : SMALL_G1 + 2]
+    vconst_ref[...] = flat[SMALL_VC : SMALL_VC + CONSTS]
+    const_ref[...] = flat[SMALL_C : SMALL_C + 2 * CONSTS]
     width = tok_ref.shape[1]
     inv1 = inv1_ref[HALO:, 0:1]
     unit = tok_ref[...].astype(F32) * inv1
@@ -1820,12 +2068,18 @@
     per = width // (groups * ranks)
     return pl.pallas_call(
         store_kernel,
-        out_shape=[sds((E, rows, cols), F32)] * 2
-        + [sds((E, cols, rows), F32)]
+        out_shape=[sds((E, rows, cols), F32)] * 3
         + [sds((width // ranks, width // groups), F32)] * 4
-        + [sds((per, 128), F32), sds(tok.shape, F32)],
+        + [
+            sds((EXPERTS_ALL, per), F32),
+            sds((2 * CONSTS, per), F32),
+            sds((CONSTS, per), F32),
+            sds((1, per), F32),
+            sds((1, per), F32),
+            sds(tok.shape, F32),
+        ],
         in_specs=whole(7),
-        out_specs=whole(9),
+        out_specs=whole(13),
         compiler_params=params(48),
         name="store",
     )(t, fin, dres, down, back, tok, inv1)
@@ -1854,101 +2108,66 @@
 ):
     groups = lax.axis_size("grp")
     ranks = lax.axis_size("fsdp")
-    f_id = lax.axis_index("fsdp")
-    width = tokens.shape[1]
-    per = gain_one.shape[0]
-
-    small = jnp.concatenate(
-        [w_router, gain_one[:, None], gain_two[:, None], v_const, w_const], axis=1
-    )
-    small = jnp.pad(small, ((0, 0), (0, 128 - small.shape[1])))
-    small = small.reshape(per // 8, 8, 128).transpose(1, 0, 2).reshape(8, per // 8 * 128)
-    tile = jnp.concatenate([w_query, w_key, w_value, w_out], axis=1)
-    tile = jnp.concatenate([tile, small], axis=0)
-
-    seq_len = lengths[0]
-    count = seq_len.shape[0]
-    ids = jnp.arange(count, dtype=jnp.int32)
-    ends = jnp.sum(jnp.where(ids[:, None] >= ids[None, :], seq_len[None, :], 0), axis=1)
-    row = f_id * TOK_DEV + jnp.arange(-HALO, TOK_DEV, dtype=jnp.int32)
-    start = jnp.max(jnp.where(ends[None, :] <= row[:, None], ends[None, :], 0), axis=1)
-    pos = jnp.maximum(row - start, 0)
-    cos, sin = rotation_tables(pos, HEAD_DIM)
-    cos = jnp.concatenate([cos] * 4, axis=1)
-    sin = jnp.concatenate([-sin, sin, -sin, sin], axis=1)
-    pos_own = jnp.broadcast_to(pos[HALO:, None], (TOK_DEV, 128))
-    prev = jnp.pad(prev_logits, ((0, 0), (0, 128 - EXPERTS_ALL)))
-    wmix = jnp.pad(w_mix, ((0, 128 - EXPERTS_ALL), (0, 128 - EXPERTS_ALL)))
-
-    outs = begin(
-        tile,
+    kept = len(KEPT)
+    prev = prev_logits.T
+    outs = ahead(
+        groups,
+        ranks,
+        lengths,
+        routes.T,
+        prev,
+        w_mix,
+        w_router.T,
+        gain_one[None, :],
+        gain_two[None, :],
+        w_const.T,
+        v_const.T,
+        w_query,
+        w_key,
+        w_value,
+        w_out,
         tokens,
         cotangent,
-        routes,
-        cos,
-        sin,
-        pos_own,
-        prev,
-        wmix,
-        w_down,
         w_gate,
         w_up,
-        groups,
-        ranks,
-    )
-    wf, small, halo, slots, q, k, v, n1, inv1, mix, lse, resid, part, probs, cols = outs[:15]
-    x, gates, w_all, g_all = outs[15:]
-    od_back, gw = moe(x, gates, w_all, g_all)
-    output, dres, gprev, down, back, tiles, fin, gmix = end(
+        w_down.transpose(0, 2, 1),
+    )
+    parts, grads, dx, routed = outs[kept:]
+    output, dres, gprev, down, back, fin, gmix, tiles = end(
         groups,
         ranks,
         w_gate.shape[1:],
         cotangent,
-        resid,
-        part,
-        probs,
-        cols,
-        slots,
-        routes,
+        tokens,
         prev,
-        wmix,
-        small,
-        od_back,
-        gw,
-        wf,
-        q,
-        k,
-        v,
-        n1,
-        inv1,
-        mix,
-        lse,
-        cos,
-        sin,
-        pos_own,
-        tokens,
-        halo,
-    )
-    grad_gate, grad_up, grad_down, gq, gk, gv, go, tiny, grad_tokens = store(
+        w_mix,
+        dx,
+        routed,
+        parts,
+        grads,
+        *outs[:kept],
+    )
+    inv1 = by_name(outs[:kept])["inv1"]
+    gate, up, downw, gq, gk, gv, go, router, const, vconst, gain1, gain2, grad_tokens = store(
         tiles, fin, dres, down, back, tokens, inv1, groups, ranks
     )
     return (
         output,
         grad_tokens,
-        gprev[:, :EXPERTS_ALL],
-        tiny[:, SMALL_G1],
+        gprev.T,
+        gain1[0],
         gq,
         gk,
         gv,
         go,
-        tiny[:, SMALL_G1 + 1],
-        tiny[:, :EXPERTS_ALL],
+        gain2[0],
+        router.T,
         gmix[:EXPERTS_ALL, :EXPERTS_ALL],
-        tiny[:, SMALL_C : SMALL_C + 2 * CONSTS],
-        tiny[:, SMALL_VC : SMALL_VC + CONSTS],
-        grad_gate,
-        grad_up,
-        grad_down,
+        const.T,
+        vconst.T,
+        gate,
+        up,
+        downw.transpose(0, 2, 1),
     )
 
 

time: 365 us -> 319 us (0.87)
  Pallas kernels: 336 us -> 310 us
  local copies, waits for them, and re-layouts: 22.2 us -> 8.03 us
  other arithmetic: 5.06 us -> 0 us
    pallas_call x3 -> x2, Pallas kernels: 240 us -> 204 us  [the longest x1 200 us: ahead(): pl.pallas_call(ahead_kernel, out_shape=[sds(*k) for k in kept + results],...]
    pallas_call x1, Pallas kernels: 95.9 us -> 106 us  [end(): pl.pallas_call(end_kernel, out_shape=[sds((TOK_DEV, width), BF16), sds((T...]
    unnamed x31 -> x23, local copies, waits for them, and re-layouts: 17 us -> 8.03 us
where the time goes in v4:
time: 319 us; the launch traced here: 318 us
  Pallas kernels  310 us (97%)
  local copies, waits for them, and re-layouts  8.03 us (3%)
    pallas_call x1, Pallas kernels, ahead(): pl.pallas_call(ahead_kernel, out_shape=[sds(*k) for k in kept + results],...  200 us
    pallas_call x1, Pallas kernels, end(): pl.pallas_call(end_kernel, out_shape=[sds((TOK_DEV, width), BF16), sds((T...  106 us
    unnamed x23, local copies, waits for them, and re-layouts  8.03 us

profile of v4, /device:TPU:0, one launch (start us, length us, event | category | flops | bytes accessed | tf_op | source)
XLA Modules:
  0.0 318.5 jit_solution(548357081908680259)
XLA Ops:
  0.7 200.4 %ahead.1 = (bf16[4,768,768]{2,1,0:T(8,128)(2,1)}, f32[768,128]{1,0:T(8,128)}, bf16[256,768]{1,0:T(8,128)(2,1)}, bf16[320,768]{1,0:T(8,128)(2,1)}, bf16[576,768]{...) custom-call(s32[1,8]{1,0:T(1,128)} %len_ref.1, ...), custom_call_target="tpu_custom_call" | custom-call | tf_op jit(solution)/shard_map/ahead/pallas_call | solution.py:1412
  201.1 0.0 copy-start
  201.1 0.0 copy-start.2
  201.1 106.1 %end.1 = (bf16[320,768]{1,0:T(8,128)(2,1)}, f32[320,768]{1,0:T(8,128)}, f32[12,320]{1,0:T(8,128)}, f32[320,768]{1,0:T(8,128)}, bf16[256,768]{1,0:T(8,128)(2,1)},...) custom-call(bf16[320,768]{1,0:T(8,128)(2,1)} %cot_ref.3, bf16[320,768]{1,0:T(8,128)(2,1)} %tok_ref.5, ...), custom_call_target="tpu_custom_call" | custom-call | tf_op jit(solution)/shard_map/end/pallas_call | solution.py:1941
  307.2 0.0 copy-done
  307.2 0.0 copy-done.2
  307.2 0.0 copy-start.1
  307.2 1.7 copy-done.1
  308.9 0.0 copy-start.3
  308.9 1.2 copy-done.3
  310.1 0.0 copy-start.4
  310.1 1.2 copy-done.4
  311.3 0.0 copy-start.5
  311.3 1.0 copy-done.5
  312.3 0.0 copy-start.6
  312.3 1.0 copy-done.6
  313.2 0.0 copy-start.7
  313.2 3.2 %store.1 = (f32[8,192,256]{2,1,0:T(8,128)}, f32[8,192,256]{2,1,0:T(8,128)}, f32[8,192,256]{2,1,0:T(8,128)}, f32[192,96]{1,0:T(8,128)}, f32[192,96]{1,0:T(8,128)}...) custom-call(bf16[8,3,192,256]{3,2,1,0:T(8,128)(2,1)S(1)} %copy-done., ...), custom_call_target="tpu_custom_call" | custom-call | tf_op jit(solution)/shard_map/store/pallas_call | solution.py:2069
  316.5 0.0 copy-done.7
  316.5 0.8 copy.37
  317.2 0.0 copy-done.8
  317.2 0.6 copy.38
  317.9 0.0 copy-done.9
  317.9 0.6 copy.39
  (2 shorter events, 0.0 us)
Async XLA Ops:
  201.1 106.1 %copy-start = (bf16[320,768]{1,0:T(8,128)(2,1)S(1)}, bf16[320,768]{1,0:T(8,128)(2,1)}, u32[]{:S(2)}) copy-start(bf16[320,768]{1,0:T(8,128)(2,1)} %tok_ref.5) | copy-start | bytes 1474564
  201.1 106.1 %copy-start.2 = (f32[576,128]{1,0:T(8,128)S(1)}, f32[576,128]{1,0:T(8,128)}, u32[]{:S(2)}) copy-start(f32[576,128]{1,0:T(8,128)} %get-tuple-element.68.rest_7_.inv1_ref) | copy-start | bytes 884740
  307.2 1.7 copy-start.1
  308.9 1.2 copy-start.3
  310.1 1.2 copy-start.4
  311.3 1.0 copy-start.5
  312.3 1.0 copy-start.6
  313.2 3.2 %copy-start.7 = (bf16[320,768]{1,0:T(8,128)(2,1)S(1)}, bf16[320,768]{1,0:T(8,128)(2,1)}, u32[]{:S(2)}) copy-start(bf16[320,768]{1,0:T(8,128)(2,1)} %get-tuple-element.114) | copy-start | bytes 1474564
  313.2 4.0 %copy-start.8 = (f32[12,320]{1,0:T(8,128)S(1)}, f32[12,320]{1,0:T(8,128)}, u32[]{:S(2)}) copy-start(f32[12,320]{1,0:T(8,128)} %get-tuple-element.84) | copy-start | bytes 46084
  313.2 4.6 %copy-start.9 = (f32[16,128]{1,0:T(8,128)S(1)}, f32[16,128]{1,0:T(8,128)}, u32[]{:S(2)}) copy-start(f32[16,128]{1,0:T(8,128)} %get-tuple-element.92) | copy-start | bytes 24580

commit v5 on v4

--- a/solution.py
+++ b/solution.py
@@ -796,7 +796,8 @@
         grow_ref,
         x_ref,
         gates_ref,
-        w_ref,
+        wgu_ref,
+        wd_ref,
         g_ref,
         xb_ref,
         gb_ref,
@@ -807,7 +808,10 @@
         dgp_ref,
         dr1_ref,
         dr2_ref,
-        acc_ref,
+        accgu_ref,
+        accd_ref,
+        hid_ref,
+        dgu_ref,
         gw_ref,
         back_ref,
         dgb_ref,
@@ -939,29 +943,33 @@
     own_rows = pl.ds(aligned(at.f * head_rows, 16), head_rows)
     own_cols = pl.ds(aligned(at.hi * ff, 128), ff)
     own_spot = pl.ds(aligned(at.hi * MOST, 16), MOST)
+
     for j in range(ranks):
         for hh in range(his):
             e, peer = at.member(j, hh)
             rows = grow_ref.at[pl.ds(aligned(e * MOST, 16), MOST)]
             spot = g_ref.at[at.l, at.f, own_spot]
-            sources = (wg_hbm.at[e], wu_hbm.at[e], wd_hbm.at[e])
             if j == 0 and hh == 0:
                 pltpu.make_async_copy(rows, spot, gr.at[at.m]).start()
+            else:
+                send(rows, spot, gs.at[j * his + hh], gr.at[at.m], peer)
+
+    def dispatch():
+        for j in range(ranks):
+            for hh in range(his):
+                e, peer = at.member(j, hh)
+                sources = (wg_hbm.at[e], wu_hbm.at[e], wd_hbm.at[e])
                 for w in range(3):
-                    pltpu.make_async_copy(
-                        sources[w], w_ref.at[w, own_rows, own_cols], wr.at[at.m, w]
-                    ).start()
-            else:
-                k = j * his + hh
-                send(rows, spot, gs.at[k], gr.at[at.m], peer)
-                for w in range(3):
-                    send(
-                        sources[w],
-                        w_ref.at[w, own_rows, own_cols],
-                        ws.at[k, w],
-                        wr.at[at.m, w],
-                        peer,
+                    first = aligned(w * his * ff + at.hi * ff, 128)
+                    spot = (
+                        wd_ref.at[own_rows, own_cols]
+                        if w == 2
+                        else wgu_ref.at[own_rows, pl.ds(first, ff)]
                     )
+                    if j == 0 and hh == 0:
+                        pltpu.make_async_copy(sources[w], spot, wr.at[at.m, w]).start()
+                    else:
+                        send(sources[w], spot, ws.at[j * his + hh, w], wr.at[at.m, w], peer)
 
     pos = token_places(len_ref, at).astype(F32)
     half_dim = HEAD_DIM // 2
@@ -992,6 +1000,8 @@
             lo * (1 - at.hi) + at.l3,
         ):
             settle(p_ref.at[g2, f2], agr.at[g2, f2])
+
+    dispatch()
 
     groups = p_ref.shape[0]
     for g2 in range(groups):
@@ -1153,23 +1163,24 @@
         gates_ref[e] = jnp.broadcast_to(row, (8, 128))
 
 
-    for j in range(ranks):
+    def give(j):
         for hh in range(his):
             e, peer = at.member(j, hh)
             k = j * his + hh
             rows = x_ref.at[pl.ds(aligned(e * MOST, 16), MOST)]
             spot = xb_ref.at[at.f, at.l, own_spot]
+            line = gb_ref.at[at.f, at.l, at.hi]
             if k == 0:
                 pltpu.make_async_copy(rows, spot, xr.at[at.m]).start()
-                pltpu.make_async_copy(
-                    gates_ref.at[e], gb_ref.at[at.f, at.l, at.hi], tr.at[at.m]
-                ).start()
+                pltpu.make_async_copy(gates_ref.at[e], line, tr.at[at.m]).start()
             else:
                 send(rows, spot, xs.at[k], xr.at[at.m], peer)
-                send(
-                    gates_ref.at[e], gb_ref.at[at.f, at.l, at.hi], ts.at[k], tr.at[at.m], peer
-                )
-    acc_ref[...] = jnp.zeros_like(acc_ref)
+                send(gates_ref.at[e], line, ts.at[k], tr.at[at.m], peer)
+
+    give(0)
+    give(1)
+    accgu_ref[...] = jnp.zeros_like(accgu_ref)
+    accd_ref[...] = jnp.zeros_like(accd_ref)
 
     def take(j):
         fj = xor4(at.f, j)
@@ -1195,6 +1206,12 @@
         settle(gb_ref.at[fj, at.l1], tqr.at[fj, 0])
         settle(xb_ref.at[fj, at.l3], qr.at[fj, 2])
         settle(gb_ref.at[fj, at.l3], tqr.at[fj, 2])
+        slot_of_chunk = lax.rem(j, 2)
+
+        @pl.when(j >= 2)
+        def _():
+            settle(op_ref.at[slot_of_chunk], last_sem.at[slot_of_chunk])
+
         diagonal = lax.broadcasted_iota(jnp.int32, (MOST, 128), 0) == lane_iota(MOST)
         pair_rows = 2 * his * MOST
 
@@ -1212,16 +1229,20 @@
                 ],
                 axis=0,
             )
-            d_exp = (g.astype(F32) * gate).astype(BF16)
-            wg = w_ref[0]
-            wu = w_ref[1]
-            wd = w_ref[2]
-            a = mm(x, wg)
-            b = mm(x, wu)
+            these = pl.ds(aligned(i * pair_rows, 16), pair_rows)
+            grow_ref[these, :] = (g.astype(F32) * gate).astype(BF16)
+            wgu = wgu_ref[...]
+            wd = wd_ref[...]
+            ab = mm(x, wgu)
+            inner = ab.shape[1] // 2
+            a = ab[:, :inner]
+            b = ab[:, inner:]
             sig = 1.0 / (1.0 + jnp.exp(-a))
-            hidden = (a * sig * b).astype(BF16)
+            act = a * sig
+            hidden = (act * b).astype(BF16)
+            hid_ref[these, :] = hidden
             shape = (2, his * MOST, width)
-            op_ref[fj, l2] = mm(hidden, wd, NT).astype(BF16).reshape(shape)
+            op_ref[slot_of_chunk, l2] = mm(hidden, wd, NT).astype(BF16).reshape(shape)
             dh_raw = mm(g, wd)
             d_route = jnp.sum(hidden.astype(F32) * dh_raw, axis=1, keepdims=True)
             for i2 in range(2):
@@ -1234,16 +1255,20 @@
                     )
                     dgp_ref[fj, 2 * i + i2, h] = jnp.broadcast_to(line, (8, 128))
             dh = dh_raw * gate
-            d_up = (dh * a * sig).astype(BF16)
-            d_gate = (dh * b * sig * (1.0 + a * (1.0 - sig))).astype(BF16)
-            od_ref[fj, l2] = (mm(d_gate, wg, NT) + mm(d_up, wu, NT)).astype(BF16).reshape(shape)
-            acc_ref[0] += mm(x, d_gate, TN)
-            acc_ref[1] += mm(x, d_up, TN)
-            acc_ref[2] += mm(d_exp, hidden, TN)
+            d_up = (dh * act).astype(BF16)
+            d_gate = (dh * b * (sig + act * (1.0 - sig))).astype(BF16)
+            dgu = jnp.concatenate([d_gate, d_up], axis=1)
+            dgu_ref[these, :] = dgu
+            od_ref[fj, l2] = mm(dgu, wgu, NT).astype(BF16).reshape(shape)
             return 0
 
         lax.fori_loop(0, lo // 2, rows_of, 0)
-        pltpu.make_async_copy(op_ref.at[fj], op_hbm.at[fj], last_sem.at[fj]).start()
+        x_all = xb_ref[fj].reshape(lo * his * MOST, width)
+        accgu_ref[...] += mm(x_all, dgu_ref[...], TN)
+        accd_ref[...] += mm(grow_ref[...], hid_ref[...], TN)
+        pltpu.make_async_copy(
+            op_ref.at[slot_of_chunk], op_hbm.at[fj], last_sem.at[slot_of_chunk]
+        ).start()
 
     def to_core(j):
         fj = xor4(at.f, j)
@@ -1298,41 +1323,47 @@
                 pl.when(j > 0)(away)
 
     take(0)
-    take(1)
+    pass_on(0)
     settle(g_ref.at[at.l1], gqr.at[0])
     settle(g_ref.at[at.l3], gqr.at[2])
-    for f2 in range(ranks):
-        for h2 in range(his):
-            for w in range(3):
-                block = w_ref.at[
-                    w, f2 * head_rows : (f2 + 1) * head_rows, h2 * ff : (h2 + 1) * ff
-                ]
-                settle(block, wr.at[f2 * his + h2, w])
+    for k in range(1, E):
+        settle(grow_ref.at[0:MOST], gs.at[k])
+    for m in range(E):
+        for w in range(3):
+            settle(wd_ref.at[0:head_rows, 0:ff], wr.at[m, w])
+    give(2)
 
     def step(t, _):
-        @pl.when(t < ranks)
+        @pl.when(t + 1 < ranks)
         def _():
-            pass_on(t)
-            compute(t)
-            to_core(t)
-
-        @pl.when(t + 2 < ranks)
+            take(t + 1)
+
+        @pl.when(t == 1)
         def _():
-            take(t + 2)
-
-        @pl.when((t >= 1) & (t <= ranks))
+            give(3)
+
+        compute(t)
+        to_core(t)
+
+        @pl.when(t + 1 < ranks)
         def _():
-            to_side(t - 1)
-
-        @pl.when(t >= 2)
+            pass_on(t + 1)
+
+        to_side(t)
+
+        @pl.when(t >= 1)
         def _():
-            to_home(t - 2)
+            to_home(t - 1)
 
         return 0
 
-    lax.fori_loop(0, ranks + 2, step, 0)
-
-    gw_ref[...] = acc_ref[...].astype(BF16)
+    lax.fori_loop(0, ranks, step, 0)
+    to_home(ranks - 1)
+
+    inner = wd_ref.shape[1]
+    gw_ref[0] = accgu_ref[:, :inner].astype(BF16)
+    gw_ref[1] = accgu_ref[:, inner:].astype(BF16)
+    gw_ref[2] = accd_ref[...].astype(BF16)
     pltpu.make_async_copy(gw_ref, gw_hbm, last_sem.at[4]).start()
 
     for m in range(E):
@@ -1354,11 +1385,10 @@
         settle(tail, hs)
 
     for k in range(1, E):
-        settle(grow_ref.at[0:MOST], gs.at[k])
         settle(x_ref.at[0:MOST], xs.at[k])
         settle(gates_ref.at[0], ts.at[k])
         for w in range(3):
-            settle(w_ref.at[0, 0:head_rows, 0:ff], ws.at[k, w])
+            settle(wd_ref.at[0:head_rows, 0:ff], ws.at[k, w])
     for i in range(3):
         settle(g_ref.at[0], gas.at[i])
     for f2 in range(ranks):
@@ -1370,13 +1400,14 @@
             settle(dr1_ref.at[0, 0], t1s.at[f2, i])
         settle(r2_ref.at[0], d2s.at[f2])
         settle(dr2_ref.at[0], t2s.at[f2])
-        settle(op_ref.at[0], last_sem.at[f2])
     for j in range(ranks):
         for hh in range(his):
             if j or hh:
                 m = at.member(j, hh)[0]
                 settle(back_ref.at[0], bs.at[m])
                 settle(dgb_ref.at[0], tbs.at[m])
+    settle(op_ref.at[0], last_sem.at[0])
+    settle(op_ref.at[1], last_sem.at[1])
     settle(gw_ref, last_sem.at[4])
     settle(back_ref, last_sem.at[5])
     settle(dgb_ref, last_sem.at[6])
@@ -1422,18 +1453,22 @@
             vm((ROWS, width), BF16),
             vm((ROWS, width), BF16),
             vm((E, 8, 128), F32),
-            vm((3, width, ff * his), BF16),
+            vm((width, 2 * ff * his), BF16),
+            vm((width, ff * his), BF16),
             vm((lo, ranks) + rows, BF16),
             vm((ranks, lo) + rows, BF16),
             vm((ranks, lo, his, 8, 128), F32),
             vm((ranks, lo) + rows, BF16),
-            vm((ranks, lo) + rows, BF16),
+            vm((2, lo) + rows, BF16),
             vm((ranks, 2) + rows, BF16),
             vm((ranks,) + rows, BF16),
             vm((ranks, lo, his, 8, 128), F32),
             vm((ranks, 2, his, 8, 128), F32),
             vm((ranks, his, 8, 128), F32),
-            vm((3, width, ff * his), F32),
+            vm((width, 2 * ff * his), F32),
+            vm((width, ff * his), F32),
+            vm((lo * rows[0], ff * his), BF16),
+            vm((lo * rows[0], 2 * ff * his), BF16),
             vm((3, width, ff * his), BF16),
             vm((E, MOST, width), BF16),
             vm((E, 8, 128), F32),

time: 319 us -> 285 us (0.89)
  Pallas kernels: 310 us -> 276 us
    pallas_call x1, Pallas kernels: 200 us -> 169 us  [ahead(): pl.pallas_call(ahead_kernel, out_shape=[sds(*k) for k in kept + results],...]
where the time goes in v5:
time: 285 us
  Pallas kernels  276 us (97%)
  local copies, waits for them, and re-layouts  8.03 us (3%)
    pallas_call x1, Pallas kernels, ahead(): pl.pallas_call(ahead_kernel, out_shape=[sds(*k) for k in kept + results],...  169 us
    pallas_call x1, Pallas kernels, end(): pl.pallas_call(end_kernel, out_shape=[sds((TOK_DEV, width), BF16), sds((T...  104 us
    unnamed x23, local copies, waits for them, and re-layouts  8.03 us

profile of v5, /device:TPU:0, one launch (start us, length us, event | category | flops | bytes accessed | tf_op | source)
XLA Modules:
  0.0 284.9 jit_solution(3656613449569036228)
XLA Ops:
  0.7 168.8 %ahead.1 = (bf16[4,768,768]{2,1,0:T(8,128)(2,1)}, f32[768,128]{1,0:T(8,128)}, bf16[256,768]{1,0:T(8,128)(2,1)}, bf16[320,768]{1,0:T(8,128)(2,1)}, bf16[576,768]{...) custom-call(s32[1,8]{1,0:T(1,128)} %len_ref.1, ...), custom_call_target="tpu_custom_call" | custom-call | tf_op jit(solution)/shard_map/ahead/pallas_call | solution.py:1443
  169.5 0.0 copy-start
  169.5 0.0 copy-start.2
  169.5 104.1 %end.1 = (bf16[320,768]{1,0:T(8,128)(2,1)}, f32[320,768]{1,0:T(8,128)}, f32[12,320]{1,0:T(8,128)}, f32[320,768]{1,0:T(8,128)}, bf16[256,768]{1,0:T(8,128)(2,1)},...) custom-call(bf16[320,768]{1,0:T(8,128)(2,1)} %cot_ref.3, bf16[320,768]{1,0:T(8,128)(2,1)} %tok_ref.5, ...), custom_call_target="tpu_custom_call" | custom-call | tf_op jit(solution)/shard_map/end/pallas_call | solution.py:1976
  273.6 0.0 copy-done
  273.6 0.0 copy-done.2
  273.6 0.0 copy-start.1
  273.6 1.7 copy-done.1
  275.3 0.0 copy-start.3
  275.3 1.2 copy-done.3
  276.5 0.0 copy-start.4
  276.5 1.2 copy-done.4
  277.7 0.0 copy-start.5
  277.7 1.0 copy-done.5
  278.7 0.0 copy-start.6
  278.7 1.0 copy-done.6
  279.6 0.0 copy-start.7
  279.6 3.2 %store.1 = (f32[8,192,256]{2,1,0:T(8,128)}, f32[8,192,256]{2,1,0:T(8,128)}, f32[8,192,256]{2,1,0:T(8,128)}, f32[192,96]{1,0:T(8,128)}, f32[192,96]{1,0:T(8,128)}...) custom-call(bf16[8,3,192,256]{3,2,1,0:T(8,128)(2,1)S(1)} %copy-done., ...), custom_call_target="tpu_custom_call" | custom-call | tf_op jit(solution)/shard_map/store/pallas_call | solution.py:2104
  282.9 0.0 copy-done.7
  282.9 0.8 copy.37
  283.6 0.0 copy-done.8
  283.7 0.6 copy.38
  284.3 0.0 copy-done.9
  284.3 0.6 copy.39
  (2 shorter events, 0.0 us)
Async XLA Ops:
  169.5 104.1 %copy-start = (bf16[320,768]{1,0:T(8,128)(2,1)S(1)}, bf16[320,768]{1,0:T(8,128)(2,1)}, u32[]{:S(2)}) copy-start(bf16[320,768]{1,0:T(8,128)(2,1)} %tok_ref.5) | copy-start | bytes 1474564
  169.5 104.1 %copy-start.2 = (f32[576,128]{1,0:T(8,128)S(1)}, f32[576,128]{1,0:T(8,128)}, u32[]{:S(2)}) copy-start(f32[576,128]{1,0:T(8,128)} %get-tuple-element.68.rest_7_.inv1_ref) | copy-start | bytes 884740
  273.6 1.7 copy-start.1
  275.3 1.2 copy-start.3
  276.5 1.2 copy-start.4
  277.7 1.0 copy-start.5
  278.7 1.0 copy-start.6
  279.6 3.2 %copy-start.7 = (bf16[320,768]{1,0:T(8,128)(2,1)S(1)}, bf16[320,768]{1,0:T(8,128)(2,1)}, u32[]{:S(2)}) copy-start(bf16[320,768]{1,0:T(8,128)(2,1)} %get-tuple-element.114) | copy-start | bytes 1474564
  279.6 4.0 %copy-start.8 = (f32[12,320]{1,0:T(8,128)S(1)}, f32[12,320]{1,0:T(8,128)}, u32[]{:S(2)}) copy-start(f32[12,320]{1,0:T(8,128)} %get-tuple-element.84) | copy-start | bytes 46084
  279.6 4.6 %copy-start.9 = (f32[16,128]{1,0:T(8,128)S(1)}, f32[16,128]{1,0:T(8,128)}, u32[]{:S(2)}) copy-start(f32[16,128]{1,0:T(8,128)} %get-tuple-element.92) | copy-start | bytes 24580

commit v6 on v5

--- a/solution.py
+++ b/solution.py
@@ -1216,6 +1216,7 @@
         pair_rows = 2 * his * MOST
 
         def rows_of(i, _):
+            pl.when((i == 1) & (j >= 1))(lambda: to_side(j - 1))
             l2 = pl.ds(2 * i, 2)
             x = xb_ref[fj, l2].reshape(pair_rows, width)
             g = g_ref[l2, fj].reshape(pair_rows, width)
@@ -1349,8 +1350,6 @@
         def _():
             pass_on(t + 1)
 
-        to_side(t)
-
         @pl.when(t >= 1)
         def _():
             to_home(t - 1)
@@ -1358,6 +1357,7 @@
         return 0
 
     lax.fori_loop(0, ranks, step, 0)
+    to_side(ranks - 1)
     to_home(ranks - 1)
 
     inner = wd_ref.shape[1]
@@ -1774,26 +1774,23 @@
             dk_ref[pl.ds(first, keys), span] += dk * scale
             dv_ref[pl.ds(first, keys), span] += dv
 
-        @pl.when(p == 2)
-        def _():
-            for j in range(ranks):
-                fj = xor4(at.f, j)
-                settle(r2o_ref.at[fj], o2r.at[fj])
-                add(opl_ref.at[fj, 0], r2o_ref.at[fj])
-                for hh in range(his):
-                    m, peer = at.member(j, hh)
-                    hi = flip(at.hi, hh)
-                    rows = opl_ref.at[fj, 0, pl.ds(aligned(hi * MOST, 16), MOST)]
-                    if j or hh:
-                        send(rows, outb_ref.at[at.m], obs.at[m], obr.at[at.m], peer)
-                    else:
-                        pltpu.make_async_copy(rows, outb_ref.at[at.m], obr.at[at.m]).start()
-
         return 0
 
     lax.fori_loop(0, HEADS // 2, pair, 0)
 
     ready("cos", "sin", "n1", "inv1", "halo", "part")
+
+    for j in range(ranks):
+        fj = xor4(at.f, j)
+        settle(r2o_ref.at[fj], o2r.at[fj])
+        add(opl_ref.at[fj, 0], r2o_ref.at[fj])
+        for hh in range(his):
+            m, peer = at.member(j, hh)
+            rows = opl_ref.at[fj, 0, pl.ds(aligned(flip(at.hi, hh) * MOST, 16), MOST)]
+            if j or hh:
+                send(rows, outb_ref.at[at.m], obs.at[m], obr.at[at.m], peer)
+            else:
+                pltpu.make_async_copy(rows, outb_ref.at[at.m], obr.at[at.m]).start()
 
     def unturn(i, _):
         span = pl.ds(pl.multiple_of(i * 256, 256), 256)
@@ -2044,16 +2041,19 @@
 
 
 def store_kernel(
-    t_ref,
-    fin_ref,
-    dres_ref,
-    down_ref,
-    back_ref,
-    tok_ref,
-    inv1_ref,
-    gate_ref,
-    up_ref,
-    downw_ref,
+    t_hbm,
+    fin_hbm,
+    dres_hbm,
+    down_hbm,
+    back_hbm,
+    tok_hbm,
+    inv1_hbm,
+    out_from,
+    gprev_from,
+    gmix_from,
+    gate_hbm,
+    up_hbm,
+    downw_hbm,
     gq_ref,
     gk_ref,
     gv_ref,
@@ -2063,12 +2063,64 @@
     vconst_ref,
     gain1_ref,
     gain2_ref,
+    gtok_hbm,
+    out_to,
+    gprev_to,
+    gmix_ref,
+    t_ref,
+    wide_ref,
+    fin_ref,
+    dres_ref,
+    down_ref,
+    back_ref,
+    tok_ref,
+    inv1_ref,
     gtok_ref,
+    mixin_ref,
+    out_ref,
+    gprev_ref,
+    t_sem,
+    wide_sem,
+    in_sem,
+    gtok_sem,
+    pass_sem,
 ):
+    pairs = [
+        (dres_hbm, dres_ref),
+        (down_hbm, down_ref),
+        (back_hbm, back_ref),
+        (tok_hbm, tok_ref),
+        (inv1_hbm, inv1_ref),
+        (fin_hbm, fin_ref),
+        (gmix_from, mixin_ref),
+        (out_from, out_ref),
+        (gprev_from, gprev_ref),
+    ]
+    for i, (src, dst) in enumerate(pairs):
+        pltpu.make_async_copy(src, dst, in_sem.at[i]).start()
     for e in range(E):
-        gate_ref[e] = t_ref[e, 0].astype(F32)
-        up_ref[e] = t_ref[e, 1].astype(F32)
-        downw_ref[e] = t_ref[e, 2].astype(F32)
+        pltpu.make_async_copy(t_hbm.at[e], t_ref.at[e], t_sem.at[e]).start()
+    for i in range(5):
+        settle(pairs[i][1], in_sem.at[i])
+    width = tok_ref.shape[1]
+    inv1 = inv1_ref[HALO:, 0:1]
+    unit = tok_ref[...].astype(F32) * inv1
+    m = jnp.concatenate(
+        [down_ref[: TOK_DEV - HALO, :], down_ref[TOK_DEV - HALO :, :] + back_ref[...]], axis=0
+    )
+    d_dealt = inv1 * (m - unit * jnp.mean(m * unit, axis=1, keepdims=True))
+    gtok_ref[...] = dres_ref[...] + d_dealt.astype(BF16).astype(F32)
+    pltpu.make_async_copy(gtok_ref, gtok_hbm, gtok_sem).start()
+    settle(out_ref, in_sem.at[7])
+    pltpu.make_async_copy(out_ref, out_to, pass_sem.at[0]).start()
+    settle(gprev_ref, in_sem.at[8])
+    pltpu.make_async_copy(gprev_ref, gprev_to, pass_sem.at[1]).start()
+    for e in range(E):
+        settle(t_ref.at[e], t_sem.at[e])
+        wide_ref[e] = t_ref[e].astype(F32)
+        for w, out in enumerate((gate_hbm, up_hbm, downw_hbm)):
+            pltpu.make_async_copy(wide_ref.at[e, w], out.at[e], wide_sem.at[e, w]).start()
+    settle(fin_ref, in_sem.at[5])
     head_rows, part_cols = gq_ref.shape
     for w, ref in enumerate((gq_ref, gk_ref, gv_ref, go_ref)):
         ref[...] = fin_ref[0:head_rows, w * part_cols : (w + 1) * part_cols]
@@ -2087,20 +2139,23 @@
     gain2_ref[...] = flat[SMALL_G1 + 1 : SMALL_G1 + 2]
     vconst_ref[...] = flat[SMALL_VC : SMALL_VC + CONSTS]
     const_ref[...] = flat[SMALL_C : SMALL_C + 2 * CONSTS]
-    width = tok_ref.shape[1]
-    inv1 = inv1_ref[HALO:, 0:1]
-    unit = tok_ref[...].astype(F32) * inv1
-    m = jnp.concatenate(
-        [down_ref[: TOK_DEV - HALO, :], down_ref[TOK_DEV - HALO :, :] + back_ref[...]], axis=0
-    )
-    d_dealt = inv1 * (m - unit * jnp.mean(m * unit, axis=1, keepdims=True))
-    gtok_ref[...] = dres_ref[...] + d_dealt.astype(BF16).astype(F32)
-
-
-def store(t, fin, dres, down, back, tok, inv1, groups, ranks):
+    settle(mixin_ref, in_sem.at[6])
+    gmix_ref[...] = mixin_ref[0:EXPERTS_ALL, 0:EXPERTS_ALL]
+    settle(out_ref, pass_sem.at[0])
+    settle(gprev_ref, pass_sem.at[1])
+    settle(gtok_ref, gtok_sem)
+    for e in range(E):
+        for w in range(3):
+            settle(wide_ref.at[e, w], wide_sem.at[e, w])
+
+
+def store(t, fin, dres, down, back, tok, inv1, out, gprev, gmix, groups, ranks):
     width = tok.shape[1]
     rows, cols = t.shape[2:]
     per = width // (groups * ranks)
+    any_spec = pl.BlockSpec(memory_space=pl.ANY)
+    dma = pltpu.SemaphoreType.DMA
+    vm = pltpu.VMEM
     return pl.pallas_call(
         store_kernel,
         out_shape=[sds((E, rows, cols), F32)] * 3
@@ -2112,12 +2167,34 @@
             sds((1, per), F32),
             sds((1, per), F32),
             sds(tok.shape, F32),
+            sds(out.shape, BF16),
+            sds(gprev.shape, F32),
+            sds((EXPERTS_ALL, EXPERTS_ALL), F32),
         ],
-        in_specs=whole(7),
-        out_specs=whole(13),
-        compiler_params=params(48),
+        in_specs=[any_spec] * 10,
+        out_specs=[any_spec] * 3 + whole(9) + [any_spec] * 3 + whole(1),
+        scratch_shapes=[
+            vm(t.shape, BF16),
+            vm(t.shape, F32),
+            vm(fin.shape, F32),
+            vm(dres.shape, F32),
+            vm(down.shape, F32),
+            vm(back.shape, BF16),
+            vm(tok.shape, BF16),
+            vm(inv1.shape, F32),
+            vm(tok.shape, F32),
+            vm(gmix.shape, F32),
+            vm(out.shape, BF16),
+            vm(gprev.shape, F32),
+            dma((E,)),
+            dma((E, 3)),
+            dma((9,)),
+            dma,
+            dma((2,)),
+        ],
+        compiler_params=params(63),
         name="store",
-    )(t, fin, dres, down, back, tok, inv1)
+    )(t, fin, dres, down, back, tok, inv1, out, gprev, gmix)
 
 
 def fast_device(
@@ -2183,8 +2260,25 @@
         *outs[:kept],
     )
     inv1 = by_name(outs[:kept])["inv1"]
-    gate, up, downw, gq, gk, gv, go, router, const, vconst, gain1, gain2, grad_tokens = store(
-        tiles, fin, dres, down, back, tokens, inv1, groups, ranks
+    (
+        gate,
+        up,
+        downw,
+        gq,
+        gk,
+        gv,
+        go,
+        router,
+        const,
+        vconst,
+        gain1,
+        gain2,
+        grad_tokens,
+        output,
+        gprev,
+        gmix,
+    ) = store(
+        tiles, fin, dres, down, back, tokens, inv1, output, gprev, gmix, groups, ranks
     )
     return (
         output,
@@ -2197,7 +2291,7 @@
         go,
         gain2[0],
         router.T,
-        gmix[:EXPERTS_ALL, :EXPERTS_ALL],
+        gmix,
         const.T,
         vconst.T,
         gate,

time: 285 us -> 280 us (0.982)
  local copies, waits for them, and re-layouts: 8.03 us -> 0 us
  Pallas kernels: 276 us -> 279 us
    unnamed x23 -> x0, local copies, waits for them, and re-layouts: 8.03 us -> none
    pallas_call x1, Pallas kernels: 3.21 us -> 6.34 us  [store(): pl.pallas_call(store_kernel, out_shape=[sds((E, rows, cols), F32)] * 3 +...]
where the time goes in v6:
time: 280 us
  Pallas kernels  279 us (100%)
    pallas_call x1, Pallas kernels, ahead(): pl.pallas_call(ahead_kernel, out_shape=[sds(*k) for k in kept + results],...  167 us
    pallas_call x1, Pallas kernels, end(): pl.pallas_call(end_kernel, out_shape=[sds((TOK_DEV, width), BF16), sds((T...  105 us
    pallas_call x1, Pallas kernels, store(): pl.pallas_call(store_kernel, out_shape=[sds((E, rows, cols), F32)] * 3 +...  6.34 us

profile of v6, /device:TPU:0, one launch (start us, length us, event | category | flops | bytes accessed | tf_op | source)
XLA Modules:
  0.0 279.6 jit_solution(11592207890872649882)
XLA Ops:
  0.7 167.2 %ahead.1 = (bf16[4,768,768]{2,1,0:T(8,128)(2,1)}, f32[768,128]{1,0:T(8,128)}, bf16[256,768]{1,0:T(8,128)(2,1)}, bf16[320,768]{1,0:T(8,128)(2,1)}, bf16[576,768]{...) custom-call(s32[1,8]{1,0:T(1,128)} %len_ref.1, ...), custom_call_target="tpu_custom_call" | custom-call | tf_op jit(solution)/shard_map/ahead/pallas_call | solution.py:1443
  167.9 105.2 %end.1 = (bf16[320,768]{1,0:T(8,128)(2,1)}, f32[320,768]{1,0:T(8,128)}, f32[12,320]{1,0:T(8,128)}, f32[320,768]{1,0:T(8,128)}, bf16[256,768]{1,0:T(8,128)(2,1)},...) custom-call(bf16[320,768]{1,0:T(8,128)(2,1)} %cot_ref.3, bf16[320,768]{1,0:T(8,128)(2,1)} %tok_hbm.1, ...), custom_call_target="tpu_custom_call" | custom-call | tf_op jit(solution)/shard_map/end/pallas_call | solution.py:1973
  273.0 6.3 %store.1 = (f32[8,192,256]{2,1,0:T(8,128)}, f32[8,192,256]{2,1,0:T(8,128)}, f32[8,192,256]{2,1,0:T(8,128)}, f32[192,96]{1,0:T(8,128)}, f32[192,96]{1,0:T(8,128)}...) custom-call(bf16[8,3,192,256]{3,2,1,0:T(8,128)(2,1)} %get-tuple-elem, ...), custom_call_target="tpu_custom_call" | custom-call | tf_op jit(solution)/shard_map/store/pallas_call | solution.py:2159

commit v7 on v6

--- a/solution.py
+++ b/solution.py
@@ -1200,76 +1200,77 @@
         send(xb_ref.at[fj, at.l2], xb_ref.at[fj, at.l2], qs.at[fj, 2], qr.at[fj, 2], core)
         send(gb_ref.at[fj, at.l2], gb_ref.at[fj, at.l2], tqs.at[fj, 2], tqr.at[fj, 2], core)
 
+    diagonal = lax.broadcasted_iota(jnp.int32, (MOST, 128), 0) == lane_iota(MOST)
+
+    def arithmetic(x, g, gate, these):
+        grow_ref[these, :] = (g.astype(F32) * gate).astype(BF16)
+        wgu = wgu_ref[...]
+        ab = mm(x, wgu)
+        inner = ab.shape[1] // 2
+        a = ab[:, :inner]
+        b = ab[:, inner:]
+        sig = 1.0 / (1.0 + jnp.exp(-a))
+        act = a * sig
+        hidden = (act * b).astype(BF16)
+        hid_ref[these, :] = hidden
+        dh_raw = mm(g, wd_ref[...])
+        d_route = jnp.sum(hidden.astype(F32) * dh_raw, axis=1, keepdims=True)
+        lines = []
+        for n in range(x.shape[0] // MOST):
+            line = jnp.where(diagonal, d_route[n * MOST : (n + 1) * MOST], 0.0)
+            lines.append(jnp.broadcast_to(jnp.sum(line, axis=0, keepdims=True), (8, 128)))
+        dh = dh_raw * gate
+        d_up = (dh * act).astype(BF16)
+        d_gate = (dh * b * (sig + act * (1.0 - sig))).astype(BF16)
+        dgu = jnp.concatenate([d_gate, d_up], axis=1)
+        dgu_ref[these, :] = dgu
+        return mm(dgu, wgu, NT).astype(BF16), lines
+
+    def column(line):
+        return pick(jnp.broadcast_to(line, (MOST, 128)), diagonal)
+
     def compute(j):
         fj = xor4(at.f, j)
         settle(xb_ref.at[fj, at.l1], qr.at[fj, 0])
         settle(gb_ref.at[fj, at.l1], tqr.at[fj, 0])
         settle(xb_ref.at[fj, at.l3], qr.at[fj, 2])
         settle(gb_ref.at[fj, at.l3], tqr.at[fj, 2])
-        slot_of_chunk = lax.rem(j, 2)
-
-        @pl.when(j >= 2)
-        def _():
-            settle(op_ref.at[slot_of_chunk], last_sem.at[slot_of_chunk])
-
-        diagonal = lax.broadcasted_iota(jnp.int32, (MOST, 128), 0) == lane_iota(MOST)
         pair_rows = 2 * his * MOST
 
         def rows_of(i, _):
-            pl.when((i == 1) & (j >= 1))(lambda: to_side(j - 1))
             l2 = pl.ds(2 * i, 2)
             x = xb_ref[fj, l2].reshape(pair_rows, width)
             g = g_ref[l2, fj].reshape(pair_rows, width)
             gate = jnp.concatenate(
                 [
-                    pick(
-                        jnp.broadcast_to(gb_ref[fj, 2 * i + i2, h][0:1, :], (MOST, 128)), diagonal
-                    )
+                    column(gb_ref[fj, 2 * i + i2, h][0:1, :])
                     for i2 in range(2)
                     for h in range(his)
                 ],
                 axis=0,
             )
             these = pl.ds(aligned(i * pair_rows, 16), pair_rows)
-            grow_ref[these, :] = (g.astype(F32) * gate).astype(BF16)
-            wgu = wgu_ref[...]
-            wd = wd_ref[...]
-            ab = mm(x, wgu)
-            inner = ab.shape[1] // 2
-            a = ab[:, :inner]
-            b = ab[:, inner:]
-            sig = 1.0 / (1.0 + jnp.exp(-a))
-            act = a * sig
-            hidden = (act * b).astype(BF16)
-            hid_ref[these, :] = hidden
-            shape = (2, his * MOST, width)
-            op_ref[slot_of_chunk, l2] = mm(hidden, wd, NT).astype(BF16).reshape(shape)
-            dh_raw = mm(g, wd)
-            d_route = jnp.sum(hidden.astype(F32) * dh_raw, axis=1, keepdims=True)
-            for i2 in range(2):
-                for h in range(his):
-                    first = (i2 * his + h) * MOST
-                    line = jnp.sum(
-                        jnp.where(diagonal, d_route[first : first + MOST], 0.0),
-                        axis=0,
-                        keepdims=True,
-                    )
-                    dgp_ref[fj, 2 * i + i2, h] = jnp.broadcast_to(line, (8, 128))
-            dh = dh_raw * gate
-            d_up = (dh * act).astype(BF16)
-            d_gate = (dh * b * (sig + act * (1.0 - sig))).astype(BF16)
-            dgu = jnp.concatenate([d_gate, d_up], axis=1)
-            dgu_ref[these, :] = dgu
-            od_ref[fj, l2] = mm(dgu, wgu, NT).astype(BF16).reshape(shape)
+            dx, lines = arithmetic(x, g, gate, these)
+            for n, line in enumerate(lines):
+                dgp_ref[fj, 2 * i + n // his, n % his] = line
+            od_ref[fj, l2] = dx.reshape((2, his * MOST, width))
             return 0
 
         lax.fori_loop(0, lo // 2, rows_of, 0)
-        x_all = xb_ref[fj].reshape(lo * his * MOST, width)
+
+    def outputs_of(j):
+        fj = xor4(at.f, j)
+        slot = lax.rem(j, 2)
+        pl.when(j >= 2)(lambda: settle(op_ref.at[slot], last_sem.at[slot]))
+        op_ref[slot] = mm(hid_ref[...], wd_ref[...], NT).astype(BF16).reshape(
+            (lo, his * MOST, width)
+        )
+        pltpu.make_async_copy(op_ref.at[slot], op_hbm.at[fj], last_sem.at[slot]).start()
+
+    def weights_of(j):
+        x_all = xb_ref[xor4(at.f, j)].reshape(lo * his * MOST, width)
         accgu_ref[...] += mm(x_all, dgu_ref[...], TN)
         accd_ref[...] += mm(grow_ref[...], hid_ref[...], TN)
-        pltpu.make_async_copy(
-            op_ref.at[slot_of_chunk], op_hbm.at[fj], last_sem.at[slot_of_chunk]
-        ).start()
 
     def to_core(j):
         fj = xor4(at.f, j)
@@ -1323,6 +1324,91 @@
 
                 pl.when(j > 0)(away)
 
+    last = ranks - 1
+    fl = xor4(at.f, last)
+
+    def half(hh):
+        hi = flip(at.hi, hh)
+        return hi, pl.ds(aligned(hi * MOST, 16), MOST), (fl if hh == 0 else ranks)
+
+    def half_give(hh):
+        k = last * his + hh
+        e, peer = at.member(last, hh)
+        rows = x_ref.at[pl.ds(aligned(e * MOST, 16), MOST)]
+        send(rows, xb_ref.at[at.f, at.l, own_spot], xs.at[k], xr.at[at.m], peer)
+        send(gates_ref.at[e], gb_ref.at[at.f, at.l, at.hi], ts.at[k], tr.at[at.m], peer)
+
+    def half_take(hh):
+        hi, spot, n = half(hh)
+        m = fl * his + hi
+        rows, line = xb_ref.at[fl, at.l, spot], gb_ref.at[fl, at.l, hi]
+        settle(rows, xr.at[m])
+        settle(line, tr.at[m])
+        for i, peer in enumerate((core, side)):
+            send(rows, rows, qs.at[n, i], qr.at[n, i], peer)
+            send(line, line, tqs.at[n, i], tqr.at[n, i], peer)
+
+    def half_pass(hh):
+        hi, spot, n = half(hh)
+        rows, line = xb_ref.at[fl, at.l2, spot], gb_ref.at[fl, at.l2, hi]
+        settle(rows, qr.at[n, 1])
+        settle(line, tqr.at[n, 1])
+        send(rows, rows, qs.at[n, 2], qr.at[n, 2], core)
+        send(line, line, tqs.at[n, 2], tqr.at[n, 2], core)
+
+    half_rows = lo * MOST
+
+    def half_compute(hh):
+        hi, spot, n = half(hh)
+        for quarter, i in ((at.l1, 0), (at.l3, 2)):
+            settle(xb_ref.at[fl, quarter, spot], qr.at[n, i])
+            settle(gb_ref.at[fl, quarter, hi], tqr.at[n, i])
+        x = xb_ref[fl, :, spot].reshape(half_rows, width)
+        g = g_ref[:, fl, spot].reshape(half_rows, width)
+        gate = jnp.concatenate([column(gb_ref[fl, i, hi][0:1, :]) for i in range(lo)], axis=0)
+        dx, lines = arithmetic(x, g, gate, pl.ds(hh * half_rows, half_rows))
+        for i, line in enumerate(lines):
+            dgp_ref[fl, i, hi] = line
+        od_ref[fl, :, spot] = dx.reshape((lo, MOST, width))
+        for i, quarter in enumerate((at.l1, at.l3)):
+            send(
+                od_ref.at[fl, quarter, spot],
+                r1_ref.at[fl, i, spot],
+                d1s.at[n, i],
+                d1r.at[n, i],
+                core,
+            )
+            send(
+                dgp_ref.at[fl, quarter, hi],
+                dr1_ref.at[fl, i, hi],
+                t1s.at[n, i],
+                t1r.at[n, i],
+                core,
+            )
+
+    def half_side(hh):
+        hi, spot, n = half(hh)
+        settle(r1_ref.at[fl, 1, spot], d1r.at[n, 1])
+        add(od_ref.at[fl, at.l2, spot], r1_ref.at[fl, 1, spot])
+        send(od_ref.at[fl, at.l2, spot], r2_ref.at[fl, spot], d2s.at[n], d2r.at[n], side)
+        settle(dr1_ref.at[fl, 1, hi], t1r.at[n, 1])
+        dgp_ref[fl, at.l2, hi] += dr1_ref[fl, 1, hi]
+        send(dgp_ref.at[fl, at.l2, hi], dr2_ref.at[fl, hi], t2s.at[n], t2r.at[n], side)
+        settle(r1_ref.at[fl, 0, spot], d1r.at[n, 0])
+        add(od_ref.at[fl, at.l, spot], r1_ref.at[fl, 0, spot])
+        settle(dr1_ref.at[fl, 0, hi], t1r.at[n, 0])
+        dgp_ref[fl, at.l, hi] += dr1_ref[fl, 0, hi]
+
+    def half_home(hh):
+        hi, spot, n = half(hh)
+        m, peer = at.member(last, hh)
+        settle(r2_ref.at[fl, spot], d2r.at[n])
+        add(od_ref.at[fl, at.l, spot], r2_ref.at[fl, spot])
+        settle(dr2_ref.at[fl, hi], t2r.at[n])
+        dgp_ref[fl, at.l, hi] += dr2_ref[fl, hi]
+        send(od_ref.at[fl, at.l, spot], back_ref.at[at.m], bs.at[m], br.at[at.m], peer)
+        send(dgp_ref.at[fl, at.l, hi], dgb_ref.at[at.m], tbs.at[m], tbr.at[at.m], peer)
+
     take(0)
     pass_on(0)
     settle(g_ref.at[at.l1], gqr.at[0])
@@ -1335,30 +1421,61 @@
     give(2)
 
     def step(t, _):
-        @pl.when(t + 1 < ranks)
+        @pl.when(t + 1 < last)
         def _():
             take(t + 1)
 
         @pl.when(t == 1)
         def _():
-            give(3)
+            half_give(0)
+
+        @pl.when(t == last - 1)
+        def _():
+            half_take(0)
+            half_give(1)
 
         compute(t)
         to_core(t)
 
-        @pl.when(t + 1 < ranks)
+        @pl.when(t + 1 < last)
         def _():
             pass_on(t + 1)
+
+        pl.when(t == last - 1)(lambda: half_pass(0))
+        outputs_of(t)
+        to_side(t)
 
         @pl.when(t >= 1)
         def _():
             to_home(t - 1)
 
+        weights_of(t)
         return 0
 
-    lax.fori_loop(0, ranks, step, 0)
-    to_side(ranks - 1)
-    to_home(ranks - 1)
+    lax.fori_loop(0, last, step, 0)
+    half_take(1)
+    half_compute(0)
+    half_pass(1)
+    to_home(last - 1)
+    half_side(0)
+    half_compute(1)
+    half_home(0)
+    slot = last % 2
+    settle(op_ref.at[slot], last_sem.at[slot])
+    half_side(1)
+    for hh in range(his):
+        op_ref[slot, :, half(hh)[1]] = (
+            mm(hid_ref[hh * half_rows : (hh + 1) * half_rows, :], wd_ref[...], NT)
+            .astype(BF16)
+            .reshape((lo, MOST, width))
+        )
+    pltpu.make_async_copy(op_ref.at[slot], op_hbm.at[fl], last_sem.at[slot]).start()
+    half_home(1)
+    x_both = jnp.concatenate(
+        [xb_ref[fl, :, half(hh)[1]].reshape(half_rows, width) for hh in range(his)], axis=0
+    )
+    accgu_ref[...] += mm(x_both, dgu_ref[...], TN)
+    accd_ref[...] += mm(grow_ref[...], hid_ref[...], TN)
 
     inner = wd_ref.shape[1]
     gw_ref[0] = accgu_ref[:, :inner].astype(BF16)
@@ -1391,15 +1508,18 @@
             settle(wd_ref.at[0:head_rows, 0:ff], ws.at[k, w])
     for i in range(3):
         settle(g_ref.at[0], gas.at[i])
-    for f2 in range(ranks):
+    for j in range(ranks + 1):
+        n = xor4(at.f, j) if j < ranks else ranks
+        spot = pl.ds(0, MOST if j >= last else his * MOST)
+        lines = pl.ds(0, 1 if j >= last else his)
         for i in range(3):
-            settle(xb_ref.at[0, 0], qs.at[f2, i])
-            settle(gb_ref.at[0, 0], tqs.at[f2, i])
+            settle(xb_ref.at[0, 0, spot], qs.at[n, i])
+            settle(gb_ref.at[0, 0, lines], tqs.at[n, i])
         for i in range(2):
-            settle(r1_ref.at[0, 0], d1s.at[f2, i])
-            settle(dr1_ref.at[0, 0], t1s.at[f2, i])
-        settle(r2_ref.at[0], d2s.at[f2])
-        settle(dr2_ref.at[0], t2s.at[f2])
+            settle(r1_ref.at[0, 0, spot], d1s.at[n, i])
+            settle(dr1_ref.at[0, 0, lines], t1s.at[n, i])
+        settle(r2_ref.at[0, spot], d2s.at[n])
+        settle(dr2_ref.at[0, lines], t2s.at[n])
     for j in range(ranks):
         for hh in range(his):
             if j or hh:
@@ -1488,22 +1608,22 @@
             dma((3,)),
             dma((E,)),
             dma((E,)),
-            dma((4, 3)),
-            dma((4, 3)),
-            dma((4, 2)),
-            dma((4, 2)),
-            dma((4,)),
-            dma((4,)),
+            dma((ranks + 1, 3)),
+            dma((ranks + 1, 3)),
+            dma((ranks + 1, 2)),
+            dma((ranks + 1, 2)),
+            dma((ranks + 1,)),
+            dma((ranks + 1,)),
             dma((E,)),
             dma((E,)),
             dma((E,)),
             dma((E,)),
-            dma((4, 3)),
-            dma((4, 3)),
-            dma((4, 2)),
-            dma((4, 2)),
-            dma((4,)),
-            dma((4,)),
+            dma((ranks + 1, 3)),
+            dma((ranks + 1, 3)),
+            dma((ranks + 1, 2)),
+            dma((ranks + 1, 2)),
+            dma((ranks + 1,)),
+            dma((ranks + 1,)),
             dma((E,)),
             dma((E,)),
         ],

time: 280 us -> 274 us (0.979)
  Pallas kernels: 279 us -> 273 us
    pallas_call x1, Pallas kernels: 167 us -> 163 us  [ahead(): pl.pallas_call(ahead_kernel, out_shape=[sds(*k) for k in kept + results],...]
where the time goes in v7:
time: 274 us
  Pallas kernels  273 us (100%)
    pallas_call x1, Pallas kernels, ahead(): pl.pallas_call(ahead_kernel, out_shape=[sds(*k) for k in kept + results],...  163 us
    pallas_call x1, Pallas kernels, end(): pl.pallas_call(end_kernel, out_shape=[sds((TOK_DEV, width), BF16), sds((T...  104 us
    pallas_call x1, Pallas kernels, store(): pl.pallas_call(store_kernel, out_shape=[sds((E, rows, cols), F32)] * 3 +...  6.34 us

profile of v7, /device:TPU:0, one launch (start us, length us, event | category | flops | bytes accessed | tf_op | source)
XLA Modules:
  0.0 274.3 jit_solution(16269782232936101162)
XLA Ops:
  0.7 163.3 %ahead.1 = (bf16[4,768,768]{2,1,0:T(8,128)(2,1)}, f32[768,128]{1,0:T(8,128)}, bf16[256,768]{1,0:T(8,128)(2,1)}, bf16[320,768]{1,0:T(8,128)(2,1)}, bf16[576,768]{...) custom-call(s32[1,8]{1,0:T(1,128)} %len_ref.1, ...), custom_call_target="tpu_custom_call" | custom-call | tf_op jit(solution)/shard_map/ahead/pallas_call | solution.py:1563
  163.9 103.8 %end.1 = (bf16[320,768]{1,0:T(8,128)(2,1)}, f32[320,768]{1,0:T(8,128)}, f32[12,320]{1,0:T(8,128)}, f32[320,768]{1,0:T(8,128)}, bf16[256,768]{1,0:T(8,128)(2,1)},...) custom-call(bf16[320,768]{1,0:T(8,128)(2,1)} %cot_ref.3, bf16[320,768]{1,0:T(8,128)(2,1)} %tok_hbm.1, ...), custom_call_target="tpu_custom_call" | custom-call | tf_op jit(solution)/shard_map/end/pallas_call | solution.py:2093
  267.7 6.3 %store.1 = (f32[8,192,256]{2,1,0:T(8,128)}, f32[8,192,256]{2,1,0:T(8,128)}, f32[8,192,256]{2,1,0:T(8,128)}, f32[192,96]{1,0:T(8,128)}, f32[192,96]{1,0:T(8,128)}...) custom-call(bf16[8,3,192,256]{3,2,1,0:T(8,128)(2,1)} %get-tuple-elem, ...), custom_call_target="tpu_custom_call" | custom-call | tf_op jit(solution)/shard_map/store/pallas_call | solution.py:2279
